TPU v7x, 32 devices: a whole 2x2x4 slice. The times are simulated.
32 devices in a mesh: seq: 32 (over z, y, x, core), head: 1.
Axes of the slice: x: 2, y: 2, z: 4, core: 2. Of those that a mesh axis runs over, the one named last changes fastest.
Arguments:
- queries: float32 [8192, 16, 256], P('seq', 'head'), may hold values from -6 to 6
- key_rows: float32 [8192, 256], P(('seq', 'head')), may hold values from -6 to 6
- value_rows: float32 [8192, 256], P(('seq', 'head')), may hold values from -6 to 6
- forward_out: float32 [8192, 16, 256], P('seq', 'head'), may hold values from -6 to 6
- out_grad: float32 [8192, 16, 256], P('seq', 'head'), may hold values from -6 to 6
- log_norm: float32 [8192, 16], P('seq', 'head'), may hold values from 6 to 9
- doc_ids: int32 [8192], P(('seq', 'head')), may hold values from 0 to 3, never falling along the last dimension, each value on 1 to 4096 neighbouring positions
Outputs:
- grad_queries: float32 [8192, 16, 256], P('seq', 'head')
- grad_keys: float32 [8192, 256], P(('seq', 'head'))
- grad_values: float32 [8192, 256], P(('seq', 'head'))
Inputs may be any that keep to these rules, and one draw needn't show every extreme that they name: `doc_ids`: never falling along the tokens; each document holds 1 to 4096 tokens, one exactly 4096.
All inputs are finite; a program needn't handle non-finite values.
Results may differ from a plain program's by a relative error of at most 0.0003.
Values sent between devices are 32-bit elements; how exact they have to be, the bound alone decides.
No kernel may reach another device: no remote copies, remote signals or barrier semaphores. Data moves between devices by JAX's collectives and lax.ppermute only.
A program may use at most 128 MiB of HBM per device.

v0:
```python
import jax
import jax.numpy as jnp
from jax import lax
from jax.sharding import PartitionSpec as P

WIN = 2048


def shifted(value, axis, steps):
    count = lax.axis_size(axis)
    leading, last = (max(0, -steps), min(count, count - steps))
    return lax.ppermute(value, axis, [(source, source + steps) for source in range(leading, last)])


def on_device(queries, key_rows, value_rows, forward_out, out_grad, log_norm, doc_ids):
    row_count, local_heads, head_width = queries.shape
    reach = WIN // row_count
    factor = head_width ** (-0.5)
    high = lax.Precision.HIGHEST
    id_float = doc_ids.astype(jnp.float32)
    own_keys, own_vals, own_ids = (
        lax.all_gather(key_rows, "head", axis=0, tiled=True),
        lax.all_gather(value_rows, "head", axis=0, tiled=True),
        lax.all_gather(id_float, "head", axis=0, tiled=True),
    )
    key_parts = []
    val_parts = []
    id_parts = []
    for distance in range(reach, 0, -1):
        far_keys, far_vals, far_ids = shifted((own_keys, own_vals, own_ids), "seq", distance)
        key_parts.append(far_keys)
        val_parts.append(far_vals)
        id_parts.append(far_ids)
    key_window = jnp.concatenate(key_parts + [own_keys], axis=0)
    val_window = jnp.concatenate(val_parts + [own_vals], axis=0)
    id_window = jnp.concatenate(id_parts + [own_ids], axis=0)
    extent = key_window.shape[0]
    query_ids = id_window[extent - row_count :]
    first_row = lax.axis_index("seq") * row_count
    query_pos = first_row + jnp.arange(row_count, dtype=jnp.int32)
    key_pos = first_row - reach * row_count + jnp.arange(extent, dtype=jnp.int32)
    spacing = query_pos[:, None] - key_pos[None, :]
    allowed = (
        (spacing >= 0)
        & (spacing < WIN)
        & (query_ids[:, None] == id_window[None, :])
        & (key_pos[None, :] >= 0)
    )
    scores = jnp.einsum("rhd,kd->hrk", queries, key_window, precision=high) * factor
    probs = jnp.where(allowed[None], jnp.exp(scores - log_norm.T[:, :, None]), 0.0)
    vals_grad = jnp.einsum("hrk,rhd->kd", probs, out_grad, precision=high)
    grad_probs = jnp.einsum("rhd,kd->hrk", out_grad, val_window, precision=high)
    delta = jnp.sum(out_grad * forward_out, axis=-1)
    grad_scores = probs * (grad_probs - delta.T[:, :, None])
    grad_queries = jnp.einsum("hrk,kd->rhd", grad_scores, key_window, precision=high) * factor
    keys_grad = jnp.einsum("hrk,rhd->kd", grad_scores, queries, precision=high) * factor
    own_kgrad = keys_grad[reach * row_count :]
    own_vgrad = vals_grad[reach * row_count :]
    for distance in range(1, reach + 1):
        lower = (reach - distance) * row_count
        back_keys, back_vals = shifted(
            (keys_grad[lower : lower + row_count], vals_grad[lower : lower + row_count]),
            "seq",
            -distance,
        )
        own_kgrad = own_kgrad + back_keys
        own_vgrad = own_vgrad + back_vals
    grad_keys, grad_values = (
        lax.psum_scatter(own_kgrad, "head", scatter_dimension=0, tiled=True),
        lax.psum_scatter(own_vgrad, "head", scatter_dimension=0, tiled=True),
    )
    return (grad_queries, grad_keys, grad_values)


def solution(mesh):
    in_specs = (
        P("seq", "head", None),
        P(("seq", "head"), None),
        P(("seq", "head"), None),
        P("seq", "head", None),
        P("seq", "head", None),
        P("seq", "head"),
        P(("seq", "head")),
    )
    out_specs = (P("seq", "head", None), P(("seq", "head"), None), P(("seq", "head"), None))
    return jax.shard_map(
        on_device, mesh=mesh, in_specs=in_specs, out_specs=out_specs, check_vma=False
    )
```

profile of v0, /device:TPU:0, one launch (start us, length us, event | category | flops | bytes accessed | tf_op | source)
XLA Modules:
  0.0 379.9 jit_solution(16530065132627670139)
XLA Ops:
  1.3 4.9 %collective-permute-start.8 = (f32[256]{0:T(256)S(1)}, f32[256]{0:T(256)S(1)}, u32[]{:S(2)}, u32[]{:S(2)}) collective-permute-start(f32[256]{0:T(256)S(1)} %convert_element_type.3), channel_id=1, source_target_pairs={{0,8},{1,9},{2,10},{3,11},{4,12},{5,13},{6,14},{7,15},{8,16},{9,17... | collective-permute-start | bytes 3080 | tf_op jit(solution)/shard_map/ppermute | solution.py:12
  6.3 3.5 collective-permute-start.9
  9.8 3.5 collective-permute-start.10
  13.2 3.7 collective-permute-start.11
  17.0 3.4 collective-permute-start.12
  20.5 4.1 %multiply_reduce_fusion = f32[256,16]{1,0:T(8,128)S(1)} fusion(f32[256,16,256]{2,1,0:T(8,128)} %param.11, f32[256,16,256]{2,1,0:T(8,128)} %param.10), kind=kLoop, calls=%fused_computation.6 | loop fusion | flops 2093056 | bytes 8404992 | tf_op jit(solution)/shard_map/reduce_sum | solution.py:53
  24.7 1.9 collective-permute-start.13
  26.6 3.8 collective-permute-start.14
  30.4 1.3 collective-permute-start.15
  31.7 2.2 collective-permute-start
  34.0 3.4 collective-permute-start.1
  37.4 1.7 collective-permute-start.2
  39.1 2.8 collective-permute-start.3
  41.9 1.6 collective-permute-start.4
  43.5 2.0 fusion.14
  45.6 2.2 collective-permute-start.5
  47.8 3.7 collective-permute-start.6
  51.6 1.3 collective-permute-start.7
  52.9 6.5 %collective-permute-start.16 = (f32[256,256]{1,0:T(8,128)}, f32[256,256]{1,0:T(8,128)S(1)}, u32[]{:S(2)}, u32[]{:S(2)}) collective-permute-start(f32[256,256]{1,0:T(8,128)} %param.9), channel_id=1, source_target_pairs={{0,8},{1,9},{2,10},{3,11},{4,12},{5,13},{6,14},{7,15},{8,16},{9,17... | collective-permute-start | bytes 786440 | tf_op jit(solution)/shard_map/ppermute | solution.py:12
  59.5 4.6 %collective-permute-done.4 = f32[256,256]{1,0:T(8,128)S(1)} collective-permute-done((f32[256,256]{1,0:T(8,128)S(1)}, f32[256,256]{1,0:T(8,128)S(1)}, u32[]{:S(2)}, u32[]{:S(2)}) %collective-permute-start.4) | collective-permute-done | bytes 262176 | tf_op jit(solution)/shard_map/ppermute | solution.py:12
  64.0 2.7 collective-permute-start.17
  66.7 4.9 %collective-permute-start.18 = (f32[256,256]{1,0:T(8,128)}, f32[256,256]{1,0:T(8,128)S(1)}, u32[]{:S(2)}, u32[]{:S(2)}) collective-permute-start(f32[256,256]{1,0:T(8,128)} %param.9), channel_id=1, source_target_pairs={{0,6},{1,7},{2,8},{3,9},{4,10},{5,11},{6,12},{7,13},{8,14},{9,15},... | collective-permute-start | bytes 786440 | tf_op jit(solution)/shard_map/ppermute | solution.py:12
  71.7 1.8 collective-permute-start.19
  73.5 9.8 %collective-permute-start.20 = (f32[256,256]{1,0:T(8,128)}, f32[256,256]{1,0:T(8,128)S(1)}, u32[]{:S(2)}, u32[]{:S(2)}) collective-permute-start(f32[256,256]{1,0:T(8,128)} %param.9), channel_id=1, source_target_pairs={{0,4},{1,5},{2,6},{3,7},{4,8},{5,9},{6,10},{7,11},{8,12},{9,13},{1... | collective-permute-start | bytes 786440 | tf_op jit(solution)/shard_map/ppermute | solution.py:12
  83.4 1.4 copy-done.3
  84.8 42.4 %fusion.2 = f32[16,256,2304]{1,2,0:T(8,128)} fusion(f32[16,256]{1,0:T(8,128)S(1)} %bitcast.35, pred[256,2304]{0,1:T(8,128)(4,1)S(1)} %fusion.14, f32[256,16,256]{2,1,0:T(8,128)S(1)} %copy-done.2, f32[2304,256]{1,0:T(8,128)S(1)} %constant_dynamic-update-slice_fusion), kind=kOutput, calls=%fused_computation.4 | convolution fusion | flops 29019340800 | bytes 44908544 | tf_op jit(solution)/shard_map/rhd,kd->hrk/dot_general | solution.py:49
  127.1 41.5 %convolution_bitcast_fusion = f32[2304,256]{1,0:T(8,128)S(1)} fusion(f32[16,256,2304]{1,2,0:T(8,128)} %fusion.2, f32[256,16,256]{2,1,0:T(8,128)S(1)} %copy-done), kind=kOutput, calls=%fused_computation.7 | convolution fusion | flops 28991029248 | bytes 44302336 | tf_op jit(solution)/shard_map/hrk,rhd->kd/dot_general | solution.py:51
  168.6 1.1 fusion.31
  169.7 2.8 collective-permute-start.21
  173.2 2.2 collective-permute-start.22
  175.4 0.7 constant_dynamic-update-slice_fusion.17
  176.1 4.5 %collective-permute-start.23 = (f32[256,256]{1,0:T(8,128)}, f32[256,256]{1,0:T(8,128)S(1)}, u32[]{:S(2)}, u32[]{:S(2)}) collective-permute-start(f32[256,256]{1,0:T(8,128)} %param.9), channel_id=1, source_target_pairs={{0,1},{1,2},{2,3},{3,4},{4,5},{5,6},{6,7},{7,8},{8,9},{9,10},{10,1... | collective-permute-start | bytes 786440 | tf_op jit(solution)/shard_map/ppermute | solution.py:12
  180.6 0.7 constant_dynamic-update-slice_fusion.16
  181.3 1.3 collective-permute-start.32
  182.6 0.7 constant_dynamic-update-slice_fusion.15
  183.3 1.3 collective-permute-start.33
  184.6 0.7 constant_dynamic-update-slice_fusion.14
  185.3 1.3 collective-permute-start.34
  186.6 0.7 constant_dynamic-update-slice_fusion.13
  187.4 1.3 collective-permute-start.35
  189.4 1.3 collective-permute-start.36
  191.4 1.7 constant_dynamic-update-slice_fusion.10
  193.1 47.4 %fusion = f32[16,256,2304]{1,2,0:T(8,128)} fusion(f32[16,256,2304]{1,2,0:T(8,128)} %fusion.2, f32[16,256]{1,0:T(8,128)S(1)} %copy.19, f32[256,16,256]{2,1,0:T(8,128)S(1)} %copy-done, f32[2304,256]{1,0:T(8,128)} %constant_dynamic-update-slice_fusion.10), kind=kOutput, calls=%fused_computation.1 | convolution fusion | flops 29009903616 | bytes 82067456 | tf_op jit(solution)/shard_map/rhd,kd->hrk/dot_general | solution.py:52
  240.5 36.3 %fusion.3 = f32[2304,256]{1,0:T(8,128)S(1)} fusion(f32[16,256,2304]{1,2,0:T(8,128)} %fusion, f32[256,16,256]{2,1,0:T(8,128)} %param.7), kind=kOutput, calls=%fused_computation.9 | convolution fusion | flops 28991619072 | bytes 44302336 | tf_op jit(solution)/shard_map/hrk,rhd->kd/dot_general | solution.py:56
  276.8 1.6 collective-permute-start.37
  278.4 1.3 fusion.32
  279.7 1.3 collective-permute-start.38
  281.0 1.3 collective-permute-start.39
  282.3 1.3 collective-permute-start.24
  283.6 1.3 collective-permute-start.25
  284.9 8.0 %collective-permute-done.37 = f32[256,256]{1,0:T(8,128)S(1)} collective-permute-done((f32[256,256]{1,0:T(8,128)S(1)}, f32[256,256]{1,0:T(8,128)S(1)}, u32[]{:S(2)}, u32[]{:S(2)}) %collective-permute-start.37) | collective-permute-done | bytes 262176 | tf_op jit(solution)/shard_map/ppermute | solution.py:12
  293.7 1.3 collective-permute-start.26
  295.0 38.3 %multiply_bitcast_fusion = f32[256,16,256]{0,2,1:T(8,128)} fusion(f32[16,256,2304]{1,2,0:T(8,128)} %fusion, f32[2304,256]{1,0:T(8,128)S(1)} %copy-done.4), kind=kOutput, calls=%fused_computation.5 | convolution fusion | flops 28992077824 | bytes 44302336 | tf_op jit(solution)/shard_map/hrk,kd->rhd/dot_general | solution.py:55
  333.3 5.4 %copy.24 = f32[256,16,256]{2,1,0:T(8,128)} copy(f32[256,16,256]{0,2,1:T(8,128)} %multiply_bitcast_fusion) | data formatting | bytes 8388608
  338.7 1.3 collective-permute-start.27
  340.0 1.3 collective-permute-start.28
  341.3 1.3 collective-permute-start.29
  342.6 1.3 collective-permute-start.30
  343.9 1.3 collective-permute-start.31
  345.2 2.2 fusion.23
  347.4 17.3 %collective-permute-done.27 = f32[256,256]{1,0:T(8,128)S(1)} collective-permute-done((f32[256,256]{1,0:T(8,128)}, f32[256,256]{1,0:T(8,128)S(1)}, u32[]{:S(2)}, u32[]{:S(2)}) %collective-permute-start.27) | collective-permute-done | bytes 262176 | tf_op jit(solution)/shard_map/ppermute | solution.py:12
  364.7 3.0 collective-permute-done.28
  367.7 9.8 %collective-permute-done.31 = f32[256,256]{1,0:T(8,128)S(1)} collective-permute-done((f32[256,256]{1,0:T(8,128)}, f32[256,256]{1,0:T(8,128)S(1)}, u32[]{:S(2)}, u32[]{:S(2)}) %collective-permute-start.31) | collective-permute-done | bytes 262176 | tf_op jit(solution)/shard_map/ppermute | solution.py:12
  377.6 2.0 fusion.30
  (81 shorter events, 4.0 us)
Async XLA Ops:
  1.3 23.4 %collective-permute-start.8 = (f32[256]{0:T(256)S(1)}, f32[256]{0:T(256)S(1)}, u32[]{:S(2)}, u32[]{:S(2)}) collective-permute-start(f32[256]{0:T(256)S(1)} %convert_element_type.3), channel_id=1, source_target_pairs={{0,8},{1,9},{2,10},{3,11},{4,12},{5,13},{6,14},{7,15},{8,16},{9,17... | collective-permute-start | bytes 3080 | tf_op jit(solution)/shard_map/ppermute | solution.py:12
  6.3 20.3 %collective-permute-start.9 = (f32[256]{0:T(256)S(1)}, f32[256]{0:T(256)S(1)}, u32[]{:S(2)}, u32[]{:S(2)}) collective-permute-start(f32[256]{0:T(256)S(1)} %convert_element_type.3), channel_id=1, source_target_pairs={{0,7},{1,8},{2,9},{3,10},{4,11},{5,12},{6,13},{7,14},{8,15},{9,16}... | collective-permute-start | bytes 3080 | tf_op jit(solution)/shard_map/ppermute | solution.py:12
  9.8 20.6 %collective-permute-start.10 = (f32[256]{0:T(256)S(1)}, f32[256]{0:T(256)S(1)}, u32[]{:S(2)}, u32[]{:S(2)}) collective-permute-start(f32[256]{0:T(256)S(1)} %convert_element_type.3), channel_id=1, source_target_pairs={{0,6},{1,7},{2,8},{3,9},{4,10},{5,11},{6,12},{7,13},{8,14},{9,15},... | collective-permute-start | bytes 3080 | tf_op jit(solution)/shard_map/ppermute | solution.py:12
  13.2 18.5 %collective-permute-start.11 = (f32[256]{0:T(256)S(1)}, f32[256]{0:T(256)S(1)}, u32[]{:S(2)}, u32[]{:S(2)}) collective-permute-start(f32[256]{0:T(256)S(1)} %convert_element_type.3), channel_id=1, source_target_pairs={{0,5},{1,6},{2,7},{3,8},{4,9},{5,10},{6,11},{7,12},{8,13},{9,14},{... | collective-permute-start | bytes 3080 | tf_op jit(solution)/shard_map/ppermute | solution.py:12
  17.0 17.0 %collective-permute-start.12 = (f32[256]{0:T(256)S(1)}, f32[256]{0:T(256)S(1)}, u32[]{:S(2)}, u32[]{:S(2)}) collective-permute-start(f32[256]{0:T(256)S(1)} %convert_element_type.3), channel_id=1, source_target_pairs={{0,4},{1,5},{2,6},{3,7},{4,8},{5,9},{6,10},{7,11},{8,12},{9,13},{1... | collective-permute-start | bytes 3080 | tf_op jit(solution)/shard_map/ppermute | solution.py:12
  20.5 11.3 %copy-start.7 = (f32[256,256]{1,0:T(8,128)S(1)}, f32[256,256]{1,0:T(8,128)}, u32[]{:S(2)}) copy-start(f32[256,256]{1,0:T(8,128)} %param.8) | copy-start | bytes 786436
  20.5 23.1 %copy-start.8 = (s32[256]{0:T(256)S(1)}, s32[256]{0:T(256)}, u32[]{:S(2)}) copy-start(s32[256]{0:T(256)} %param.13) | copy-start | bytes 3076
  24.7 12.7 %collective-permute-start.13 = (f32[256]{0:T(256)S(1)}, f32[256]{0:T(256)S(1)}, u32[]{:S(2)}, u32[]{:S(2)}) collective-permute-start(f32[256]{0:T(256)S(1)} %convert_element_type.3), channel_id=1, source_target_pairs={{0,3},{1,4},{2,5},{3,6},{4,7},{5,8},{6,9},{7,10},{8,11},{9,12},{10... | collective-permute-start | bytes 3080 | tf_op jit(solution)/shard_map/ppermute | solution.py:12
  26.6 12.5 %collective-permute-start.14 = (f32[256]{0:T(256)S(1)}, f32[256]{0:T(256)S(1)}, u32[]{:S(2)}, u32[]{:S(2)}) collective-permute-start(f32[256]{0:T(256)S(1)} %convert_element_type.3), channel_id=1, source_target_pairs={{0,2},{1,3},{2,4},{3,5},{4,6},{5,7},{6,8},{7,9},{8,10},{9,11},{10,... | collective-permute-start | bytes 3080 | tf_op jit(solution)/shard_map/ppermute | solution.py:12
  30.4 11.5 %collective-permute-start.15 = (f32[256]{0:T(256)S(1)}, f32[256]{0:T(256)S(1)}, u32[]{:S(2)}, u32[]{:S(2)}) collective-permute-start(f32[256]{0:T(256)S(1)} %convert_element_type.3), channel_id=1, source_target_pairs={{0,1},{1,2},{2,3},{3,4},{4,5},{5,6},{6,7},{7,8},{8,9},{9,10},{10,1... | collective-permute-start | bytes 3080 | tf_op jit(solution)/shard_map/ppermute | solution.py:12
  31.7 13.8 %collective-permute-start = (f32[256,256]{1,0:T(8,128)S(1)}, f32[256,256]{1,0:T(8,128)S(1)}, u32[]{:S(2)}, u32[]{:S(2)}) collective-permute-start(f32[256,256]{1,0:T(8,128)S(1)} %copy-done.7), channel_id=1, source_target_pairs={{0,8},{1,9},{2,10},{3,11},{4,12},{5,13},{6,14},{7,15},{8,16},{9,17... | collective-permute-start | bytes 786440 | tf_op jit(solution)/shard_map/ppermute | solution.py:12
  34.0 13.8 %collective-permute-start.1 = (f32[256,256]{1,0:T(8,128)S(1)}, f32[256,256]{1,0:T(8,128)S(1)}, u32[]{:S(2)}, u32[]{:S(2)}) collective-permute-start(f32[256,256]{1,0:T(8,128)S(1)} %copy-done.7), channel_id=1, source_target_pairs={{0,7},{1,8},{2,9},{3,10},{4,11},{5,12},{6,13},{7,14},{8,15},{9,16}... | collective-permute-start | bytes 786440 | tf_op jit(solution)/shard_map/ppermute | solution.py:12
  37.4 14.2 %collective-permute-start.2 = (f32[256,256]{1,0:T(8,128)S(1)}, f32[256,256]{1,0:T(8,128)S(1)}, u32[]{:S(2)}, u32[]{:S(2)}) collective-permute-start(f32[256,256]{1,0:T(8,128)S(1)} %copy-done.7), channel_id=1, source_target_pairs={{0,6},{1,7},{2,8},{3,9},{4,10},{5,11},{6,12},{7,13},{8,14},{9,15},... | collective-permute-start | bytes 786440 | tf_op jit(solution)/shard_map/ppermute | solution.py:12
  39.1 13.8 %collective-permute-start.3 = (f32[256,256]{1,0:T(8,128)S(1)}, f32[256,256]{1,0:T(8,128)S(1)}, u32[]{:S(2)}, u32[]{:S(2)}) collective-permute-start(f32[256,256]{1,0:T(8,128)S(1)} %copy-done.7), channel_id=1, source_target_pairs={{0,5},{1,6},{2,7},{3,8},{4,9},{5,10},{6,11},{7,12},{8,13},{9,14},{... | collective-permute-start | bytes 786440 | tf_op jit(solution)/shard_map/ppermute | solution.py:12
  41.9 22.1 %collective-permute-start.4 = (f32[256,256]{1,0:T(8,128)S(1)}, f32[256,256]{1,0:T(8,128)S(1)}, u32[]{:S(2)}, u32[]{:S(2)}) collective-permute-start(f32[256,256]{1,0:T(8,128)S(1)} %copy-done.7), channel_id=1, source_target_pairs={{0,4},{1,5},{2,6},{3,7},{4,8},{5,9},{6,10},{7,11},{8,12},{9,13},{1... | collective-permute-start | bytes 786440 | tf_op jit(solution)/shard_map/ppermute | solution.py:12
  45.5 39.2 %copy-start.2 = (f32[256,16,256]{2,1,0:T(8,128)S(1)}, f32[256,16,256]{2,1,0:T(8,128)}, u32[]{:S(2)}) copy-start(f32[256,16,256]{2,1,0:T(8,128)} %param.7) | copy-start | bytes 12582916
  45.6 39.2 %copy-start.9 = (f32[256,16]{0,1:T(8,128)S(1)}, f32[256,16]{0,1:T(8,128)}, u32[]{:S(2)}) copy-start(f32[256,16]{0,1:T(8,128)} %param.12) | copy-start | bytes 49156
  45.6 21.2 %collective-permute-start.5 = (f32[256,256]{1,0:T(8,128)S(1)}, f32[256,256]{1,0:T(8,128)S(1)}, u32[]{:S(2)}, u32[]{:S(2)}) collective-permute-start(f32[256,256]{1,0:T(8,128)S(1)} %copy-done.7), channel_id=1, source_target_pairs={{0,3},{1,4},{2,5},{3,6},{4,7},{5,8},{6,9},{7,10},{8,11},{9,12},{10... | collective-permute-start | bytes 786440 | tf_op jit(solution)/shard_map/ppermute | solution.py:12
  47.8 23.9 %collective-permute-start.6 = (f32[256,256]{1,0:T(8,128)S(1)}, f32[256,256]{1,0:T(8,128)S(1)}, u32[]{:S(2)}, u32[]{:S(2)}) collective-permute-start(f32[256,256]{1,0:T(8,128)S(1)} %copy-done.7), channel_id=1, source_target_pairs={{0,2},{1,3},{2,4},{3,5},{4,6},{5,7},{6,8},{7,9},{8,10},{9,11},{10,... | collective-permute-start | bytes 786440 | tf_op jit(solution)/shard_map/ppermute | solution.py:12
  51.6 21.9 %collective-permute-start.7 = (f32[256,256]{1,0:T(8,128)S(1)}, f32[256,256]{1,0:T(8,128)S(1)}, u32[]{:S(2)}, u32[]{:S(2)}) collective-permute-start(f32[256,256]{1,0:T(8,128)S(1)} %copy-done.7), channel_id=1, source_target_pairs={{0,1},{1,2},{2,3},{3,4},{4,5},{5,6},{6,7},{7,8},{8,9},{9,10},{10,1... | collective-permute-start | bytes 786440 | tf_op jit(solution)/shard_map/ppermute | solution.py:12
  52.9 116.7 %collective-permute-start.16 = (f32[256,256]{1,0:T(8,128)}, f32[256,256]{1,0:T(8,128)S(1)}, u32[]{:S(2)}, u32[]{:S(2)}) collective-permute-start(f32[256,256]{1,0:T(8,128)} %param.9), channel_id=1, source_target_pairs={{0,8},{1,9},{2,10},{3,11},{4,12},{5,13},{6,14},{7,15},{8,16},{9,17... | collective-permute-start | bytes 786440 | tf_op jit(solution)/shard_map/ppermute | solution.py:12
  64.0 109.1 %collective-permute-start.17 = (f32[256,256]{1,0:T(8,128)}, f32[256,256]{1,0:T(8,128)S(1)}, u32[]{:S(2)}, u32[]{:S(2)}) collective-permute-start(f32[256,256]{1,0:T(8,128)} %param.9), channel_id=1, source_target_pairs={{0,7},{1,8},{2,9},{3,10},{4,11},{5,12},{6,13},{7,14},{8,15},{9,16}... | collective-permute-start | bytes 786440 | tf_op jit(solution)/shard_map/ppermute | solution.py:12
  66.7 109.4 %collective-permute-start.18 = (f32[256,256]{1,0:T(8,128)}, f32[256,256]{1,0:T(8,128)S(1)}, u32[]{:S(2)}, u32[]{:S(2)}) collective-permute-start(f32[256,256]{1,0:T(8,128)} %param.9), channel_id=1, source_target_pairs={{0,6},{1,7},{2,8},{3,9},{4,10},{5,11},{6,12},{7,13},{8,14},{9,15},... | collective-permute-start | bytes 786440 | tf_op jit(solution)/shard_map/ppermute | solution.py:12
  71.7 109.7 %collective-permute-start.19 = (f32[256,256]{1,0:T(8,128)}, f32[256,256]{1,0:T(8,128)S(1)}, u32[]{:S(2)}, u32[]{:S(2)}) collective-permute-start(f32[256,256]{1,0:T(8,128)} %param.9), channel_id=1, source_target_pairs={{0,5},{1,6},{2,7},{3,8},{4,9},{5,10},{6,11},{7,12},{8,13},{9,14},{... | collective-permute-start | bytes 786440 | tf_op jit(solution)/shard_map/ppermute | solution.py:12
  73.5 109.8 %collective-permute-start.20 = (f32[256,256]{1,0:T(8,128)}, f32[256,256]{1,0:T(8,128)S(1)}, u32[]{:S(2)}, u32[]{:S(2)}) collective-permute-start(f32[256,256]{1,0:T(8,128)} %param.9), channel_id=1, source_target_pairs={{0,4},{1,5},{2,6},{3,7},{4,8},{5,9},{6,10},{7,11},{8,12},{9,13},{1... | collective-permute-start | bytes 786440 | tf_op jit(solution)/shard_map/ppermute | solution.py:12
  83.3 1.4 copy-start.3
  84.7 42.4 %copy-start = (f32[256,16,256]{2,1,0:T(8,128)S(1)}, f32[256,16,256]{2,1,0:T(8,128)}, u32[]{:S(2)}) copy-start(f32[256,16,256]{2,1,0:T(8,128)} %param.11) | copy-start | bytes 12582916
  169.7 15.7 %collective-permute-start.21 = (f32[256,256]{1,0:T(8,128)}, f32[256,256]{1,0:T(8,128)S(1)}, u32[]{:S(2)}, u32[]{:S(2)}) collective-permute-start(f32[256,256]{1,0:T(8,128)} %param.9), channel_id=1, source_target_pairs={{0,3},{1,4},{2,5},{3,6},{4,7},{5,8},{6,9},{7,10},{8,11},{9,12},{10... | collective-permute-start | bytes 786440 | tf_op jit(solution)/shard_map/ppermute | solution.py:12
  173.2 14.2 %collective-permute-start.22 = (f32[256,256]{1,0:T(8,128)}, f32[256,256]{1,0:T(8,128)S(1)}, u32[]{:S(2)}, u32[]{:S(2)}) collective-permute-start(f32[256,256]{1,0:T(8,128)} %param.9), channel_id=1, source_target_pairs={{0,2},{1,3},{2,4},{3,5},{4,6},{5,7},{6,8},{7,9},{8,10},{9,11},{10,... | collective-permute-start | bytes 786440 | tf_op jit(solution)/shard_map/ppermute | solution.py:12
  176.1 13.3 %collective-permute-start.23 = (f32[256,256]{1,0:T(8,128)}, f32[256,256]{1,0:T(8,128)S(1)}, u32[]{:S(2)}, u32[]{:S(2)}) collective-permute-start(f32[256,256]{1,0:T(8,128)} %param.9), channel_id=1, source_target_pairs={{0,1},{1,2},{2,3},{3,4},{4,5},{5,6},{6,7},{7,8},{8,9},{9,10},{10,1... | collective-permute-start | bytes 786440 | tf_op jit(solution)/shard_map/ppermute | solution.py:12
  181.3 95.5 %collective-permute-start.32 = (f32[256,256]{1,0:T(8,128)}, f32[256,256]{1,0:T(8,128)S(1)}, u32[]{:S(2)}, u32[]{:S(2)}) collective-permute-start(f32[256,256]{1,0:T(8,128)} %get-tuple-element.9), channel_id=1, source_target_pairs={{1,0},{2,1},{3,2},{4,3},{5,4},{6,5},{7,6},{8,7},{9,8},{10,9},{11,1... | collective-permute-start | bytes 786440 | tf_op jit(solution)/shard_map/ppermute | solution.py:12
  183.3 96.4 %collective-permute-start.33 = (f32[256,256]{1,0:T(8,128)}, f32[256,256]{1,0:T(8,128)S(1)}, u32[]{:S(2)}, u32[]{:S(2)}) collective-permute-start(f32[256,256]{1,0:T(8,128)} %get-tuple-element.16), channel_id=1, source_target_pairs={{2,0},{3,1},{4,2},{5,3},{6,4},{7,5},{8,6},{9,7},{10,8},{11,9},{12,... | collective-permute-start | bytes 786440 | tf_op jit(solution)/shard_map/ppermute | solution.py:12
  185.3 95.7 %collective-permute-start.34 = (f32[256,256]{1,0:T(8,128)}, f32[256,256]{1,0:T(8,128)S(1)}, u32[]{:S(2)}, u32[]{:S(2)}) collective-permute-start(f32[256,256]{1,0:T(8,128)} %get-tuple-element.15), channel_id=1, source_target_pairs={{3,0},{4,1},{5,2},{6,3},{7,4},{8,5},{9,6},{10,7},{11,8},{12,9},{13... | collective-permute-start | bytes 786440 | tf_op jit(solution)/shard_map/ppermute | solution.py:12
  187.4 95.0 %collective-permute-start.35 = (f32[256,256]{1,0:T(8,128)}, f32[256,256]{1,0:T(8,128)}, u32[]{:S(2)}, u32[]{:S(2)}) collective-permute-start(f32[256,256]{1,0:T(8,128)} %get-tuple-element.14), channel_id=1, source_target_pairs={{4,0},{5,1},{6,2},{7,3},{8,4},{9,5},{10,6},{11,7},{12,8},{13,9},{1... | collective-permute-start | bytes 786440 | tf_op jit(solution)/shard_map/ppermute | solution.py:12
  189.4 94.3 %collective-permute-start.36 = (f32[256,256]{1,0:T(8,128)}, f32[256,256]{1,0:T(8,128)}, u32[]{:S(2)}, u32[]{:S(2)}) collective-permute-start(f32[256,256]{1,0:T(8,128)} %get-tuple-element.13), channel_id=1, source_target_pairs={{5,0},{6,1},{7,2},{8,3},{9,4},{10,5},{11,6},{12,7},{13,8},{14,9},{... | collective-permute-start | bytes 786440 | tf_op jit(solution)/shard_map/ppermute | solution.py:12
  276.8 1.6 copy-start.1
  276.8 18.2 %copy-start.4 = (f32[2304,256]{1,0:T(8,128)S(1)}, f32[2304,256]{1,0:T(8,128)}, u32[]{:S(2)}) copy-start(f32[2304,256]{1,0:T(8,128)} %copy-done.3) | copy-start | bytes 7077892
  276.8 16.2 %collective-permute-start.37 = (f32[256,256]{1,0:T(8,128)S(1)}, f32[256,256]{1,0:T(8,128)S(1)}, u32[]{:S(2)}, u32[]{:S(2)}) collective-permute-start(f32[256,256]{1,0:T(8,128)S(1)} %get-tuple-element.12), channel_id=1, source_target_pairs={{6,0},{7,1},{8,2},{9,3},{10,4},{11,5},{12,6},{13,7},{14,8},{15,9},... | collective-permute-start | bytes 786440 | tf_op jit(solution)/shard_map/ppermute | solution.py:12
  279.7 59.0 %collective-permute-start.38 = (f32[256,256]{1,0:T(8,128)S(1)}, f32[256,256]{1,0:T(8,128)}, u32[]{:S(2)}, u32[]{:S(2)}) collective-permute-start(f32[256,256]{1,0:T(8,128)S(1)} %get-tuple-element.11), channel_id=1, source_target_pairs={{7,0},{8,1},{9,2},{10,3},{11,4},{12,5},{13,6},{14,7},{15,8},{16,9}... | collective-permute-start | bytes 786440 | tf_op jit(solution)/shard_map/ppermute | solution.py:12
  281.0 12.0 %copy-start.5 = (f32[256,256]{1,0:T(8,128)}, f32[256,256]{1,0:T(8,128)S(1)}, u32[]{:S(2)}) copy-start(f32[256,256]{1,0:T(8,128)S(1)} %collective-permute-done.34) | copy-start | bytes 786436
  281.0 59.0 %collective-permute-start.39 = (f32[256,256]{1,0:T(8,128)S(1)}, f32[256,256]{1,0:T(8,128)}, u32[]{:S(2)}, u32[]{:S(2)}) collective-permute-start(f32[256,256]{1,0:T(8,128)S(1)} %get-tuple-element.10), channel_id=1, source_target_pairs={{8,0},{9,1},{10,2},{11,3},{12,4},{13,5},{14,6},{15,7},{16,8},{17,9... | collective-permute-start | bytes 786440 | tf_op jit(solution)/shard_map/ppermute | solution.py:12
  282.3 59.0 %collective-permute-start.24 = (f32[256,256]{1,0:T(8,128)}, f32[256,256]{1,0:T(8,128)}, u32[]{:S(2)}, u32[]{:S(2)}) collective-permute-start(f32[256,256]{1,0:T(8,128)} %get-tuple-element.17), channel_id=1, source_target_pairs={{1,0},{2,1},{3,2},{4,3},{5,4},{6,5},{7,6},{8,7},{9,8},{10,9},{11,1... | collective-permute-start | bytes 786440 | tf_op jit(solution)/shard_map/ppermute | solution.py:12
  283.6 59.0 %collective-permute-start.25 = (f32[256,256]{1,0:T(8,128)}, f32[256,256]{1,0:T(8,128)}, u32[]{:S(2)}, u32[]{:S(2)}) collective-permute-start(f32[256,256]{1,0:T(8,128)} %get-tuple-element.24), channel_id=1, source_target_pairs={{2,0},{3,1},{4,2},{5,3},{6,4},{7,5},{8,6},{9,7},{10,8},{11,9},{12,... | collective-permute-start | bytes 786440 | tf_op jit(solution)/shard_map/ppermute | solution.py:12
  293.0 0.7 copy-start.6
  293.7 50.2 %collective-permute-start.26 = (f32[256,256]{1,0:T(8,128)}, f32[256,256]{1,0:T(8,128)}, u32[]{:S(2)}, u32[]{:S(2)}) collective-permute-start(f32[256,256]{1,0:T(8,128)} %get-tuple-element.23), channel_id=1, source_target_pairs={{3,0},{4,1},{5,2},{6,3},{7,4},{8,5},{9,6},{10,7},{11,8},{12,9},{13... | collective-permute-start | bytes 786440 | tf_op jit(solution)/shard_map/ppermute | solution.py:12
  338.7 26.0 %collective-permute-start.27 = (f32[256,256]{1,0:T(8,128)}, f32[256,256]{1,0:T(8,128)S(1)}, u32[]{:S(2)}, u32[]{:S(2)}) collective-permute-start(f32[256,256]{1,0:T(8,128)} %get-tuple-element.22), channel_id=1, source_target_pairs={{4,0},{5,1},{6,2},{7,3},{8,4},{9,5},{10,6},{11,7},{12,8},{13,9},{1... | collective-permute-start | bytes 786440 | tf_op jit(solution)/shard_map/ppermute | solution.py:12
  340.0 27.7 %collective-permute-start.28 = (f32[256,256]{1,0:T(8,128)}, f32[256,256]{1,0:T(8,128)S(1)}, u32[]{:S(2)}, u32[]{:S(2)}) collective-permute-start(f32[256,256]{1,0:T(8,128)} %get-tuple-element.21), channel_id=1, source_target_pairs={{5,0},{6,1},{7,2},{8,3},{9,4},{10,5},{11,6},{12,7},{13,8},{14,9},{... | collective-permute-start | bytes 786440 | tf_op jit(solution)/shard_map/ppermute | solution.py:12
  341.3 26.4 %collective-permute-start.29 = (f32[256,256]{1,0:T(8,128)}, f32[256,256]{1,0:T(8,128)S(1)}, u32[]{:S(2)}, u32[]{:S(2)}) collective-permute-start(f32[256,256]{1,0:T(8,128)} %get-tuple-element.20), channel_id=1, source_target_pairs={{6,0},{7,1},{8,2},{9,3},{10,4},{11,5},{12,6},{13,7},{14,8},{15,9},... | collective-permute-start | bytes 786440 | tf_op jit(solution)/shard_map/ppermute | solution.py:12
  342.6 25.1 %collective-permute-start.30 = (f32[256,256]{1,0:T(8,128)}, f32[256,256]{1,0:T(8,128)S(1)}, u32[]{:S(2)}, u32[]{:S(2)}) collective-permute-start(f32[256,256]{1,0:T(8,128)} %get-tuple-element.19), channel_id=1, source_target_pairs={{7,0},{8,1},{9,2},{10,3},{11,4},{12,5},{13,6},{14,7},{15,8},{16,9}... | collective-permute-start | bytes 786440 | tf_op jit(solution)/shard_map/ppermute | solution.py:12
  343.9 33.6 %collective-permute-start.31 = (f32[256,256]{1,0:T(8,128)}, f32[256,256]{1,0:T(8,128)S(1)}, u32[]{:S(2)}, u32[]{:S(2)}) collective-permute-start(f32[256,256]{1,0:T(8,128)} %get-tuple-element.18), channel_id=1, source_target_pairs={{8,0},{9,1},{10,2},{11,3},{12,4},{13,5},{14,6},{15,7},{16,8},{17,9... | collective-permute-start | bytes 786440 | tf_op jit(solution)/shard_map/ppermute | solution.py:12
where the time goes:
time: 385 us; the launch traced here: 380 us
  matrix products  206 us (54%)
  starting transfers between devices  101 us (26%)
  waiting for transfers between devices  42.8 us (11%)
  local copies, waits for them, and re-layouts  17.7 us (5%)
  other arithmetic  11.1 us (3%)
    ppermute x40, starting transfers between devices, shifted(): lax.ppermute(value, axis, [(source, source + steps) for source in range(l...  101 us
    dot_general x1, matrix products, on_device(): grad_probs = jnp.einsum('rhd,kd->hrk', out_grad, val_window, precision=high)  47.4 us
    ppermute x40, waiting for transfers between devices, shifted(): lax.ppermute(value, axis, [(source, source + steps) for source in range(l...  42.8 us
    dot_general x1, matrix products, on_device(): jnp.einsum('rhd,kd->hrk', queries, key_window, precision=high) * factor  42.4 us
    dot_general x1, matrix products, on_device(): vals_grad = jnp.einsum('hrk,rhd->kd', probs, out_grad, precision=high)  41.5 us
    dot_general x1, matrix products, on_device(): jnp.einsum('hrk,kd->rhd', grad_scores, key_window, precision=high) * factor  38.3 us
    dot_general x1, matrix products, on_device(): jnp.einsum('hrk,rhd->kd', grad_scores, queries, precision=high) * factor  36.3 us
    unnamed x45, local copies, waits for them, and re-layouts  13.6 us
  transfers between devices with their start and end apart: 40, of which 5 were waited for; matrix products, arithmetic and copies ran while one was open for 60% of the time, Pallas kernels for 0%

commit v1 on v0

v1 whole, which is shorter than its diff:
```python
import functools
import math

import jax
import jax.numpy as jnp
from jax import lax
from jax.experimental import pallas as pl
from jax.experimental.pallas import tpu as pltpu
from jax.sharding import PartitionSpec as P

WIN = 2048
TILE = 256
LOG2E = math.log2(math.e)
LN2 = math.log(2.0)
MASKED = -1e30
NN = (((1,), (0,)), ((), ()))
NT = (((1,), (1,)), ((), ()))
F32 = jnp.float32
BF16 = jnp.bfloat16


def shifted(value, axis, steps):
    count = lax.axis_size(axis)
    leading, last = (max(0, -steps), min(count, count - steps))
    return lax.ppermute(value, axis, [(source, source + steps) for source in range(leading, last)])


def dot(a, b, dims):
    return lax.dot_general(a, b, dims, preferred_element_type=F32)


def halves(x):
    high = x.astype(BF16)
    return high, (x - high.astype(F32)).astype(BF16)


def kernel(blocks, slab_count, rows, has_sum, *refs):
    q_ref, g_ref, vec_ref, *rest = refs
    slabs, rest = rest[:slab_count], rest[slab_count:]
    sum_ref, rest = (rest[0], rest[1:]) if has_sum else (None, rest)
    dq_ref, rest = rest[0], rest[1:]
    outs, rest = rest[:slab_count], rest[slab_count:]
    k_hi, k_lo, kt_hi, kt_lo, v_hi, v_lo, dk_acc, dv_acc, first_ref = rest
    tile = pl.program_id(0)
    width = q_ref.shape[1]

    @pl.when(tile == 0)
    def _():
        dk_acc[...] = jnp.zeros_like(dk_acc)
        dv_acc[...] = jnp.zeros_like(dv_acc)
        for s, slab in enumerate(slabs):
            at = pl.ds(s * rows, rows)
            keys, values = slab[0:rows, :], slab[rows : 2 * rows, :]
            k_hi[at, :], k_lo[at, :] = halves(keys)
            kt_hi[:, at], kt_lo[:, at] = halves(keys.T)
            v_hi[at, :], v_lo[at, :] = halves(values)
            ids = slab[2 * rows :, :]
            same = jnp.where(ids == vec_ref[5:6, 0:1], F32(1), F32(0))
            count = jnp.sum(jnp.sum(same, axis=0, keepdims=True), axis=1, keepdims=True)
            first_ref[s : s + 1, :] = jnp.broadcast_to(rows - count, (1, TILE))

    q_hi, q_lo = halves(q_ref[...] * F32(LOG2E / math.sqrt(width)))
    g_hi, g_lo = halves(g_ref[...])
    log_norm, delta = vec_ref[0:1, :], vec_ref[1:2, :]

    def span(block):
        start, size, _ = block
        if callable(start):
            start = pl.multiple_of(start(tile), 128)
        return pl.ds(start, size), start

    def front(block):
        at, start = span(block)
        scores = dot(k_hi[at, :], q_hi, NT) + dot(k_lo[at, :], q_hi, NT) + dot(k_hi[at, :], q_lo, NT)
        grad_probs = dot(v_hi[at, :], g_hi, NT) + dot(v_lo[at, :], g_hi, NT) + dot(v_hi[at, :], g_lo, NT)
        return scores, grad_probs

    def back(block, scores, grad_probs, dqt):
        at, start = span(block)
        size, both = block[1], block[2]
        row = lax.broadcasted_iota(jnp.int32, (size, TILE), 0).astype(F32)
        if both:
            low = jnp.maximum(vec_ref[2:3, :], first_ref[0:1, :]) - lax.convert_element_type(start, F32)
            high = vec_ref[4:5, :] - lax.convert_element_type(start, F32)
            allowed = (row >= low) & (row <= high)
        else:
            allowed = row >= jnp.maximum(vec_ref[3:4, :], first_ref[start // rows : start // rows + 1, :])
        probs = jnp.exp2(jnp.where(allowed, scores - log_norm, F32(MASKED)))
        grad_scores = probs * (grad_probs - delta)
        p_hi, p_lo = halves(probs)
        s_hi, s_lo = halves(grad_scores)
        dv_acc[at, :] += dot(p_hi, g_hi, NN) + dot(p_lo, g_hi, NN) + dot(p_hi, g_lo, NN)
        dk_acc[at, :] += dot(s_hi, q_hi, NN) + dot(s_lo, q_hi, NN) + dot(s_hi, q_lo, NN)
        new = dot(kt_hi[:, at], s_hi, NN) + dot(kt_lo[:, at], s_hi, NN) + dot(kt_hi[:, at], s_lo, NN)
        return new if dqt is None else dqt + new

    dqt = None
    coming = front(blocks[0])
    for n, block in enumerate(blocks):
        here = coming
        if n + 1 < len(blocks):
            coming = front(blocks[n + 1])
        dqt = back(block, *here, dqt)
    dq = dqt.T * F32(1 / math.sqrt(width))
    dq_ref[...] = dq if sum_ref is None else dq + sum_ref[...]

    @pl.when(tile == pl.num_programs(0) - 1)
    def _():
        for s, out in enumerate(outs):
            at = pl.ds(s * rows, rows)
            out[0:rows, :] = dk_acc[at, :] * F32(LN2)
            out[rows : 2 * rows, :] = dv_acc[at, :]


def attend(blocks, q, g, vec, slabs, rows, dq_sum):
    total, width = q.shape
    count = len(slabs)
    keys = count * rows
    tiles = total // TILE
    tile_spec = pl.BlockSpec((TILE, width), lambda i: (i, 0))
    whole = lambda shape: pl.BlockSpec(shape, lambda i: (0, 0))
    sums = [] if dq_sum is None else [dq_sum]
    computed = sum(b[1] for b in blocks)
    results = pl.pallas_call(
        functools.partial(kernel, blocks, count, rows, bool(sums)),
        grid=(tiles,),
        in_specs=[tile_spec, tile_spec, pl.BlockSpec((8, TILE), lambda i: (0, i))]
        + [whole(slabs[0].shape)] * count
        + [tile_spec] * len(sums),
        out_specs=[tile_spec] + [whole((2 * rows, width))] * count,
        out_shape=[jax.ShapeDtypeStruct((total, width), F32)]
        + [jax.ShapeDtypeStruct((2 * rows, width), F32)] * count,
        scratch_shapes=[
            pltpu.VMEM((keys, width), BF16),
            pltpu.VMEM((keys, width), BF16),
            pltpu.VMEM((width, keys), BF16),
            pltpu.VMEM((width, keys), BF16),
            pltpu.VMEM((keys, width), BF16),
            pltpu.VMEM((keys, width), BF16),
            pltpu.VMEM((keys, width), F32),
            pltpu.VMEM((keys, width), F32),
            pltpu.VMEM((8, TILE), F32),
        ],
        compiler_params=pltpu.CompilerParams(vmem_limit_bytes=48 * 1024 * 1024),
        cost_estimate=pl.CostEstimate(
            flops=30 * total * computed * width, bytes_accessed=12 * total * width, transcendentals=total * computed
        ),
    )(q, g, vec, *slabs, *sums)
    return results[0], results[1:]


def on_device(queries, key_rows, value_rows, forward_out, out_grad, log_norm, doc_ids):
    rows, heads, width = queries.shape
    reach = WIN // rows
    ids = doc_ids.astype(F32) + 1.0
    if lax.axis_size("head") > 1:
        gather = functools.partial(lax.all_gather, axis_name="head", axis=0, tiled=True)
        key_rows, value_rows, ids = gather(key_rows), gather(value_rows), gather(ids)
    id_rows = 8 * pl.cdiv(rows, 8 * width)
    id_part = jnp.pad(ids, (0, id_rows * width - rows)).reshape(id_rows, width)
    own = jnp.concatenate([key_rows, value_rows, id_part], axis=0)
    slab = {0: own}
    for distance in [reach] + list(range(reach - 1, 0, -1)):
        slab[distance] = shifted(own, "seq", distance)

    token = jnp.arange(rows, dtype=F32)
    before = jnp.sum((ids[None, :] < ids[:, None]).astype(F32), axis=1)
    first = before == 0
    per_token = jnp.stack(
        [
            jnp.where(first, token + 1, rows + before),
            jnp.where(first, 0.0, 1e9),
            token + rows,
            jnp.broadcast_to(ids[0], (rows,)),
        ]
    )
    spread = jnp.broadcast_to(per_token[:, :, None], (4, rows, heads)).reshape(4, rows * heads)
    delta = jnp.sum(out_grad * forward_out, axis=-1).reshape(1, -1)
    scaled = (log_norm * F32(LOG2E)).reshape(1, -1)
    vec = jnp.concatenate([scaled, delta, spread, jnp.zeros((2, rows * heads), F32)], axis=0)

    q = queries.reshape(rows * heads, width)
    g = out_grad.reshape(rows * heads, width)
    tokens = TILE // heads
    edge = max(tokens, 128)
    edges = ((lambda i: (i * tokens) // edge * edge, rows + edge, True),)
    back = {}
    dq, (back[reach], own_part) = attend(edges, q, g, vec, [slab[reach], own], rows, None)
    middle = reach // 2
    groups = [list(range(reach - 1, middle - 1, -1)), list(range(middle - 1, 1, -1)), [1]]
    for group in groups:
        blocks = tuple((n * rows, rows, False) for n in range(len(group)))
        dq, parts = attend(blocks, q, g, vec, [slab[d] for d in group], rows, dq)
        back.update(zip(group, parts))
    for distance in [reach] + [d for group in groups for d in group]:
        own_part = own_part + shifted(back[distance], "seq", -distance)
    keys_grad, values_grad = own_part[:rows], own_part[rows:]
    if lax.axis_size("head") > 1:
        keys_grad, values_grad = (
            lax.psum_scatter(x, "head", scatter_dimension=0, tiled=True) for x in (keys_grad, values_grad)
        )
    return dq.reshape(rows, heads, width), keys_grad, values_grad


def solution(mesh):
    in_specs = (
        P("seq", "head", None),
        P(("seq", "head"), None),
        P(("seq", "head"), None),
        P("seq", "head", None),
        P("seq", "head", None),
        P("seq", "head"),
        P(("seq", "head")),
    )
    out_specs = (P("seq", "head", None), P(("seq", "head"), None), P(("seq", "head"), None))
    return jax.shard_map(
        on_device, mesh=mesh, in_specs=in_specs, out_specs=out_specs, check_vma=False
    )
```

time: 385 us -> 254 us (0.66)
  matrix products: 206 us -> 0 us
  Pallas kernels: 0 us -> 111 us
  starting transfers between devices: 101 us -> 36.4 us
  waiting for transfers between devices: 42.8 us -> 91.9 us
  local copies, waits for them, and re-layouts: 17.7 us -> 6.75 us
  other arithmetic: 11.1 us -> 6.19 us
    dot_general x5 -> x0, matrix products: 206 us -> none  [the longest x1 47.4 us: on_device(): grad_probs = jnp.einsum('rhd,kd->hrk', out_grad, val_window, precision=high)]
    pallas_call x0 -> x4, Pallas kernels: none -> 111 us  [attend(): pl.pallas_call(functools.partial(kernel, blocks, count, rows, bool(sums))...]
    ppermute x40 -> x16, starting transfers between devices: 101 us -> 36.4 us  [shifted(): lax.ppermute(value, axis, [(source, source + steps) for source in range(l...]
    ppermute x40 -> x16, waiting for transfers between devices: 42.8 us -> 91.9 us  [shifted(): lax.ppermute(value, axis, [(source, source + steps) for source in range(l...]
    unnamed x45 -> x4, local copies, waits for them, and re-layouts: 13.6 us -> 1.94 us
  transfers between devices with their start and end apart: 40 -> 16, of which waited for: 5 -> 4; matrix products, arithmetic and copies ran while one was open for 60% -> 4% of each run, Pallas kernels for 0% -> 37%
where the time goes in v1:
time: 254 us; the launch traced here: 253 us
  Pallas kernels  111 us (44%)
  waiting for transfers between devices  91.9 us (36%)
  starting transfers between devices  36.4 us (14%)
  local copies, waits for them, and re-layouts  6.75 us (3%)
  other arithmetic  6.19 us (2%)
    pallas_call x4, Pallas kernels, attend(): pl.pallas_call(functools.partial(kernel, blocks, count, rows, bool(sums))...  111 us
    ppermute x16, waiting for transfers between devices, shifted(): lax.ppermute(value, axis, [(source, source + steps) for source in range(l...  91.9 us
    ppermute x16, starting transfers between devices, shifted(): lax.ppermute(value, axis, [(source, source + steps) for source in range(l...  36.4 us
  transfers between devices with their start and end apart: 16, of which 4 were waited for; matrix products, arithmetic and copies ran while one was open for 4% of the time, Pallas kernels for 37%

profile of v1, /device:TPU:0, one launch (start us, length us, event | category | flops | bytes accessed | tf_op | source)
XLA Modules:
  0.0 252.6 jit_solution(7292858145956137174)
XLA Ops:
  0.6 0.7 convert_add_fusion
  1.3 1.0 constant_dynamic-update-slice_fusion.2
  2.3 1.0 constant_dynamic-update-slice_fusion.1
  3.3 5.0 %collective-permute-start.7 = (f32[520,256]{1,0:T(8,128)S(1)}, f32[520,256]{1,0:T(8,128)S(1)}, u32[]{:S(2)}, u32[]{:S(2)}) collective-permute-start(f32[520,256]{1,0:T(8,128)S(1)} %constant_dynamic-update-slice_fusion.refs_4_), channel_id=1, source_target_pairs={{0,8},{1,9},{2,10},{3,11},{4,12},{5,13},{6,14},{7,15},{8,16},{9,17... | collective-permute-start | bytes 1597448 | tf_op jit(solution)/shard_map/ppermute | solution.py:25
  8.3 3.5 %collective-permute-start.3 = (f32[520,256]{1,0:T(8,128)S(1)}, f32[520,256]{1,0:T(8,128)S(1)}, u32[]{:S(2)}, u32[]{:S(2)}) collective-permute-start(f32[520,256]{1,0:T(8,128)S(1)} %constant_dynamic-update-slice_fusion.refs_4_), channel_id=1, source_target_pairs={{0,7},{1,8},{2,9},{3,10},{4,11},{5,12},{6,13},{7,14},{8,15},{9,16}... | collective-permute-start | bytes 1597448 | tf_op jit(solution)/shard_map/ppermute | solution.py:25
  11.8 3.5 %collective-permute-start.4 = (f32[520,256]{1,0:T(8,128)S(1)}, f32[520,256]{1,0:T(8,128)S(1)}, u32[]{:S(2)}, u32[]{:S(2)}) collective-permute-start(f32[520,256]{1,0:T(8,128)S(1)} %constant_dynamic-update-slice_fusion.refs_4_), channel_id=1, source_target_pairs={{0,6},{1,7},{2,8},{3,9},{4,10},{5,11},{6,12},{7,13},{8,14},{9,15},... | collective-permute-start | bytes 1597448 | tf_op jit(solution)/shard_map/ppermute | solution.py:25
  15.3 3.7 %collective-permute-start.5 = (f32[520,256]{1,0:T(8,128)S(1)}, f32[520,256]{1,0:T(8,128)S(1)}, u32[]{:S(2)}, u32[]{:S(2)}) collective-permute-start(f32[520,256]{1,0:T(8,128)S(1)} %constant_dynamic-update-slice_fusion.refs_4_), channel_id=1, source_target_pairs={{0,5},{1,6},{2,7},{3,8},{4,9},{5,10},{6,11},{7,12},{8,13},{9,14},{... | collective-permute-start | bytes 1597448 | tf_op jit(solution)/shard_map/ppermute | solution.py:25
  19.0 3.4 %collective-permute-start.6 = (f32[520,256]{1,0:T(8,128)S(1)}, f32[520,256]{1,0:T(8,128)S(1)}, u32[]{:S(2)}, u32[]{:S(2)}) collective-permute-start(f32[520,256]{1,0:T(8,128)S(1)} %constant_dynamic-update-slice_fusion.refs_4_), channel_id=1, source_target_pairs={{0,4},{1,5},{2,6},{3,7},{4,8},{5,9},{6,10},{7,11},{8,12},{9,13},{1... | collective-permute-start | bytes 1597448 | tf_op jit(solution)/shard_map/ppermute | solution.py:25
  22.5 0.2 convert_reduce_fusion
  22.7 0.5 slice.9
  23.2 0.7 pad.12.clone
  23.9 0.1 maximum_maximum_fusion.1
  24.0 1.0 broadcast_in_dim.18
  25.0 1.3 reshape.72
  26.3 0.7 broadcast_multiply_fusion
  27.1 0.1 copy.12
  27.2 0.1 reshape.70
  27.3 4.1 %multiply_reduce_fusion = f32[256,16]{1,0:T(8,128)S(1)} fusion(f32[256,16,256]{2,1,0:T(8,128)} %param.11, f32[256,16,256]{2,1,0:T(8,128)} %param.10), kind=kLoop, calls=%fused_computation | loop fusion | flops 2093056 | bytes 8404992 | tf_op jit(solution)/shard_map/reduce_sum | solution.py:178
  31.4 0.1 reshape.71
  31.5 0.1 pad.8.clone
  31.6 0.1 maximum_maximum_fusion.refs_2_
  31.7 0.0 collective-permute-done.7.refs_3_
  31.7 1.9 collective-permute-start.1
  33.5 23.4 %shard_map.94 = (f32[4096,256]{1,0:T(8,128)}, f32[512,256]{1,0:T(8,128)S(1)}, f32[512,256]{1,0:T(8,128)S(1)}) custom-call(f32[4096,256]{1,0:T(8,128)} %bitcast.5, f32[4096,256]{1,0:T(8,128)} %bitcast.9, f32[8,4096]{1,0:T(8,128)S(1)} %maximum_maximum_fusion.refs_2_, f32[520,256]{1,0:T(8,128)S(1)} %collective-permute-done.7.refs_3_, ...), custom_call_target="tpu_custom_call" | custom-call | flops 12079595520 | bytes 12582912 | tf_op jit(solution)/shard_map/pallas_call | solution.py:124
  56.9 0.0 collective-permute-done.3.refs_3_
  56.9 3.8 %collective-permute-start.2 = (f32[520,256]{1,0:T(8,128)S(1)}, f32[520,256]{1,0:T(8,128)S(1)}, u32[]{:S(2)}, u32[]{:S(2)}) collective-permute-start(f32[520,256]{1,0:T(8,128)S(1)} %constant_dynamic-update-slice_fusion.refs_4_), channel_id=1, source_target_pairs={{0,2},{1,3},{2,4},{3,5},{4,6},{5,7},{6,8},{7,9},{8,10},{9,11},{10,... | collective-permute-start | bytes 1597448 | tf_op jit(solution)/shard_map/ppermute | solution.py:25
  60.7 0.0 collective-permute-done.4.refs_4_
  60.7 1.3 collective-permute-start
  62.1 0.0 collective-permute-done.5.refs_5_
  62.1 0.0 collective-permute-done.6.refs_6_
  62.1 42.8 %shard_map.95 = (f32[4096,256]{1,0:T(8,128)}, f32[512,256]{1,0:T(8,128)S(1)}, f32[512,256]{1,0:T(8,128)S(1)}, f32[512,256]{1,0:T(8,128)S(1)}, f32[512,256]{1,0:T(8,128)S(1)}) custom-call(f32[4096,256]{1,0:T(8,128)} %bitcast.6, f32[4096,256]{1,0:T(8,128)} %bitcast.10, f32[8,4096]{1,0:T(8,128)S(1)} %maximum_maximum_fusion.refs_2_, ...), custom_call_target="tpu_custom_call" | custom-call | flops 32212254720 | bytes 12582912 | tf_op jit(solution)/shard_map/pallas_call | solution.py:124
  104.9 0.0 collective-permute-done.1.refs_3_
  104.9 0.0 collective-permute-done.2.refs_4_
  104.9 0.0 copy-start
  104.9 26.2 %shard_map.96 = (f32[4096,256]{1,0:T(8,128)}, f32[512,256]{1,0:T(8,128)S(1)}, f32[512,256]{1,0:T(8,128)S(1)}) custom-call(f32[4096,256]{1,0:T(8,128)} %bitcast.7, f32[4096,256]{1,0:T(8,128)} %bitcast.11, f32[8,4096]{1,0:T(8,128)S(1)} %maximum_maximum_fusion.refs_2_, f32[520,256]{1,0:T(8,128)S(1)} %collective-permute-done.1.refs_3_, ...), custom_call_target="tpu_custom_call" | custom-call | flops 16106127360 | bytes 12582912 | tf_op jit(solution)/shard_map/pallas_call | solution.py:124
  131.1 0.0 collective-permute-done.refs_3_
  131.1 0.0 copy-done
  131.1 18.1 %shard_map.97 = (f32[4096,256]{1,0:T(8,128)}, f32[512,256]{1,0:T(8,128)S(1)}) custom-call(f32[4096,256]{1,0:T(8,128)S(1)} %bitcast.8, f32[4096,256]{1,0:T(8,128)} %bitcast.12, f32[8,4096]{1,0:T(8,128)S(1)} %maximum_maximum_fusion.refs_2_, f32[520,256]{1,0:T(8,128)S(1)} %collective-permute-done.refs_3_, f32[4096,256]{1,0:T(8,128)} %get-tuple-element.18.refs_4_), custom_call_target="tpu_custom_call" | custom-call | flops 8053063680 | bytes 12582912 | tf_op jit(solution)/shard_map/pallas_call | solution.py:124
  149.2 1.3 collective-permute-start.15
  150.5 1.3 collective-permute-start.13
  151.8 1.3 collective-permute-start.14
  153.1 1.3 collective-permute-start.10
  154.4 1.3 collective-permute-start.11
  155.7 0.0 collective-permute-done.15
  155.7 1.3 collective-permute-start.12
  157.0 11.7 %collective-permute-done.13 = f32[512,256]{1,0:T(8,128)S(1)} collective-permute-done((f32[512,256]{1,0:T(8,128)S(1)}, f32[512,256]{1,0:T(8,128)S(1)}, u32[]{:S(2)}, u32[]{:S(2)}) %collective-permute-start.13) | collective-permute-done | bytes 524320 | tf_op jit(solution)/shard_map/ppermute | solution.py:25
  168.7 1.3 collective-permute-start.9
  170.0 20.5 %collective-permute-done.14 = f32[512,256]{1,0:T(8,128)S(1)} collective-permute-done((f32[512,256]{1,0:T(8,128)S(1)}, f32[512,256]{1,0:T(8,128)S(1)}, u32[]{:S(2)}, u32[]{:S(2)}) %collective-permute-start.14) | collective-permute-done | bytes 524320 | tf_op jit(solution)/shard_map/ppermute | solution.py:25
  190.6 1.3 collective-permute-start.8
  191.8 0.0 collective-permute-done.10
  191.8 0.0 collective-permute-done.11
  191.9 12.9 %collective-permute-done.12 = f32[512,256]{1,0:T(8,128)S(1)} collective-permute-done((f32[512,256]{1,0:T(8,128)S(1)}, f32[512,256]{1,0:T(8,128)S(1)}, u32[]{:S(2)}, u32[]{:S(2)}) %collective-permute-start.12) | collective-permute-done | bytes 524320 | tf_op jit(solution)/shard_map/ppermute | solution.py:25
  204.8 0.0 collective-permute-done.9
  204.8 46.7 %collective-permute-done.8 = f32[512,256]{1,0:T(8,128)S(1)} collective-permute-done((f32[512,256]{1,0:T(8,128)S(1)}, f32[512,256]{1,0:T(8,128)S(1)}, u32[]{:S(2)}, u32[]{:S(2)}) %collective-permute-start.8) | collective-permute-done | bytes 524320 | tf_op jit(solution)/shard_map/ppermute | solution.py:25
  251.5 0.3 add_add_fusion
  251.8 0.8 fusion
  (7 shorter events, 0.0 us)
Async XLA Ops:
  3.3 28.4 %collective-permute-start.7 = (f32[520,256]{1,0:T(8,128)S(1)}, f32[520,256]{1,0:T(8,128)S(1)}, u32[]{:S(2)}, u32[]{:S(2)}) collective-permute-start(f32[520,256]{1,0:T(8,128)S(1)} %constant_dynamic-update-slice_fusion.refs_4_), channel_id=1, source_target_pairs={{0,8},{1,9},{2,10},{3,11},{4,12},{5,13},{6,14},{7,15},{8,16},{9,17... | collective-permute-start | bytes 1597448 | tf_op jit(solution)/shard_map/ppermute | solution.py:25
  8.3 48.7 %collective-permute-start.3 = (f32[520,256]{1,0:T(8,128)S(1)}, f32[520,256]{1,0:T(8,128)S(1)}, u32[]{:S(2)}, u32[]{:S(2)}) collective-permute-start(f32[520,256]{1,0:T(8,128)S(1)} %constant_dynamic-update-slice_fusion.refs_4_), channel_id=1, source_target_pairs={{0,7},{1,8},{2,9},{3,10},{4,11},{5,12},{6,13},{7,14},{8,15},{9,16}... | collective-permute-start | bytes 1597448 | tf_op jit(solution)/shard_map/ppermute | solution.py:25
  11.8 48.9 %collective-permute-start.4 = (f32[520,256]{1,0:T(8,128)S(1)}, f32[520,256]{1,0:T(8,128)S(1)}, u32[]{:S(2)}, u32[]{:S(2)}) collective-permute-start(f32[520,256]{1,0:T(8,128)S(1)} %constant_dynamic-update-slice_fusion.refs_4_), channel_id=1, source_target_pairs={{0,6},{1,7},{2,8},{3,9},{4,10},{5,11},{6,12},{7,13},{8,14},{9,15},... | collective-permute-start | bytes 1597448 | tf_op jit(solution)/shard_map/ppermute | solution.py:25
  15.3 46.8 %collective-permute-start.5 = (f32[520,256]{1,0:T(8,128)S(1)}, f32[520,256]{1,0:T(8,128)S(1)}, u32[]{:S(2)}, u32[]{:S(2)}) collective-permute-start(f32[520,256]{1,0:T(8,128)S(1)} %constant_dynamic-update-slice_fusion.refs_4_), channel_id=1, source_target_pairs={{0,5},{1,6},{2,7},{3,8},{4,9},{5,10},{6,11},{7,12},{8,13},{9,14},{... | collective-permute-start | bytes 1597448 | tf_op jit(solution)/shard_map/ppermute | solution.py:25
  19.0 43.0 %collective-permute-start.6 = (f32[520,256]{1,0:T(8,128)S(1)}, f32[520,256]{1,0:T(8,128)S(1)}, u32[]{:S(2)}, u32[]{:S(2)}) collective-permute-start(f32[520,256]{1,0:T(8,128)S(1)} %constant_dynamic-update-slice_fusion.refs_4_), channel_id=1, source_target_pairs={{0,4},{1,5},{2,6},{3,7},{4,8},{5,9},{6,10},{7,11},{8,12},{9,13},{1... | collective-permute-start | bytes 1597448 | tf_op jit(solution)/shard_map/ppermute | solution.py:25
  31.7 73.2 %collective-permute-start.1 = (f32[520,256]{1,0:T(8,128)S(1)}, f32[520,256]{1,0:T(8,128)S(1)}, u32[]{:S(2)}, u32[]{:S(2)}) collective-permute-start(f32[520,256]{1,0:T(8,128)S(1)} %constant_dynamic-update-slice_fusion.refs_4_), channel_id=1, source_target_pairs={{0,3},{1,4},{2,5},{3,6},{4,7},{5,8},{6,9},{7,10},{8,11},{9,12},{10... | collective-permute-start | bytes 1597448 | tf_op jit(solution)/shard_map/ppermute | solution.py:25
  56.9 48.0 %collective-permute-start.2 = (f32[520,256]{1,0:T(8,128)S(1)}, f32[520,256]{1,0:T(8,128)S(1)}, u32[]{:S(2)}, u32[]{:S(2)}) collective-permute-start(f32[520,256]{1,0:T(8,128)S(1)} %constant_dynamic-update-slice_fusion.refs_4_), channel_id=1, source_target_pairs={{0,2},{1,3},{2,4},{3,5},{4,6},{5,7},{6,8},{7,9},{8,10},{9,11},{10,... | collective-permute-start | bytes 1597448 | tf_op jit(solution)/shard_map/ppermute | solution.py:25
  60.7 70.4 %collective-permute-start = (f32[520,256]{1,0:T(8,128)S(1)}, f32[520,256]{1,0:T(8,128)S(1)}, u32[]{:S(2)}, u32[]{:S(2)}) collective-permute-start(f32[520,256]{1,0:T(8,128)S(1)} %constant_dynamic-update-slice_fusion.refs_4_), channel_id=1, source_target_pairs={{0,1},{1,2},{2,3},{3,4},{4,5},{5,6},{6,7},{7,8},{8,9},{9,10},{10,1... | collective-permute-start | bytes 1597448 | tf_op jit(solution)/shard_map/ppermute | solution.py:25
  104.9 26.2 %copy-start = (f32[256,16,256]{2,1,0:T(8,128)S(1)}, f32[256,16,256]{2,1,0:T(8,128)}, u32[]{:S(2)}) copy-start(f32[256,16,256]{2,1,0:T(8,128)} %param.7) | copy-start | bytes 12582916
  149.2 6.5 %collective-permute-start.15 = (f32[512,256]{1,0:T(8,128)S(1)}, f32[512,256]{1,0:T(8,128)S(1)}, u32[]{:S(2)}, u32[]{:S(2)}) collective-permute-start(f32[512,256]{1,0:T(8,128)S(1)} %get-tuple-element.28), channel_id=1, source_target_pairs={{1,0},{2,1},{3,2},{4,3},{5,4},{6,5},{7,6},{8,7},{9,8},{10,9},{11,1... | collective-permute-start | bytes 1572872 | tf_op jit(solution)/shard_map/ppermute | solution.py:25
  150.5 18.2 %collective-permute-start.13 = (f32[512,256]{1,0:T(8,128)S(1)}, f32[512,256]{1,0:T(8,128)S(1)}, u32[]{:S(2)}, u32[]{:S(2)}) collective-permute-start(f32[512,256]{1,0:T(8,128)S(1)} %get-tuple-element.26), channel_id=1, source_target_pairs={{3,0},{4,1},{5,2},{6,3},{7,4},{8,5},{9,6},{10,7},{11,8},{12,9},{13... | collective-permute-start | bytes 1572872 | tf_op jit(solution)/shard_map/ppermute | solution.py:25
  151.8 38.7 %collective-permute-start.14 = (f32[512,256]{1,0:T(8,128)S(1)}, f32[512,256]{1,0:T(8,128)S(1)}, u32[]{:S(2)}, u32[]{:S(2)}) collective-permute-start(f32[512,256]{1,0:T(8,128)S(1)} %get-tuple-element.27), channel_id=1, source_target_pairs={{2,0},{3,1},{4,2},{5,3},{6,4},{7,5},{8,6},{9,7},{10,8},{11,9},{12,... | collective-permute-start | bytes 1572872 | tf_op jit(solution)/shard_map/ppermute | solution.py:25
  153.1 38.7 %collective-permute-start.10 = (f32[512,256]{1,0:T(8,128)S(1)}, f32[512,256]{1,0:T(8,128)S(1)}, u32[]{:S(2)}, u32[]{:S(2)}) collective-permute-start(f32[512,256]{1,0:T(8,128)S(1)} %get-tuple-element.23), channel_id=1, source_target_pairs={{6,0},{7,1},{8,2},{9,3},{10,4},{11,5},{12,6},{13,7},{14,8},{15,9},... | collective-permute-start | bytes 1572872 | tf_op jit(solution)/shard_map/ppermute | solution.py:25
  154.4 37.4 %collective-permute-start.11 = (f32[512,256]{1,0:T(8,128)S(1)}, f32[512,256]{1,0:T(8,128)S(1)}, u32[]{:S(2)}, u32[]{:S(2)}) collective-permute-start(f32[512,256]{1,0:T(8,128)S(1)} %get-tuple-element.24), channel_id=1, source_target_pairs={{5,0},{6,1},{7,2},{8,3},{9,4},{10,5},{11,6},{12,7},{13,8},{14,9},{... | collective-permute-start | bytes 1572872 | tf_op jit(solution)/shard_map/ppermute | solution.py:25
  155.7 49.0 %collective-permute-start.12 = (f32[512,256]{1,0:T(8,128)S(1)}, f32[512,256]{1,0:T(8,128)S(1)}, u32[]{:S(2)}, u32[]{:S(2)}) collective-permute-start(f32[512,256]{1,0:T(8,128)S(1)} %get-tuple-element.25), channel_id=1, source_target_pairs={{4,0},{5,1},{6,2},{7,3},{8,4},{9,5},{10,6},{11,7},{12,8},{13,9},{1... | collective-permute-start | bytes 1572872 | tf_op jit(solution)/shard_map/ppermute | solution.py:25
  168.7 36.0 %collective-permute-start.9 = (f32[512,256]{1,0:T(8,128)S(1)}, f32[512,256]{1,0:T(8,128)S(1)}, u32[]{:S(2)}, u32[]{:S(2)}) collective-permute-start(f32[512,256]{1,0:T(8,128)S(1)} %get-tuple-element.22), channel_id=1, source_target_pairs={{7,0},{8,1},{9,2},{10,3},{11,4},{12,5},{13,6},{14,7},{15,8},{16,9}... | collective-permute-start | bytes 1572872 | tf_op jit(solution)/shard_map/ppermute | solution.py:25
  190.6 60.9 %collective-permute-start.8 = (f32[512,256]{1,0:T(8,128)S(1)}, f32[512,256]{1,0:T(8,128)S(1)}, u32[]{:S(2)}, u32[]{:S(2)}) collective-permute-start(f32[512,256]{1,0:T(8,128)S(1)} %get-tuple-element.21), channel_id=1, source_target_pairs={{8,0},{9,1},{10,2},{11,3},{12,4},{13,5},{14,6},{15,7},{16,8},{17,9... | collective-permute-start | bytes 1572872 | tf_op jit(solution)/shard_map/ppermute | solution.py:25

commit v2 on v1

v2 whole, which is shorter than its diff:
```python
import functools
import math

import jax
import jax.numpy as jnp
from jax import lax
from jax.experimental import pallas as pl
from jax.experimental.pallas import tpu as pltpu
from jax.sharding import PartitionSpec as P


WIN = 2048
TILE = 256
LOG2E = math.log2(math.e)
LN2 = math.log(2.0)
MASKED = -1e30
NN = (((1,), (0,)), ((), ()))
NT = (((1,), (1,)), ((), ()))
F32 = jnp.float32
BF16 = jnp.bfloat16


def shifted(value, axis, steps):
    count = lax.axis_size(axis)
    leading, last = (max(0, -steps), min(count, count - steps))
    return lax.ppermute(value, axis, [(source, source + steps) for source in range(leading, last)])


def swapped(value, axis):
    count = lax.axis_size(axis)
    return lax.ppermute(value, axis, [(source, source ^ 1) for source in range(count)])


def dot(a, b, dims):
    return lax.dot_general(a, b, dims, preferred_element_type=F32)


def halves(x):
    high = x.astype(BF16)
    return high, (x - high.astype(F32)).astype(BF16)


def kernel(blocks, sources, steps, rows, has_sum, *refs):
    operands = 1 + max(max(s) if isinstance(s, tuple) else s for s in sources)
    q_ref, g_ref, vec_ref, *rest = refs
    slabs, rest = rest[:operands], rest[operands:]
    sum_ref, rest = (rest[0], rest[1:]) if has_sum else (None, rest)
    dq_ref, rest = rest[0], rest[1:]
    outs, rest = rest[: len(sources)], rest[len(sources) :]
    k_hi, k_lo, kt_hi, kt_lo, v_hi, v_lo, dk_acc, dv_acc, first_ref = rest
    step = pl.program_id(0)
    width = q_ref.shape[1]

    @pl.when(step == 0)
    def _():
        dk_acc[...] = jnp.zeros_like(dk_acc)
        dv_acc[...] = jnp.zeros_like(dv_acc)
        odd = vec_ref[6:7, 0:1] > 0.5

        def part(source, at):
            if isinstance(source, tuple):
                return jnp.where(odd, slabs[source[1]][at, :], slabs[source[0]][at, :])
            return slabs[source][at, :]

        for s, source in enumerate(sources):
            at = pl.ds(s * rows, rows)
            keys, values = part(source, pl.ds(0, rows)), part(source, pl.ds(rows, rows))
            k_hi[at, :], k_lo[at, :] = halves(keys)
            kt_hi[:, at], kt_lo[:, at] = halves(keys.T)
            v_hi[at, :], v_lo[at, :] = halves(values)
            ids = part(source, pl.ds(2 * rows, slabs[0].shape[0] - 2 * rows))
            same = jnp.where(ids == vec_ref[5:6, 0:1], F32(1), F32(0))
            count = jnp.sum(jnp.sum(same, axis=0, keepdims=True), axis=1, keepdims=True)
            first_ref[s : s + 1, :] = jnp.broadcast_to(rows - count, (1, TILE))

    ready = {}

    def load(tile):
        if tile not in ready:
            at = pl.ds(tile * TILE, TILE)
            ready[tile] = (
                *halves(q_ref[at, :] * F32(LOG2E / math.sqrt(width))),
                *halves(g_ref[at, :]),
                vec_ref[:, at],
            )
        return ready[tile]

    def span(tile, block):
        start, size, _ = block
        if callable(start):
            start = pl.multiple_of(start(step * steps + tile), 128)
        return pl.ds(start, size), start

    def front(tile, block):
        q_hi, q_lo, g_hi, g_lo, _ = load(tile)
        at, _ = span(tile, block)
        scores = dot(k_hi[at, :], q_hi, NT) + dot(k_lo[at, :], q_hi, NT) + dot(k_hi[at, :], q_lo, NT)
        grad_probs = dot(v_hi[at, :], g_hi, NT) + dot(v_lo[at, :], g_hi, NT) + dot(v_hi[at, :], g_lo, NT)
        return scores, grad_probs

    totals = {}

    def back(tile, block, scores, grad_probs):
        q_hi, q_lo, g_hi, g_lo, vec = load(tile)
        at, start = span(tile, block)
        size, both = block[1], block[2]
        row = lax.broadcasted_iota(jnp.int32, (size, TILE), 0).astype(F32)
        if both:
            base = lax.convert_element_type(start, F32)
            low = jnp.maximum(vec[2:3, :], first_ref[0:1, :]) - base
            allowed = (row >= low) & (row <= vec[4:5, :] - base)
        else:
            allowed = row >= jnp.maximum(vec[3:4, :], first_ref[start // rows : start // rows + 1, :])
        probs = jnp.exp2(jnp.where(allowed, scores - vec[0:1, :], F32(MASKED)))
        grad_scores = probs * (grad_probs - vec[1:2, :])
        p_hi, p_lo = halves(probs)
        s_hi, s_lo = halves(grad_scores)
        dv_acc[at, :] += dot(p_hi, g_hi, NN) + dot(p_lo, g_hi, NN) + dot(p_hi, g_lo, NN)
        dk_acc[at, :] += dot(s_hi, q_hi, NN) + dot(s_lo, q_hi, NN) + dot(s_hi, q_lo, NN)
        new = dot(kt_hi[:, at], s_hi, NN) + dot(kt_lo[:, at], s_hi, NN) + dot(kt_hi[:, at], s_lo, NN)
        totals[tile] = totals[tile] + new if tile in totals else new

    work = [(tile, n) for tile in range(steps) for n in range(len(blocks))]
    coming = front(work[0][0], blocks[work[0][1]])
    for order, (tile, n) in enumerate(work):
        here = coming
        if order + 1 < len(work):
            coming = front(work[order + 1][0], blocks[work[order + 1][1]])
        back(tile, blocks[n], *here)
        if n + 1 == len(blocks):
            at = pl.ds(tile * TILE, TILE)
            dq = totals[tile].T * F32(1 / math.sqrt(width))
            dq_ref[at, :] = dq if sum_ref is None else dq + sum_ref[at, :]

    @pl.when(step == pl.num_programs(0) - 1)
    def _():
        for s, out in enumerate(outs):
            at = pl.ds(s * rows, rows)
            out[0:rows, :] = dk_acc[at, :] * F32(LN2)
            out[rows : 2 * rows, :] = dv_acc[at, :]


def attend(blocks, sources, q, g, vec, slabs, rows, dq_sum):
    total, width = q.shape
    count = len(sources)
    keys = count * rows
    tiles = total // TILE
    steps = math.gcd(tiles, 4)
    tile_spec = pl.BlockSpec((steps * TILE, width), lambda i: (i, 0))
    whole = lambda shape: pl.BlockSpec(shape, lambda i: (0, 0))
    sums = [] if dq_sum is None else [dq_sum]
    computed = sum(b[1] for b in blocks)
    results = pl.pallas_call(
        functools.partial(kernel, blocks, sources, steps, rows, bool(sums)),
        grid=(tiles // steps,),
        in_specs=[tile_spec, tile_spec, pl.BlockSpec((8, steps * TILE), lambda i: (0, i))]
        + [whole(slabs[0].shape)] * len(slabs)
        + [tile_spec] * len(sums),
        out_specs=[tile_spec] + [whole((2 * rows, width))] * count,
        out_shape=[jax.ShapeDtypeStruct((total, width), F32)]
        + [jax.ShapeDtypeStruct((2 * rows, width), F32)] * count,
        scratch_shapes=[
            pltpu.VMEM((keys, width), BF16),
            pltpu.VMEM((keys, width), BF16),
            pltpu.VMEM((width, keys), BF16),
            pltpu.VMEM((width, keys), BF16),
            pltpu.VMEM((keys, width), BF16),
            pltpu.VMEM((keys, width), BF16),
            pltpu.VMEM((keys, width), F32),
            pltpu.VMEM((keys, width), F32),
            pltpu.VMEM((8, TILE), F32),
        ],
        compiler_params=pltpu.CompilerParams(vmem_limit_bytes=63 * 1024 * 1024),
        cost_estimate=pl.CostEstimate(
            flops=30 * total * computed * width, bytes_accessed=12 * total * width, transcendentals=total * computed
        ),
    )(q, g, vec, *slabs, *sums)
    return results[0], results[1:]


def program(queries, key_rows, value_rows, forward_out, out_grad, log_norm, doc_ids):
    rows, heads, width = queries.shape
    reach = WIN // rows
    ids = doc_ids.astype(F32) + 1.0
    if lax.axis_size("head") > 1:
        gather = functools.partial(lax.all_gather, axis_name="head", axis=0, tiled=True)
        key_rows, value_rows, ids = gather(key_rows), gather(value_rows), gather(ids)
    id_rows = 8 * pl.cdiv(rows, 8 * width)
    id_part = jnp.pad(ids, (0, id_rows * width - rows)).reshape(id_rows, width)
    own = jnp.concatenate([key_rows, value_rows, id_part], axis=0)
    odd = lax.axis_index("seq") % 2 == 1

    mine, other = {0: own}, {}
    for distance in range(reach, 0, -2):
        mine[distance] = shifted(own, "seq", distance)
    for distance in range(reach, -1, -2):
        other[distance] = swapped(mine[distance], "seq")

    token = jnp.arange(rows, dtype=F32)
    before = jnp.sum((ids[None, :] < ids[:, None]).astype(F32), axis=1)
    first = before == 0
    per_token = jnp.stack(
        [
            jnp.where(first, token + 1, rows + before),
            jnp.where(first, 0.0, 1e9),
            token + rows,
            jnp.broadcast_to(ids[0], (rows,)),
            jnp.broadcast_to(odd.astype(F32), (rows,)),
        ]
    )
    spread = jnp.broadcast_to(per_token[:, :, None], (5, rows, heads)).reshape(5, rows * heads)
    delta = jnp.sum(out_grad * forward_out, axis=-1).reshape(1, -1)
    scaled = (log_norm * F32(LOG2E)).reshape(1, -1)
    vec = jnp.concatenate([scaled, delta, spread, jnp.zeros((1, rows * heads), F32)], axis=0)

    q = queries.reshape(rows * heads, width)
    g = out_grad.reshape(rows * heads, width)
    tokens = TILE // heads
    edge = max(tokens, 128)
    edges = ((lambda i: (i * tokens) // edge * edge, rows + edge, True), (2 * rows, rows, False))
    dq, (far, own_part, cross) = attend(
        edges, (0, 1, (2, 3)), q, g, vec, [mine[reach], own, other[reach], other[0]], rows, None
    )
    cross = swapped(cross, "seq")
    far = far + jnp.where(odd, cross, 0.0)
    own_part = own_part + jnp.where(odd, 0.0, cross)
    returned = [shifted(far, "seq", -reach)]
    rest = list(range(reach - 2, 0, -2))
    groups = [rest[:-1], rest[-1:]] if len(rest) > 1 else [rest]
    for group in groups:
        slabs = [x for d in group for x in (mine[d], other[d])]
        blocks = tuple((s * rows, rows, False) for s in range(len(slabs)))
        dq, parts = attend(blocks, tuple(range(len(slabs))), q, g, vec, slabs, rows, dq)
        for s, d in enumerate(group):
            handed = swapped(parts[2 * s + 1], "seq")
            joined = parts[2 * s] + handed
            returned.append(shifted(joined, "seq", -d))
    for part in returned:
        own_part = own_part + part
    keys_grad, values_grad = own_part[:rows], own_part[rows:]
    if lax.axis_size("head") > 1:
        keys_grad, values_grad = (
            lax.psum_scatter(x, "head", scatter_dimension=0, tiled=True) for x in (keys_grad, values_grad)
        )
    return dq.reshape(rows, heads, width), keys_grad, values_grad


def solution(mesh):
    in_specs = (
        P("seq", "head", None),
        P(("seq", "head"), None),
        P(("seq", "head"), None),
        P("seq", "head", None),
        P("seq", "head", None),
        P("seq", "head"),
        P(("seq", "head")),
    )
    out_specs = (P("seq", "head", None), P(("seq", "head"), None), P(("seq", "head"), None))
    return jax.shard_map(program, mesh=mesh, in_specs=in_specs, out_specs=out_specs, check_vma=False)
```

time: 254 us -> 201 us (0.79)
  the two profiles are of different devices: /device:TPU:0 before, /device:TPU:6 now
where the time goes in v2:
time: 201 us
  Pallas kernels  90.8 us (45%)
  waiting for transfers between devices  69.1 us (34%)
  starting transfers between devices  23 us (11%)
  other arithmetic  10.5 us (5%)
  local copies, waits for them, and re-layouts  6.52 us (3%)
    pallas_call x3, Pallas kernels, attend(): pl.pallas_call(functools.partial(kernel, blocks, sources, steps, rows, bo...  90.8 us
    ppermute x8, waiting for transfers between devices, shifted(): lax.ppermute(value, axis, [(source, source + steps) for source in range(l...  69.1 us
    ppermute x8, starting transfers between devices, shifted(): lax.ppermute(value, axis, [(source, source + steps) for source in range(l...  21.7 us
    reduce_sum x1, other arithmetic, program(): delta = jnp.sum(out_grad * forward_out, axis=-1).reshape(1, -1)  4.1 us
  transfers between devices with their start and end apart: 17, of which 7 were waited for; matrix products, arithmetic and copies ran while one was open for 6% of the time, Pallas kernels for 45%

profile of v2, /device:TPU:6, one launch (start us, length us, event | category | flops | bytes accessed | tf_op | source)
XLA Modules:
  0.0 200.9 jit_solution(4294958097343179895)
XLA Ops:
  0.6 0.7 convert_add_fusion
  1.3 1.0 constant_dynamic-update-slice_fusion.2
  2.3 1.0 constant_dynamic-update-slice_fusion.1
  3.3 0.0 copy-start.2
  3.3 3.5 %collective-permute-start.6 = (f32[520,256]{1,0:T(8,128)S(1)}, f32[520,256]{1,0:T(8,128)S(1)}, u32[]{:S(2)}, u32[]{:S(2)}) collective-permute-start(f32[520,256]{1,0:T(8,128)S(1)} %constant_dynamic-update-slice_fusion.refs_4_), channel_id=1, source_target_pairs={{0,8},{1,9},{2,10},{3,11},{4,12},{5,13},{6,14},{7,15},{8,16},{9,17... | collective-permute-start | bytes 1597448 | tf_op jit(solution)/shard_map/ppermute | solution.py:26
  6.8 0.1 collective-permute-start.8
  6.9 3.4 %collective-permute-start.2 = (f32[520,256]{1,0:T(8,128)S(1)}, f32[520,256]{1,0:T(8,128)}, u32[]{:S(2)}, u32[]{:S(2)}) collective-permute-start(f32[520,256]{1,0:T(8,128)S(1)} %constant_dynamic-update-slice_fusion.refs_4_), channel_id=1, source_target_pairs={{0,6},{1,7},{2,8},{3,9},{4,10},{5,11},{6,12},{7,13},{8,14},{9,15},... | collective-permute-start | bytes 1597448 | tf_op jit(solution)/shard_map/ppermute | solution.py:26
  10.3 3.4 %collective-permute-start.4 = (f32[520,256]{1,0:T(8,128)S(1)}, f32[520,256]{1,0:T(8,128)}, u32[]{:S(2)}, u32[]{:S(2)}) collective-permute-start(f32[520,256]{1,0:T(8,128)S(1)} %constant_dynamic-update-slice_fusion.refs_4_), channel_id=1, source_target_pairs={{0,4},{1,5},{2,6},{3,7},{4,8},{5,9},{6,10},{7,11},{8,12},{9,13},{1... | collective-permute-start | bytes 1597448 | tf_op jit(solution)/shard_map/ppermute | solution.py:26
  13.8 4.3 %collective-permute-start = (f32[520,256]{1,0:T(8,128)S(1)}, f32[520,256]{1,0:T(8,128)}, u32[]{:S(2)}, u32[]{:S(2)}) collective-permute-start(f32[520,256]{1,0:T(8,128)S(1)} %constant_dynamic-update-slice_fusion.refs_4_), channel_id=1, source_target_pairs={{0,2},{1,3},{2,4},{3,5},{4,6},{5,7},{6,8},{7,9},{8,10},{9,11},{10,... | collective-permute-start | bytes 1597448 | tf_op jit(solution)/shard_map/ppermute | solution.py:26
  18.1 0.2 convert_reduce_fusion
  18.3 0.7 broadcast_multiply_fusion
  19.0 0.5 slice.9
  19.5 0.6 stack_broadcast_in_dim.6
  20.2 0.2 broadcast_in_dim.24
  20.4 0.3 reshape.72
  20.8 0.1 copy.12
  20.9 0.1 reshape.70
  21.0 4.1 %multiply_reduce_fusion = f32[256,16]{1,0:T(8,128)S(1)} fusion(f32[256,16,256]{2,1,0:T(8,128)} %param.11, f32[256,16,256]{2,1,0:T(8,128)} %param.10), kind=kLoop, calls=%fused_computation | loop fusion | flops 2093056 | bytes 8404992 | tf_op jit(solution)/shard_map/reduce_sum | solution.py:212
  25.1 0.0 copy-done.2
  25.1 0.1 reshape.71
  25.2 0.1 pad.8.clone
  25.3 0.0 collective-permute-done.6.refs_3_
  25.3 0.0 collective-permute-start.7
  25.4 0.8 maximum_maximum_fusion.refs_2_
  26.2 4.5 %collective-permute-done.2.refs_3_ = f32[520,256]{1,0:T(8,128)} collective-permute-done((f32[520,256]{1,0:T(8,128)S(1)}, f32[520,256]{1,0:T(8,128)}, u32[]{:S(2)}, u32[]{:S(2)}) %collective-permute-start.2) | collective-permute-done | bytes 532512 | tf_op jit(solution)/shard_map/ppermute | solution.py:26
  30.7 0.0 collective-permute-start.3
  30.7 11.4 %collective-permute-done.4.refs_5_ = f32[520,256]{1,0:T(8,128)} collective-permute-done((f32[520,256]{1,0:T(8,128)S(1)}, f32[520,256]{1,0:T(8,128)}, u32[]{:S(2)}, u32[]{:S(2)}) %collective-permute-start.4) | collective-permute-done | bytes 532512 | tf_op jit(solution)/shard_map/ppermute | solution.py:26
  42.1 0.0 collective-permute-start.5
  42.1 10.3 %collective-permute-done.refs_3_ = f32[520,256]{1,0:T(8,128)} collective-permute-done((f32[520,256]{1,0:T(8,128)S(1)}, f32[520,256]{1,0:T(8,128)}, u32[]{:S(2)}, u32[]{:S(2)}) %collective-permute-start) | collective-permute-done | bytes 532512 | tf_op jit(solution)/shard_map/ppermute | solution.py:26
  52.4 0.0 collective-permute-start.1
  52.4 0.0 collective-permute-done.8.refs_6_
  52.4 0.0 copy-done.3
  52.4 0.0 collective-permute-done.7.refs_5_
  52.4 0.8 copy-done.4
  53.2 0.8 copy-done.5
  54.0 27.4 %shard_map.94 = (f32[4096,256]{1,0:T(8,128)}, f32[512,256]{1,0:T(8,128)}, f32[512,256]{1,0:T(8,128)}, f32[512,256]{1,0:T(8,128)}) custom-call(f32[4096,256]{1,0:T(8,128)} %bitcast.10, f32[4096,256]{1,0:T(8,128)} %bitcast.6, f32[8,4096]{1,0:T(8,128)} %maximum_maximum_fusion.refs_2_, f32[520,256]{1,0:T(8,128)} %copy-done.3, f32[520,256]{1,0:T(8,128)} %copy-done.2, ...), custom_call_target="tpu_custom_call" | custom-call | flops 20132659200 | bytes 12582912 | tf_op jit(solution)/shard_map/pallas_call | solution.py:153
  81.4 0.0 collective-permute-done.3.refs_4_
  81.4 0.0 collective-permute-done.5.refs_6_
  81.4 40.3 %shard_map.95 = (f32[4096,256]{1,0:T(8,128)}, f32[512,256]{1,0:T(8,128)}, f32[512,256]{1,0:T(8,128)}, f32[512,256]{1,0:T(8,128)}, f32[512,256]{1,0:T(8,128)}) custom-call(f32[4096,256]{1,0:T(8,128)} %bitcast.11, f32[4096,256]{1,0:T(8,128)} %bitcast.7, f32[8,4096]{1,0:T(8,128)} %maximum_maximum_fusion.refs_2_, f32[520,256]{1,0:T(8,128)} %collective-permute-done.2.refs_3_, ...), custom_call_target="tpu_custom_call" | custom-call | flops 32212254720 | bytes 12582912 | tf_op jit(solution)/shard_map/pallas_call | solution.py:153
  121.8 0.6 collective-permute-start.11
  122.3 0.1 collective-permute-start.9
  122.4 0.4 collective-permute-start.13
  122.8 0.0 collective-permute-done.1.refs_4_
  122.8 23.1 %shard_map.96 = (f32[4096,256]{1,0:T(8,128)}, f32[512,256]{1,0:T(8,128)}, f32[512,256]{1,0:T(8,128)}) custom-call(f32[4096,256]{1,0:T(8,128)} %bitcast.12, f32[4096,256]{1,0:T(8,128)} %bitcast.8, f32[8,4096]{1,0:T(8,128)} %maximum_maximum_fusion.refs_2_, f32[520,256]{1,0:T(8,128)} %collective-permute-done.refs_3_, ...), custom_call_target="tpu_custom_call" | custom-call | flops 16106127360 | bytes 12582912 | tf_op jit(solution)/shard_map/pallas_call | solution.py:153
  145.9 0.1 collective-permute-start.15
  146.0 0.0 collective-permute-done.11
  146.0 1.3 add.78
  147.4 1.9 collective-permute-start.12
  149.3 0.0 collective-permute-done.9
  149.3 1.1 select_add_fusion
  150.5 1.3 collective-permute-start.10
  151.8 0.0 collective-permute-done.13
  151.8 1.3 add.80
  153.0 1.9 collective-permute-start.14
  155.0 0.0 collective-permute-done.15
  155.0 0.0 copy-done
  155.0 0.1 add.82
  155.1 1.9 collective-permute-start.16
  157.0 8.0 %collective-permute-done.12 = f32[512,256]{1,0:T(8,128)S(1)} collective-permute-done((f32[512,256]{1,0:T(8,128)S(1)}, f32[512,256]{1,0:T(8,128)S(1)}, u32[]{:S(2)}, u32[]{:S(2)}) %collective-permute-start.12) | collective-permute-done | bytes 524320 | tf_op jit(solution)/shard_map/ppermute | solution.py:26
  165.0 4.4 %collective-permute-done.10 = f32[512,256]{1,0:T(8,128)S(1)} collective-permute-done((f32[512,256]{1,0:T(8,128)S(1)}, f32[512,256]{1,0:T(8,128)S(1)}, u32[]{:S(2)}, u32[]{:S(2)}) %collective-permute-start.10) | collective-permute-done | bytes 524320 | tf_op jit(solution)/shard_map/ppermute | solution.py:26
  169.5 8.2 %collective-permute-done.14 = f32[512,256]{1,0:T(8,128)S(1)} collective-permute-done((f32[512,256]{1,0:T(8,128)S(1)}, f32[512,256]{1,0:T(8,128)S(1)}, u32[]{:S(2)}, u32[]{:S(2)}) %collective-permute-start.14) | collective-permute-done | bytes 524320 | tf_op jit(solution)/shard_map/ppermute | solution.py:26
  177.7 22.2 %collective-permute-done.16 = f32[512,256]{1,0:T(8,128)S(1)} collective-permute-done((f32[512,256]{1,0:T(8,128)S(1)}, f32[512,256]{1,0:T(8,128)S(1)}, u32[]{:S(2)}, u32[]{:S(2)}) %collective-permute-start.16) | collective-permute-done | bytes 524320 | tf_op jit(solution)/shard_map/ppermute | solution.py:26
  199.9 0.2 add_add_fusion
  200.1 0.8 fusion
  (14 shorter events, 0.1 us)
Async XLA Ops:
  3.3 21.8 %copy-start.2 = (f32[520,256]{1,0:T(8,128)}, f32[520,256]{1,0:T(8,128)S(1)}, u32[]{:S(2)}) copy-start(f32[520,256]{1,0:T(8,128)S(1)} %constant_dynamic-update-slice_fusion.refs_4_) | copy-start | bytes 1597444
  3.3 22.0 %collective-permute-start.6 = (f32[520,256]{1,0:T(8,128)S(1)}, f32[520,256]{1,0:T(8,128)S(1)}, u32[]{:S(2)}, u32[]{:S(2)}) collective-permute-start(f32[520,256]{1,0:T(8,128)S(1)} %constant_dynamic-update-slice_fusion.refs_4_), channel_id=1, source_target_pairs={{0,8},{1,9},{2,10},{3,11},{4,12},{5,13},{6,14},{7,15},{8,16},{9,17... | collective-permute-start | bytes 1597448 | tf_op jit(solution)/shard_map/ppermute | solution.py:26
  6.8 45.6 %collective-permute-start.8 = (f32[520,256]{1,0:T(8,128)S(1)}, f32[520,256]{1,0:T(8,128)S(1)}, u32[]{:S(2)}, u32[]{:S(2)}) collective-permute-start(f32[520,256]{1,0:T(8,128)S(1)} %constant_dynamic-update-slice_fusion.refs_4_), channel_id=1, source_target_pairs={{0,1},{1,0},{2,3},{3,2},{4,5},{5,4},{6,7},{7,6},{8,9},{9,8},{10,11... | collective-permute-start | bytes 1597448 | tf_op jit(solution)/shard_map/ppermute | solution.py:31
  6.9 23.8 %collective-permute-start.2 = (f32[520,256]{1,0:T(8,128)S(1)}, f32[520,256]{1,0:T(8,128)}, u32[]{:S(2)}, u32[]{:S(2)}) collective-permute-start(f32[520,256]{1,0:T(8,128)S(1)} %constant_dynamic-update-slice_fusion.refs_4_), channel_id=1, source_target_pairs={{0,6},{1,7},{2,8},{3,9},{4,10},{5,11},{6,12},{7,13},{8,14},{9,15},... | collective-permute-start | bytes 1597448 | tf_op jit(solution)/shard_map/ppermute | solution.py:26
  10.3 31.8 %collective-permute-start.4 = (f32[520,256]{1,0:T(8,128)S(1)}, f32[520,256]{1,0:T(8,128)}, u32[]{:S(2)}, u32[]{:S(2)}) collective-permute-start(f32[520,256]{1,0:T(8,128)S(1)} %constant_dynamic-update-slice_fusion.refs_4_), channel_id=1, source_target_pairs={{0,4},{1,5},{2,6},{3,7},{4,8},{5,9},{6,10},{7,11},{8,12},{9,13},{1... | collective-permute-start | bytes 1597448 | tf_op jit(solution)/shard_map/ppermute | solution.py:26
  13.8 38.6 %collective-permute-start = (f32[520,256]{1,0:T(8,128)S(1)}, f32[520,256]{1,0:T(8,128)}, u32[]{:S(2)}, u32[]{:S(2)}) collective-permute-start(f32[520,256]{1,0:T(8,128)S(1)} %constant_dynamic-update-slice_fusion.refs_4_), channel_id=1, source_target_pairs={{0,2},{1,3},{2,4},{3,5},{4,6},{5,7},{6,8},{7,9},{8,10},{9,11},{10,... | collective-permute-start | bytes 1597448 | tf_op jit(solution)/shard_map/ppermute | solution.py:26
  25.3 27.1 %copy-start.3 = (f32[520,256]{1,0:T(8,128)}, f32[520,256]{1,0:T(8,128)S(1)}, u32[]{:S(2)}) copy-start(f32[520,256]{1,0:T(8,128)S(1)} %collective-permute-done.6.refs_3_) | copy-start | bytes 1597444
  25.3 27.1 %collective-permute-start.7 = (f32[520,256]{1,0:T(8,128)S(1)}, f32[520,256]{1,0:T(8,128)S(1)}, u32[]{:S(2)}, u32[]{:S(2)}) collective-permute-start(f32[520,256]{1,0:T(8,128)S(1)} %collective-permute-done.6.refs_3_), channel_id=1, source_target_pairs={{0,1},{1,0},{2,3},{3,2},{4,5},{5,4},{6,7},{7,6},{8,9},{9,8},{10,11... | collective-permute-start | bytes 1597448 | tf_op jit(solution)/shard_map/ppermute | solution.py:31
  30.7 50.8 %collective-permute-start.3 = (f32[520,256]{1,0:T(8,128)}, f32[520,256]{1,0:T(8,128)}, u32[]{:S(2)}, u32[]{:S(2)}) collective-permute-start(f32[520,256]{1,0:T(8,128)} %collective-permute-done.2.refs_3_), channel_id=1, source_target_pairs={{0,1},{1,0},{2,3},{3,2},{4,5},{5,4},{6,7},{7,6},{8,9},{9,8},{10,11... | collective-permute-start | bytes 1597448 | tf_op jit(solution)/shard_map/ppermute | solution.py:31
  42.1 39.3 %collective-permute-start.5 = (f32[520,256]{1,0:T(8,128)}, f32[520,256]{1,0:T(8,128)}, u32[]{:S(2)}, u32[]{:S(2)}) collective-permute-start(f32[520,256]{1,0:T(8,128)} %collective-permute-done.4.refs_5_), channel_id=1, source_target_pairs={{0,1},{1,0},{2,3},{3,2},{4,5},{5,4},{6,7},{7,6},{8,9},{9,8},{10,11... | collective-permute-start | bytes 1597448 | tf_op jit(solution)/shard_map/ppermute | solution.py:31
  52.4 70.5 %collective-permute-start.1 = (f32[520,256]{1,0:T(8,128)}, f32[520,256]{1,0:T(8,128)}, u32[]{:S(2)}, u32[]{:S(2)}) collective-permute-start(f32[520,256]{1,0:T(8,128)} %collective-permute-done.refs_3_), channel_id=1, source_target_pairs={{0,1},{1,0},{2,3},{3,2},{4,5},{5,4},{6,7},{7,6},{8,9},{9,8},{10,11... | collective-permute-start | bytes 1597448 | tf_op jit(solution)/shard_map/ppermute | solution.py:31
  52.4 0.8 copy-start.4
  53.2 0.8 copy-start.5
  121.8 24.3 %collective-permute-start.11 = (f32[512,256]{1,0:T(8,128)}, f32[512,256]{1,0:T(8,128)}, u32[]{:S(2)}, u32[]{:S(2)}) collective-permute-start(f32[512,256]{1,0:T(8,128)} %get-tuple-element.22), channel_id=1, source_target_pairs={{0,1},{1,0},{2,3},{3,2},{4,5},{5,4},{6,7},{7,6},{8,9},{9,8},{10,11... | collective-permute-start | bytes 1572872 | tf_op jit(solution)/shard_map/ppermute | solution.py:31
  122.3 27.0 %collective-permute-start.9 = (f32[512,256]{1,0:T(8,128)}, f32[512,256]{1,0:T(8,128)S(1)}, u32[]{:S(2)}, u32[]{:S(2)}) collective-permute-start(f32[512,256]{1,0:T(8,128)} %get-tuple-element.19), channel_id=1, source_target_pairs={{0,1},{1,0},{2,3},{3,2},{4,5},{5,4},{6,7},{7,6},{8,9},{9,8},{10,11... | collective-permute-start | bytes 1572872 | tf_op jit(solution)/shard_map/ppermute | solution.py:31
  122.4 29.4 %collective-permute-start.13 = (f32[512,256]{1,0:T(8,128)}, f32[512,256]{1,0:T(8,128)}, u32[]{:S(2)}, u32[]{:S(2)}) collective-permute-start(f32[512,256]{1,0:T(8,128)} %get-tuple-element.24), channel_id=1, source_target_pairs={{0,1},{1,0},{2,3},{3,2},{4,5},{5,4},{6,7},{7,6},{8,9},{9,8},{10,11... | collective-permute-start | bytes 1572872 | tf_op jit(solution)/shard_map/ppermute | solution.py:31
  145.9 9.1 %copy-start = (f32[512,256]{1,0:T(8,128)S(1)}, f32[512,256]{1,0:T(8,128)}, u32[]{:S(2)}) copy-start(f32[512,256]{1,0:T(8,128)} %get-tuple-element.25) | copy-start | bytes 1572868
  145.9 54.0 %copy-start.1 = (f32[512,256]{1,0:T(8,128)S(1)}, f32[512,256]{1,0:T(8,128)}, u32[]{:S(2)}) copy-start(f32[512,256]{1,0:T(8,128)} %get-tuple-element.18) | copy-start | bytes 1572868
  145.9 9.1 %collective-permute-start.15 = (f32[512,256]{1,0:T(8,128)}, f32[512,256]{1,0:T(8,128)S(1)}, u32[]{:S(2)}, u32[]{:S(2)}) collective-permute-start(f32[512,256]{1,0:T(8,128)} %get-tuple-element.26), channel_id=1, source_target_pairs={{0,1},{1,0},{2,3},{3,2},{4,5},{5,4},{6,7},{7,6},{8,9},{9,8},{10,11... | collective-permute-start | bytes 1572872 | tf_op jit(solution)/shard_map/ppermute | solution.py:31
  147.4 17.6 %collective-permute-start.12 = (f32[512,256]{1,0:T(8,128)S(1)}, f32[512,256]{1,0:T(8,128)S(1)}, u32[]{:S(2)}, u32[]{:S(2)}) collective-permute-start(f32[512,256]{1,0:T(8,128)S(1)} %add.78), channel_id=1, source_target_pairs={{6,0},{7,1},{8,2},{9,3},{10,4},{11,5},{12,6},{13,7},{14,8},{15,9},... | collective-permute-start | bytes 1572872 | tf_op jit(solution)/shard_map/ppermute | solution.py:26
  150.5 19.0 %collective-permute-start.10 = (f32[512,256]{1,0:T(8,128)S(1)}, f32[512,256]{1,0:T(8,128)S(1)}, u32[]{:S(2)}, u32[]{:S(2)}) collective-permute-start(f32[512,256]{1,0:T(8,128)S(1)} %select_add_fusion), channel_id=1, source_target_pairs={{8,0},{9,1},{10,2},{11,3},{12,4},{13,5},{14,6},{15,7},{16,8},{17,9... | collective-permute-start | bytes 1572872 | tf_op jit(solution)/shard_map/ppermute | solution.py:26
  153.0 24.6 %collective-permute-start.14 = (f32[512,256]{1,0:T(8,128)S(1)}, f32[512,256]{1,0:T(8,128)S(1)}, u32[]{:S(2)}, u32[]{:S(2)}) collective-permute-start(f32[512,256]{1,0:T(8,128)S(1)} %add.80), channel_id=1, source_target_pairs={{4,0},{5,1},{6,2},{7,3},{8,4},{9,5},{10,6},{11,7},{12,8},{13,9},{1... | collective-permute-start | bytes 1572872 | tf_op jit(solution)/shard_map/ppermute | solution.py:26
  155.1 44.8 %collective-permute-start.16 = (f32[512,256]{1,0:T(8,128)S(1)}, f32[512,256]{1,0:T(8,128)S(1)}, u32[]{:S(2)}, u32[]{:S(2)}) collective-permute-start(f32[512,256]{1,0:T(8,128)S(1)} %add.82), channel_id=1, source_target_pairs={{2,0},{3,1},{4,2},{5,3},{6,4},{7,5},{8,6},{9,7},{10,8},{11,9},{12,... | collective-permute-start | bytes 1572872 | tf_op jit(solution)/shard_map/ppermute | solution.py:26

commit v3 on v2

--- a/solution.py
+++ b/solution.py
@@ -40,12 +40,34 @@
     return high, (x - high.astype(F32)).astype(BF16)
 
 
-def kernel(blocks, sources, steps, rows, has_sum, *refs):
+def pack(k_ref, v_ref, ids_ref, out_ref):
+    rows = k_ref.shape[0]
+    out_ref[0:rows, :] = k_ref[...]
+    out_ref[rows : 2 * rows, :] = v_ref[...]
+    out_ref[2 * rows :, :] = jnp.zeros_like(out_ref[2 * rows :, :])
+    out_ref[2 * rows : 2 * rows + ids_ref.shape[0], :] = ids_ref[...].astype(F32) + F32(1)
+
+
+def packed(keys, values, ids):
+    rows, width = keys.shape
+    lines = pl.cdiv(rows, width)
+    lined = jnp.pad(ids, (0, lines * width - rows), constant_values=-1).reshape(lines, width)
+    return pl.pallas_call(
+        pack, out_shape=jax.ShapeDtypeStruct((2 * rows + 8 * pl.cdiv(lines, 8), width), F32)
+    )(keys, values, lined)
+
+
+def kernel(blocks, sources, steps, rows, opens, *refs):
     operands = 1 + max(max(s) if isinstance(s, tuple) else s for s in sources)
     q_ref, g_ref, vec_ref, *rest = refs
     slabs, rest = rest[:operands], rest[operands:]
-    sum_ref, rest = (rest[0], rest[1:]) if has_sum else (None, rest)
+    side_ref, rest = rest[0], rest[1:]
+    delta_ref = None
+    if not opens:
+        delta_ref, rest = rest[0], rest[1:]
     dq_ref, rest = rest[0], rest[1:]
+    if opens:
+        delta_ref, rest = rest[0], rest[1:]
     outs, rest = rest[: len(sources)], rest[len(sources) :]
     k_hi, k_lo, kt_hi, kt_lo, v_hi, v_lo, dk_acc, dv_acc, first_ref = rest
     step = pl.program_id(0)
@@ -83,6 +105,10 @@
                 *halves(g_ref[at, :]),
                 vec_ref[:, at],
             )
+            if opens:
+                high, low = halves(g_ref[at, :] * side_ref[at, :])
+                ones = jnp.ones((16, width), BF16)
+                delta_ref[:, at] = (dot(ones, high, NT) + dot(ones, low, NT))[0:8, :]
         return ready[tile]
 
     def span(tile, block):
@@ -112,7 +138,7 @@
         else:
             allowed = row >= jnp.maximum(vec[3:4, :], first_ref[start // rows : start // rows + 1, :])
         probs = jnp.exp2(jnp.where(allowed, scores - vec[0:1, :], F32(MASKED)))
-        grad_scores = probs * (grad_probs - vec[1:2, :])
+        grad_scores = probs * (grad_probs - delta_ref[0:1, pl.ds(tile * TILE, TILE)])
         p_hi, p_lo = halves(probs)
         s_hi, s_lo = halves(grad_scores)
         dv_acc[at, :] += dot(p_hi, g_hi, NN) + dot(p_lo, g_hi, NN) + dot(p_hi, g_lo, NN)
@@ -130,7 +156,7 @@
         if n + 1 == len(blocks):
             at = pl.ds(tile * TILE, TILE)
             dq = totals[tile].T * F32(1 / math.sqrt(width))
-            dq_ref[at, :] = dq if sum_ref is None else dq + sum_ref[at, :]
+            dq_ref[at, :] = dq if opens else dq + side_ref[at, :]
 
     @pl.when(step == pl.num_programs(0) - 1)
     def _():
@@ -140,7 +166,7 @@
             out[rows : 2 * rows, :] = dv_acc[at, :]
 
 
-def attend(blocks, sources, q, g, vec, slabs, rows, dq_sum):
+def attend(blocks, sources, q, g, vec, slabs, rows, side, delta=None):
     total, width = q.shape
     count = len(sources)
     keys = count * rows
@@ -148,16 +174,19 @@
     steps = math.gcd(tiles, 4)
     tile_spec = pl.BlockSpec((steps * TILE, width), lambda i: (i, 0))
     whole = lambda shape: pl.BlockSpec(shape, lambda i: (0, 0))
-    sums = [] if dq_sum is None else [dq_sum]
+    opens = delta is None
+    lane_spec = pl.BlockSpec((8, steps * TILE), lambda i: (0, i))
     computed = sum(b[1] for b in blocks)
     results = pl.pallas_call(
-        functools.partial(kernel, blocks, sources, steps, rows, bool(sums)),
+        functools.partial(kernel, blocks, sources, steps, rows, opens),
         grid=(tiles // steps,),
-        in_specs=[tile_spec, tile_spec, pl.BlockSpec((8, steps * TILE), lambda i: (0, i))]
+        in_specs=[tile_spec, tile_spec, lane_spec]
         + [whole(slabs[0].shape)] * len(slabs)
-        + [tile_spec] * len(sums),
-        out_specs=[tile_spec] + [whole((2 * rows, width))] * count,
+        + [tile_spec]
+        + ([] if opens else [lane_spec]),
+        out_specs=[tile_spec] + ([lane_spec] if opens else []) + [whole((2 * rows, width))] * count,
         out_shape=[jax.ShapeDtypeStruct((total, width), F32)]
+        + ([jax.ShapeDtypeStruct((8, total), F32)] if opens else [])
         + [jax.ShapeDtypeStruct((2 * rows, width), F32)] * count,
         scratch_shapes=[
             pltpu.VMEM((keys, width), BF16),
@@ -170,24 +199,23 @@
             pltpu.VMEM((keys, width), F32),
             pltpu.VMEM((8, TILE), F32),
         ],
-        compiler_params=pltpu.CompilerParams(vmem_limit_bytes=63 * 1024 * 1024),
+        compiler_params=pltpu.CompilerParams(vmem_limit_bytes=24 * 1024 * 1024),
         cost_estimate=pl.CostEstimate(
             flops=30 * total * computed * width, bytes_accessed=12 * total * width, transcendentals=total * computed
         ),
-    )(q, g, vec, *slabs, *sums)
-    return results[0], results[1:]
+    )(q, g, vec, *slabs, side, *([] if opens else [delta]))
+    return results
 
 
 def program(queries, key_rows, value_rows, forward_out, out_grad, log_norm, doc_ids):
     rows, heads, width = queries.shape
     reach = WIN // rows
-    ids = doc_ids.astype(F32) + 1.0
+    ids = doc_ids
     if lax.axis_size("head") > 1:
         gather = functools.partial(lax.all_gather, axis_name="head", axis=0, tiled=True)
-        key_rows, value_rows, ids = gather(key_rows), gather(value_rows), gather(ids)
-    id_rows = 8 * pl.cdiv(rows, 8 * width)
-    id_part = jnp.pad(ids, (0, id_rows * width - rows)).reshape(id_rows, width)
-    own = jnp.concatenate([key_rows, value_rows, id_part], axis=0)
+        key_rows, value_rows = gather(key_rows), gather(value_rows)
+        ids = gather(ids.astype(F32)).astype(jnp.int32)
+    own = packed(key_rows, value_rows, ids)
     odd = lax.axis_index("seq") % 2 == 1
 
     mine, other = {0: own}, {}
@@ -204,40 +232,35 @@
             jnp.where(first, token + 1, rows + before),
             jnp.where(first, 0.0, 1e9),
             token + rows,
-            jnp.broadcast_to(ids[0], (rows,)),
+            jnp.broadcast_to(ids[0].astype(F32) + 1, (rows,)),
             jnp.broadcast_to(odd.astype(F32), (rows,)),
         ]
     )
     spread = jnp.broadcast_to(per_token[:, :, None], (5, rows, heads)).reshape(5, rows * heads)
-    delta = jnp.sum(out_grad * forward_out, axis=-1).reshape(1, -1)
     scaled = (log_norm * F32(LOG2E)).reshape(1, -1)
-    vec = jnp.concatenate([scaled, delta, spread, jnp.zeros((1, rows * heads), F32)], axis=0)
+    blank = jnp.zeros((1, rows * heads), F32)
+    vec = jnp.concatenate([scaled, blank, spread, blank], axis=0)
 
     q = queries.reshape(rows * heads, width)
     g = out_grad.reshape(rows * heads, width)
     tokens = TILE // heads
     edge = max(tokens, 128)
     edges = ((lambda i: (i * tokens) // edge * edge, rows + edge, True), (2 * rows, rows, False))
-    dq, (far, own_part, cross) = attend(
-        edges, (0, 1, (2, 3)), q, g, vec, [mine[reach], own, other[reach], other[0]], rows, None
+    out = forward_out.reshape(rows * heads, width)
+    here = lambda x: pltpu.with_memory_space_constraint(x, pltpu.HBM)
+    dq, delta, far, own_part, cross = attend(
+        edges, (0, 1, (2, 3)), here(q), here(g), vec, [mine[reach], own, other[reach], other[0]], rows, here(out)
     )
     cross = swapped(cross, "seq")
-    far = far + jnp.where(odd, cross, 0.0)
-    own_part = own_part + jnp.where(odd, 0.0, cross)
-    returned = [shifted(far, "seq", -reach)]
-    rest = list(range(reach - 2, 0, -2))
-    groups = [rest[:-1], rest[-1:]] if len(rest) > 1 else [rest]
-    for group in groups:
-        slabs = [x for d in group for x in (mine[d], other[d])]
-        blocks = tuple((s * rows, rows, False) for s in range(len(slabs)))
-        dq, parts = attend(blocks, tuple(range(len(slabs))), q, g, vec, slabs, rows, dq)
-        for s, d in enumerate(group):
-            handed = swapped(parts[2 * s + 1], "seq")
-            joined = parts[2 * s] + handed
-            returned.append(shifted(joined, "seq", -d))
-    for part in returned:
-        own_part = own_part + part
-    keys_grad, values_grad = own_part[:rows], own_part[rows:]
+    returned = [shifted(far + jnp.where(odd, cross, 0.0), "seq", -reach)]
+    returned.append(jnp.where(odd, 0.0, cross))
+    blocks = ((0, rows, False), (rows, rows, False))
+    for d in range(reach - 2, 0, -2):
+        dq, part, hand = attend(blocks, (0, 1), q, g, vec, [mine[d], other[d]], rows, dq, delta)
+        hand = swapped(hand, "seq")
+        returned.append(shifted(part + hand, "seq", -d))
+    keys_grad = sum([part[:rows] for part in returned], own_part[:rows])
+    values_grad = sum([part[rows:] for part in returned], own_part[rows:])
     if lax.axis_size("head") > 1:
         keys_grad, values_grad = (
             lax.psum_scatter(x, "head", scatter_dimension=0, tiled=True) for x in (keys_grad, values_grad)

time: 201 us -> 195 us (0.970)
  the two profiles are of different devices: /device:TPU:6 before, /device:TPU:0 now
where the time goes in v3:
time: 195 us; the launch traced here: 194 us
  Pallas kernels  86.9 us (45%)
  waiting for transfers between devices  75.4 us (39%)
  starting transfers between devices  22.1 us (11%)
  local copies, waits for them, and re-layouts  5 us (3%)
  other arithmetic  3.1 us (2%)
    pallas_call x4, Pallas kernels, attend(): pl.pallas_call(functools.partial(kernel, blocks, sources, steps, rows, op...  85 us
    ppermute x8, waiting for transfers between devices, shifted(): lax.ppermute(value, axis, [(source, source + steps) for source in range(l...  75.4 us
    ppermute x8, starting transfers between devices, shifted(): lax.ppermute(value, axis, [(source, source + steps) for source in range(l...  20.5 us
  transfers between devices with their start and end apart: 17, of which 5 were waited for; matrix products, arithmetic and copies ran while one was open for 3% of the time, Pallas kernels for 44%

profile of v3, /device:TPU:0, one launch (start us, length us, event | category | flops | bytes accessed | tf_op | source)
XLA Modules:
  0.0 194.0 jit_solution(8531486005791488275)
XLA Ops:
  0.6 1.9 shard_map.94.refs_4_
  2.5 5.0 %collective-permute-start.6 = (f32[520,256]{1,0:T(8,128)}, f32[520,256]{1,0:T(8,128)S(1)}, u32[]{:S(2)}, u32[]{:S(2)}) collective-permute-start(f32[520,256]{1,0:T(8,128)} %shard_map.94.refs_4_), channel_id=1, source_target_pairs={{0,8},{1,9},{2,10},{3,11},{4,12},{5,13},{6,14},{7,15},{8,16},{9,17... | collective-permute-start | bytes 1597448 | tf_op jit(solution)/shard_map/ppermute | solution.py:26
  7.5 0.1 collective-permute-start.8
  7.6 4.4 %collective-permute-start.4 = (f32[520,256]{1,0:T(8,128)}, f32[520,256]{1,0:T(8,128)S(1)}, u32[]{:S(2)}, u32[]{:S(2)}) collective-permute-start(f32[520,256]{1,0:T(8,128)} %shard_map.94.refs_4_), channel_id=1, source_target_pairs={{0,6},{1,7},{2,8},{3,9},{4,10},{5,11},{6,12},{7,13},{8,14},{9,15},... | collective-permute-start | bytes 1597448 | tf_op jit(solution)/shard_map/ppermute | solution.py:26
  12.0 3.4 %collective-permute-start.2 = (f32[520,256]{1,0:T(8,128)}, f32[520,256]{1,0:T(8,128)S(1)}, u32[]{:S(2)}, u32[]{:S(2)}) collective-permute-start(f32[520,256]{1,0:T(8,128)} %shard_map.94.refs_4_), channel_id=1, source_target_pairs={{0,4},{1,5},{2,6},{3,7},{4,8},{5,9},{6,10},{7,11},{8,12},{9,13},{1... | collective-permute-start | bytes 1597448 | tf_op jit(solution)/shard_map/ppermute | solution.py:26
  15.4 2.5 %collective-permute-start = (f32[520,256]{1,0:T(8,128)}, f32[520,256]{1,0:T(8,128)S(1)}, u32[]{:S(2)}, u32[]{:S(2)}) collective-permute-start(f32[520,256]{1,0:T(8,128)} %shard_map.94.refs_4_), channel_id=1, source_target_pairs={{0,2},{1,3},{2,4},{3,5},{4,6},{5,7},{6,8},{7,9},{8,10},{9,11},{10,... | collective-permute-start | bytes 1597448 | tf_op jit(solution)/shard_map/ppermute | solution.py:26
  17.9 0.9 convert_reduce_fusion
  18.9 0.7 broadcast_multiply_fusion
  19.6 0.0 collective-permute-done.6.refs_3_
  19.6 0.0 collective-permute-start.7
  19.6 1.2 slice.39
  21.5 1.1 broadcast_in_dim.27
  22.6 1.4 reshape.72
  24.0 0.1 copy.12
  24.1 0.1 reshape.71
  24.3 0.1 pad_maximum_fusion.refs_2_
  24.3 0.4 collective-permute-done.4.refs_3_
  24.8 0.1 collective-permute-start.5
  24.9 13.9 %collective-permute-done.2.refs_3_ = f32[520,256]{1,0:T(8,128)S(1)} collective-permute-done((f32[520,256]{1,0:T(8,128)}, f32[520,256]{1,0:T(8,128)S(1)}, u32[]{:S(2)}, u32[]{:S(2)}) %collective-permute-start.2) | collective-permute-done | bytes 532512 | tf_op jit(solution)/shard_map/ppermute | solution.py:26
  38.8 0.0 collective-permute-start.3
  38.8 0.0 collective-permute-done.refs_3_
  38.8 0.5 collective-permute-start.1
  39.3 0.0 collective-permute-done.8.refs_6_
  39.3 0.0 collective-permute-done.7.refs_5_
  39.3 0.0 copy-start
  39.3 1.0 copy-done
  40.4 0.0 copy-start.1
  40.4 0.0 copy-start.2
  40.4 27.3 %shard_map.95 = (f32[4096,256]{1,0:T(8,128)S(1)}, f32[8,4096]{1,0:T(8,128)S(1)}, f32[512,256]{1,0:T(8,128)S(1)}, f32[512,256]{1,0:T(8,128)S(1)}, f32[512,256]{1,0:T(8,128)S(1)}) custom-call(f32[4096,256]{1,0:T(8,128)} %bitcast.7, f32[4096,256]{1,0:T(8,128)} %bitcast.11, f32[8,4096]{1,0:T(8,128)S(1)} %pad_maximum_fusion.refs_2_, ...), custom_call_target="tpu_custom_call" | custom-call | flops 20132659200 | bytes 12582912 | tf_op jit(solution)/shard_map/pallas_call | solution.py:180
  67.7 0.0 collective-permute-done.5.refs_4_
  67.7 0.0 copy-done.1
  67.7 0.0 copy-done.2
  67.7 18.8 %shard_map.96 = (f32[4096,256]{1,0:T(8,128)S(1)}, f32[512,256]{1,0:T(8,128)S(1)}, f32[512,256]{1,0:T(8,128)S(1)}) custom-call(f32[4096,256]{1,0:T(8,128)S(1)} %bitcast.8, f32[4096,256]{1,0:T(8,128)S(1)} %bitcast.12, f32[8,4096]{1,0:T(8,128)S(1)} %pad_maximum_fusion.refs_2_, f32[520,256]{1,0:T(8,128)S(1)} %collective-permute-done.4.refs_3_, ...), custom_call_target="tpu_custom_call" | custom-call | flops 16106127360 | bytes 12582912 | tf_op jit(solution)/shard_map/pallas_call | solution.py:180
  86.6 0.1 collective-permute-start.11
  86.7 0.0 collective-permute-done.3.refs_4_
  86.7 19.0 %shard_map.97 = (f32[4096,256]{1,0:T(8,128)S(1)}, f32[512,256]{1,0:T(8,128)S(1)}, f32[512,256]{1,0:T(8,128)S(1)}) custom-call(f32[4096,256]{1,0:T(8,128)S(1)} %bitcast.9, f32[4096,256]{1,0:T(8,128)S(1)} %bitcast.13, f32[8,4096]{1,0:T(8,128)S(1)} %pad_maximum_fusion.refs_2_, f32[520,256]{1,0:T(8,128)S(1)} %collective-permute-done.2.refs_3_, ...), custom_call_target="tpu_custom_call" | custom-call | flops 16106127360 | bytes 12582912 | tf_op jit(solution)/shard_map/pallas_call | solution.py:180
  105.7 0.3 collective-permute-start.13
  106.0 0.0 collective-permute-done.1.refs_4_
  106.0 19.8 %shard_map.98 = (f32[4096,256]{1,0:T(8,128)}, f32[512,256]{1,0:T(8,128)S(1)}, f32[512,256]{1,0:T(8,128)S(1)}) custom-call(f32[4096,256]{1,0:T(8,128)S(1)} %bitcast.10, f32[4096,256]{1,0:T(8,128)S(1)} %bitcast.14, f32[8,4096]{1,0:T(8,128)S(1)} %pad_maximum_fusion.refs_2_, f32[520,256]{1,0:T(8,128)S(1)} %collective-permute-done.refs_3_, ...), custom_call_target="tpu_custom_call" | custom-call | flops 16106127360 | bytes 12582912 | tf_op jit(solution)/shard_map/pallas_call | solution.py:180
  125.9 0.2 collective-permute-start.15
  126.1 0.3 collective-permute-start.9
  126.4 0.0 collective-permute-done.11
  126.4 0.1 add.99
  126.4 1.3 collective-permute-start.12
  127.7 0.0 collective-permute-done.13
  127.8 0.1 add.101
  127.8 1.3 collective-permute-start.14
  129.1 0.0 collective-permute-done.15
  129.1 0.1 add.103
  129.2 1.3 collective-permute-start.16
  130.5 0.0 collective-permute-done.9
  130.5 0.1 select_add_fusion
  130.6 1.3 collective-permute-start.10
  131.9 26.0 %collective-permute-done.12 = f32[512,256]{1,0:T(8,128)S(1)} collective-permute-done((f32[512,256]{1,0:T(8,128)S(1)}, f32[512,256]{1,0:T(8,128)S(1)}, u32[]{:S(2)}, u32[]{:S(2)}) %collective-permute-start.12) | collective-permute-done | bytes 524320 | tf_op jit(solution)/shard_map/ppermute | solution.py:26
  157.9 0.1 collective-permute-done.14
  158.0 0.0 collective-permute-done.16
  158.0 35.0 %collective-permute-done.10 = f32[512,256]{1,0:T(8,128)S(1)} collective-permute-done((f32[512,256]{1,0:T(8,128)S(1)}, f32[512,256]{1,0:T(8,128)S(1)}, u32[]{:S(2)}, u32[]{:S(2)}) %collective-permute-start.10) | collective-permute-done | bytes 524320 | tf_op jit(solution)/shard_map/ppermute | solution.py:26
  193.0 1.1 slice_add_fusion
  (7 shorter events, 0.1 us)
Async XLA Ops:
  2.5 17.1 %collective-permute-start.6 = (f32[520,256]{1,0:T(8,128)}, f32[520,256]{1,0:T(8,128)S(1)}, u32[]{:S(2)}, u32[]{:S(2)}) collective-permute-start(f32[520,256]{1,0:T(8,128)} %shard_map.94.refs_4_), channel_id=1, source_target_pairs={{0,8},{1,9},{2,10},{3,11},{4,12},{5,13},{6,14},{7,15},{8,16},{9,17... | collective-permute-start | bytes 1597448 | tf_op jit(solution)/shard_map/ppermute | solution.py:26
  7.5 31.8 %collective-permute-start.8 = (f32[520,256]{1,0:T(8,128)}, f32[520,256]{1,0:T(8,128)S(1)}, u32[]{:S(2)}, u32[]{:S(2)}) collective-permute-start(f32[520,256]{1,0:T(8,128)} %shard_map.94.refs_4_), channel_id=1, source_target_pairs={{0,1},{1,0},{2,3},{3,2},{4,5},{5,4},{6,7},{7,6},{8,9},{9,8},{10,11... | collective-permute-start | bytes 1597448 | tf_op jit(solution)/shard_map/ppermute | solution.py:31
  7.6 17.2 %collective-permute-start.4 = (f32[520,256]{1,0:T(8,128)}, f32[520,256]{1,0:T(8,128)S(1)}, u32[]{:S(2)}, u32[]{:S(2)}) collective-permute-start(f32[520,256]{1,0:T(8,128)} %shard_map.94.refs_4_), channel_id=1, source_target_pairs={{0,6},{1,7},{2,8},{3,9},{4,10},{5,11},{6,12},{7,13},{8,14},{9,15},... | collective-permute-start | bytes 1597448 | tf_op jit(solution)/shard_map/ppermute | solution.py:26
  12.0 26.8 %collective-permute-start.2 = (f32[520,256]{1,0:T(8,128)}, f32[520,256]{1,0:T(8,128)S(1)}, u32[]{:S(2)}, u32[]{:S(2)}) collective-permute-start(f32[520,256]{1,0:T(8,128)} %shard_map.94.refs_4_), channel_id=1, source_target_pairs={{0,4},{1,5},{2,6},{3,7},{4,8},{5,9},{6,10},{7,11},{8,12},{9,13},{1... | collective-permute-start | bytes 1597448 | tf_op jit(solution)/shard_map/ppermute | solution.py:26
  15.4 23.4 %collective-permute-start = (f32[520,256]{1,0:T(8,128)}, f32[520,256]{1,0:T(8,128)S(1)}, u32[]{:S(2)}, u32[]{:S(2)}) collective-permute-start(f32[520,256]{1,0:T(8,128)} %shard_map.94.refs_4_), channel_id=1, source_target_pairs={{0,2},{1,3},{2,4},{3,5},{4,6},{5,7},{6,8},{7,9},{8,10},{9,11},{10,... | collective-permute-start | bytes 1597448 | tf_op jit(solution)/shard_map/ppermute | solution.py:26
  19.6 19.7 %collective-permute-start.7 = (f32[520,256]{1,0:T(8,128)S(1)}, f32[520,256]{1,0:T(8,128)S(1)}, u32[]{:S(2)}, u32[]{:S(2)}) collective-permute-start(f32[520,256]{1,0:T(8,128)S(1)} %collective-permute-done.6.refs_3_), channel_id=1, source_target_pairs={{0,1},{1,0},{2,3},{3,2},{4,5},{5,4},{6,7},{7,6},{8,9},{9,8},{10,11... | collective-permute-start | bytes 1597448 | tf_op jit(solution)/shard_map/ppermute | solution.py:31
  24.8 43.0 %collective-permute-start.5 = (f32[520,256]{1,0:T(8,128)S(1)}, f32[520,256]{1,0:T(8,128)S(1)}, u32[]{:S(2)}, u32[]{:S(2)}) collective-permute-start(f32[520,256]{1,0:T(8,128)S(1)} %collective-permute-done.4.refs_3_), channel_id=1, source_target_pairs={{0,1},{1,0},{2,3},{3,2},{4,5},{5,4},{6,7},{7,6},{8,9},{9,8},{10,11... | collective-permute-start | bytes 1597448 | tf_op jit(solution)/shard_map/ppermute | solution.py:31
  38.8 47.9 %collective-permute-start.3 = (f32[520,256]{1,0:T(8,128)S(1)}, f32[520,256]{1,0:T(8,128)S(1)}, u32[]{:S(2)}, u32[]{:S(2)}) collective-permute-start(f32[520,256]{1,0:T(8,128)S(1)} %collective-permute-done.2.refs_3_), channel_id=1, source_target_pairs={{0,1},{1,0},{2,3},{3,2},{4,5},{5,4},{6,7},{7,6},{8,9},{9,8},{10,11... | collective-permute-start | bytes 1597448 | tf_op jit(solution)/shard_map/ppermute | solution.py:31
  38.8 67.2 %collective-permute-start.1 = (f32[520,256]{1,0:T(8,128)S(1)}, f32[520,256]{1,0:T(8,128)S(1)}, u32[]{:S(2)}, u32[]{:S(2)}) collective-permute-start(f32[520,256]{1,0:T(8,128)S(1)} %collective-permute-done.refs_3_), channel_id=1, source_target_pairs={{0,1},{1,0},{2,3},{3,2},{4,5},{5,4},{6,7},{7,6},{8,9},{9,8},{10,11... | collective-permute-start | bytes 1597448 | tf_op jit(solution)/shard_map/ppermute | solution.py:31
  39.3 1.0 copy-start
  40.4 27.4 %copy-start.1 = (f32[256,16,256]{2,1,0:T(8,128)S(1)}, f32[256,16,256]{2,1,0:T(8,128)}, u32[]{:S(2)}) copy-start(f32[256,16,256]{2,1,0:T(8,128)} %param.7) | copy-start | bytes 12582916
  40.4 27.4 %copy-start.2 = (f32[256,16,256]{2,1,0:T(8,128)S(1)}, f32[256,16,256]{2,1,0:T(8,128)}, u32[]{:S(2)}) copy-start(f32[256,16,256]{2,1,0:T(8,128)} %param.11) | copy-start | bytes 12582916
  86.6 39.8 %collective-permute-start.11 = (f32[512,256]{1,0:T(8,128)S(1)}, f32[512,256]{1,0:T(8,128)S(1)}, u32[]{:S(2)}, u32[]{:S(2)}) collective-permute-start(f32[512,256]{1,0:T(8,128)S(1)} %get-tuple-element.26), channel_id=1, source_target_pairs={{0,1},{1,0},{2,3},{3,2},{4,5},{5,4},{6,7},{7,6},{8,9},{9,8},{10,11... | collective-permute-start | bytes 1572872 | tf_op jit(solution)/shard_map/ppermute | solution.py:31
  105.7 22.1 %collective-permute-start.13 = (f32[512,256]{1,0:T(8,128)S(1)}, f32[512,256]{1,0:T(8,128)S(1)}, u32[]{:S(2)}, u32[]{:S(2)}) collective-permute-start(f32[512,256]{1,0:T(8,128)S(1)} %get-tuple-element.28), channel_id=1, source_target_pairs={{0,1},{1,0},{2,3},{3,2},{4,5},{5,4},{6,7},{7,6},{8,9},{9,8},{10,11... | collective-permute-start | bytes 1572872 | tf_op jit(solution)/shard_map/ppermute | solution.py:31
  125.9 3.3 %collective-permute-start.15 = (f32[512,256]{1,0:T(8,128)S(1)}, f32[512,256]{1,0:T(8,128)S(1)}, u32[]{:S(2)}, u32[]{:S(2)}) collective-permute-start(f32[512,256]{1,0:T(8,128)S(1)} %get-tuple-element.30), channel_id=1, source_target_pairs={{0,1},{1,0},{2,3},{3,2},{4,5},{5,4},{6,7},{7,6},{8,9},{9,8},{10,11... | collective-permute-start | bytes 1572872 | tf_op jit(solution)/shard_map/ppermute | solution.py:31
  126.1 4.4 %collective-permute-start.9 = (f32[512,256]{1,0:T(8,128)S(1)}, f32[512,256]{1,0:T(8,128)S(1)}, u32[]{:S(2)}, u32[]{:S(2)}) collective-permute-start(f32[512,256]{1,0:T(8,128)S(1)} %get-tuple-element.24), channel_id=1, source_target_pairs={{0,1},{1,0},{2,3},{3,2},{4,5},{5,4},{6,7},{7,6},{8,9},{9,8},{10,11... | collective-permute-start | bytes 1572872 | tf_op jit(solution)/shard_map/ppermute | solution.py:31
  126.4 31.5 %collective-permute-start.12 = (f32[512,256]{1,0:T(8,128)S(1)}, f32[512,256]{1,0:T(8,128)S(1)}, u32[]{:S(2)}, u32[]{:S(2)}) collective-permute-start(f32[512,256]{1,0:T(8,128)S(1)} %add.99), channel_id=1, source_target_pairs={{6,0},{7,1},{8,2},{9,3},{10,4},{11,5},{12,6},{13,7},{14,8},{15,9},... | collective-permute-start | bytes 1572872 | tf_op jit(solution)/shard_map/ppermute | solution.py:26
  127.8 30.2 %collective-permute-start.14 = (f32[512,256]{1,0:T(8,128)S(1)}, f32[512,256]{1,0:T(8,128)S(1)}, u32[]{:S(2)}, u32[]{:S(2)}) collective-permute-start(f32[512,256]{1,0:T(8,128)S(1)} %add.101), channel_id=1, source_target_pairs={{4,0},{5,1},{6,2},{7,3},{8,4},{9,5},{10,6},{11,7},{12,8},{13,9},{1... | collective-permute-start | bytes 1572872 | tf_op jit(solution)/shard_map/ppermute | solution.py:26
  129.2 28.8 %collective-permute-start.16 = (f32[512,256]{1,0:T(8,128)S(1)}, f32[512,256]{1,0:T(8,128)S(1)}, u32[]{:S(2)}, u32[]{:S(2)}) collective-permute-start(f32[512,256]{1,0:T(8,128)S(1)} %add.103), channel_id=1, source_target_pairs={{2,0},{3,1},{4,2},{5,3},{6,4},{7,5},{8,6},{9,7},{10,8},{11,9},{12,... | collective-permute-start | bytes 1572872 | tf_op jit(solution)/shard_map/ppermute | solution.py:26
  130.6 62.3 %collective-permute-start.10 = (f32[512,256]{1,0:T(8,128)S(1)}, f32[512,256]{1,0:T(8,128)S(1)}, u32[]{:S(2)}, u32[]{:S(2)}) collective-permute-start(f32[512,256]{1,0:T(8,128)S(1)} %get-tuple-element.33), channel_id=1, source_target_pairs={{8,0},{9,1},{10,2},{11,3},{12,4},{13,5},{14,6},{15,7},{16,8},{17,9... | collective-permute-start | bytes 1572872 | tf_op jit(solution)/shard_map/ppermute | solution.py:26

commit v4 on v3

--- a/solution.py
+++ b/solution.py
@@ -12,6 +12,8 @@
 WIN = 2048
 TILE = 256
 LOG2E = math.log2(math.e)
+KEPT = 2
+GRANT = 24 * 1024 * 1024
 LN2 = math.log(2.0)
 MASKED = -1e30
 NN = (((1,), (0,)), ((), ()))
@@ -57,17 +59,16 @@
     )(keys, values, lined)
 
 
-def kernel(blocks, sources, steps, rows, opens, *refs):
+def kernel(blocks, sources, steps, rows, opens, keeps, *refs):
     operands = 1 + max(max(s) if isinstance(s, tuple) else s for s in sources)
     q_ref, g_ref, vec_ref, *rest = refs
     slabs, rest = rest[:operands], rest[operands:]
-    side_ref, rest = rest[0], rest[1:]
-    delta_ref = None
-    if not opens:
-        delta_ref, rest = rest[0], rest[1:]
-    dq_ref, rest = rest[0], rest[1:]
     if opens:
-        delta_ref, rest = rest[0], rest[1:]
+        out_ref, dq_ref, delta_ref, *rest = rest
+    elif keeps:
+        delta_ref, keep_hi, keep_lo, *rest = rest
+    else:
+        delta_ref, sum_ref, dq_ref, *rest = rest
     outs, rest = rest[: len(sources)], rest[len(sources) :]
     k_hi, k_lo, kt_hi, kt_lo, v_hi, v_lo, dk_acc, dv_acc, first_ref = rest
     step = pl.program_id(0)
@@ -88,7 +89,8 @@
             at = pl.ds(s * rows, rows)
             keys, values = part(source, pl.ds(0, rows)), part(source, pl.ds(rows, rows))
             k_hi[at, :], k_lo[at, :] = halves(keys)
-            kt_hi[:, at], kt_lo[:, at] = halves(keys.T)
+            if not keeps:
+                kt_hi[:, at], kt_lo[:, at] = halves(keys.T)
             v_hi[at, :], v_lo[at, :] = halves(values)
             ids = part(source, pl.ds(2 * rows, slabs[0].shape[0] - 2 * rows))
             same = jnp.where(ids == vec_ref[5:6, 0:1], F32(1), F32(0))
@@ -106,7 +108,7 @@
                 vec_ref[:, at],
             )
             if opens:
-                high, low = halves(g_ref[at, :] * side_ref[at, :])
+                high, low = halves(g_ref[at, :] * out_ref[at, :])
                 ones = jnp.ones((16, width), BF16)
                 delta_ref[:, at] = (dot(ones, high, NT) + dot(ones, low, NT))[0:8, :]
         return ready[tile]
@@ -143,6 +145,10 @@
         s_hi, s_lo = halves(grad_scores)
         dv_acc[at, :] += dot(p_hi, g_hi, NN) + dot(p_lo, g_hi, NN) + dot(p_hi, g_lo, NN)
         dk_acc[at, :] += dot(s_hi, q_hi, NN) + dot(s_lo, q_hi, NN) + dot(s_hi, q_lo, NN)
+        if keeps:
+            across = pl.ds(tile * TILE, TILE)
+            keep_hi[at, across], keep_lo[at, across] = s_hi, s_lo
+            return
         new = dot(kt_hi[:, at], s_hi, NN) + dot(kt_lo[:, at], s_hi, NN) + dot(kt_hi[:, at], s_lo, NN)
         totals[tile] = totals[tile] + new if tile in totals else new
 
@@ -153,10 +159,10 @@
         if order + 1 < len(work):
             coming = front(work[order + 1][0], blocks[work[order + 1][1]])
         back(tile, blocks[n], *here)
-        if n + 1 == len(blocks):
+        if not keeps and n + 1 == len(blocks):
             at = pl.ds(tile * TILE, TILE)
             dq = totals[tile].T * F32(1 / math.sqrt(width))
-            dq_ref[at, :] = dq if opens else dq + side_ref[at, :]
+            dq_ref[at, :] = dq if opens else sum_ref[at, :] + dq
 
     @pl.when(step == pl.num_programs(0) - 1)
     def _():
@@ -166,28 +172,36 @@
             out[rows : 2 * rows, :] = dv_acc[at, :]
 
 
-def attend(blocks, sources, q, g, vec, slabs, rows, side, delta=None):
+def attend(blocks, sources, q, g, vec, slabs, rows, *side):
     total, width = q.shape
     count = len(sources)
     keys = count * rows
     tiles = total // TILE
     steps = math.gcd(tiles, 4)
+    opens, keeps = side[0].shape[0] == total, len(side) == 1 and side[0].shape[0] != total
     tile_spec = pl.BlockSpec((steps * TILE, width), lambda i: (i, 0))
+    lane_spec = pl.BlockSpec((8, steps * TILE), lambda i: (0, i))
+    keep_spec = pl.BlockSpec((keys, steps * TILE), lambda i: (0, i))
     whole = lambda shape: pl.BlockSpec(shape, lambda i: (0, 0))
-    opens = delta is None
-    lane_spec = pl.BlockSpec((8, steps * TILE), lambda i: (0, i))
     computed = sum(b[1] for b in blocks)
-    results = pl.pallas_call(
-        functools.partial(kernel, blocks, sources, steps, rows, opens),
+    taken, given = [tile_spec], [tile_spec]
+    shapes = [jax.ShapeDtypeStruct((total, width), F32)]
+    if opens:
+        given = [tile_spec, lane_spec]
+        shapes.append(jax.ShapeDtypeStruct((8, total), F32))
+    elif keeps:
+        taken, given = [lane_spec], [keep_spec] * 2
+        shapes = [pltpu.HBM((keys, total), BF16)] * 2
+    else:
+        taken = [lane_spec, tile_spec]
+    return pl.pallas_call(
+        functools.partial(kernel, blocks, sources, steps, rows, opens, keeps),
         grid=(tiles // steps,),
         in_specs=[tile_spec, tile_spec, lane_spec]
         + [whole(slabs[0].shape)] * len(slabs)
-        + [tile_spec]
-        + ([] if opens else [lane_spec]),
-        out_specs=[tile_spec] + ([lane_spec] if opens else []) + [whole((2 * rows, width))] * count,
-        out_shape=[jax.ShapeDtypeStruct((total, width), F32)]
-        + ([jax.ShapeDtypeStruct((8, total), F32)] if opens else [])
-        + [jax.ShapeDtypeStruct((2 * rows, width), F32)] * count,
+        + taken,
+        out_specs=given + [whole((2 * rows, width))] * count,
+        out_shape=shapes + [jax.ShapeDtypeStruct((2 * rows, width), F32)] * count,
         scratch_shapes=[
             pltpu.VMEM((keys, width), BF16),
             pltpu.VMEM((keys, width), BF16),
@@ -199,12 +213,55 @@
             pltpu.VMEM((keys, width), F32),
             pltpu.VMEM((8, TILE), F32),
         ],
-        compiler_params=pltpu.CompilerParams(vmem_limit_bytes=24 * 1024 * 1024),
+        compiler_params=pltpu.CompilerParams(vmem_limit_bytes=GRANT),
         cost_estimate=pl.CostEstimate(
             flops=30 * total * computed * width, bytes_accessed=12 * total * width, transcendentals=total * computed
         ),
-    )(q, g, vec, *slabs, side, *([] if opens else [delta]))
-    return results
+    )(q, g, vec, *slabs, *side)
+
+
+def close(steps, count, rows, *refs):
+    part_ref, refs = refs[0], refs[1:]
+    kept, slabs, dq_ref, kt_hi, kt_lo = refs[:count], refs[count : 2 * count], refs[-3], refs[-2], refs[-1]
+    width = part_ref.shape[1]
+
+    @pl.when(pl.program_id(0) == 0)
+    def _():
+        for s, slab in enumerate(slabs):
+            at = pl.ds(s * rows, rows)
+            kt_hi[:, at], kt_lo[:, at] = halves(slab[...].T)
+
+    for tile in range(steps):
+        at = pl.ds(tile * TILE, TILE)
+        total = None
+        for n in range(0, count, 2):
+            keys = pl.ds(n * rows, 2 * rows)
+            high, low = kept[n][:, at], kept[n + 1][:, at]
+            new = dot(kt_hi[:, keys], high, NN) + dot(kt_lo[:, keys], high, NN) + dot(kt_hi[:, keys], low, NN)
+            total = new if total is None else total + new
+        dq_ref[at, :] = part_ref[at, :] + total.T * F32(1 / math.sqrt(width))
+
+
+def query_grads(part, kept, slabs, rows):
+    total, width = part.shape
+    tiles = total // TILE
+    steps = math.gcd(tiles, 2)
+    count = len(slabs)
+    tile_spec = pl.BlockSpec((steps * TILE, width), lambda i: (i, 0))
+    return pl.pallas_call(
+        functools.partial(close, steps, count, rows),
+        grid=(tiles // steps,),
+        in_specs=[tile_spec]
+        + [pl.BlockSpec((2 * rows, steps * TILE), lambda i: (0, i))] * count
+        + [pl.BlockSpec((rows, width), lambda i: (0, 0))] * count,
+        out_specs=tile_spec,
+        out_shape=jax.ShapeDtypeStruct((total, width), F32),
+        scratch_shapes=[pltpu.VMEM((width, count * rows), BF16)] * 2,
+        compiler_params=pltpu.CompilerParams(vmem_limit_bytes=GRANT),
+        cost_estimate=pl.CostEstimate(
+            flops=6 * total * count * rows * width, bytes_accessed=4 * total * (count * rows + 2 * width), transcendentals=0
+        ),
+    )(part, *kept, *slabs)
 
 
 def program(queries, key_rows, value_rows, forward_out, out_grad, log_norm, doc_ids):
@@ -255,10 +312,17 @@
     returned = [shifted(far + jnp.where(odd, cross, 0.0), "seq", -reach)]
     returned.append(jnp.where(odd, 0.0, cross))
     blocks = ((0, rows, False), (rows, rows, False))
+    kept, slabs = [], []
     for d in range(reach - 2, 0, -2):
-        dq, part, hand = attend(blocks, (0, 1), q, g, vec, [mine[d], other[d]], rows, dq, delta)
+        if d > KEPT:
+            dq, part, hand = attend(blocks, (0, 1), q, g, vec, [mine[d], other[d]], rows, delta, dq)
+        else:
+            high, low, part, hand = attend(blocks, (0, 1), q, g, vec, [mine[d], other[d]], rows, delta)
+            kept += [high, low]
+            slabs += [mine[d], other[d]]
         hand = swapped(hand, "seq")
         returned.append(shifted(part + hand, "seq", -d))
+    dq = query_grads(here(dq), [here(x) for x in kept], [here(x) for x in slabs], rows)
     keys_grad = sum([part[:rows] for part in returned], own_part[:rows])
     values_grad = sum([part[rows:] for part in returned], own_part[rows:])
     if lax.axis_size("head") > 1:

time: 195 us -> 191 us (0.979)
  waiting for transfers between devices: 75.4 us -> 64.1 us
  Pallas kernels: 86.9 us -> 94.2 us
    ppermute x8, waiting for transfers between devices: 75.4 us -> 64 us  [shifted(): lax.ppermute(value, axis, [(source, source + steps) for source in range(l...]
    pallas_call x0 -> x1, Pallas kernels: none -> 11.3 us  [query_grads(): pl.pallas_call(functools.partial(close, steps, count, rows), grid=(tiles...]
    pallas_call x4, Pallas kernels: 85 us -> 81 us  [attend(): pl.pallas_call(functools.partial(kernel, blocks, sources, steps, rows, op...]
  transfers between devices with their start and end apart: 17 -> 17, of which waited for: 5 -> 5; matrix products, arithmetic and copies ran while one was open for 3% -> 3% of each run, Pallas kernels for 44% -> 49%
where the time goes in v4:
time: 191 us; the launch traced here: 190 us
  Pallas kernels  94.2 us (49%)
  waiting for transfers between devices  64.1 us (34%)
  starting transfers between devices  22.3 us (12%)
  local copies, waits for them, and re-layouts  5.01 us (3%)
  other arithmetic  3.08 us (2%)
    pallas_call x4, Pallas kernels, attend(): pl.pallas_call(functools.partial(kernel, blocks, sources, steps, rows, op...  81 us
    ppermute x8, waiting for transfers between devices, shifted(): lax.ppermute(value, axis, [(source, source + steps) for source in range(l...  64 us
    ppermute x8, starting transfers between devices, shifted(): lax.ppermute(value, axis, [(source, source + steps) for source in range(l...  20.5 us
    pallas_call x1, Pallas kernels, query_grads(): pl.pallas_call(functools.partial(close, steps, count, rows), grid=(tiles...  11.3 us
  transfers between devices with their start and end apart: 17, of which 5 were waited for; matrix products, arithmetic and copies ran while one was open for 3% of the time, Pallas kernels for 49%

profile of v4, /device:TPU:0, one launch (start us, length us, event | category | flops | bytes accessed | tf_op | source)
XLA Modules:
  0.0 190.2 jit_solution(935024540200117958)
XLA Ops:
  0.6 1.9 shard_map.94.refs_4_
  2.5 5.0 %collective-permute-start.2 = (f32[520,256]{1,0:T(8,128)}, f32[520,256]{1,0:T(8,128)S(1)}, u32[]{:S(2)}, u32[]{:S(2)}) collective-permute-start(f32[520,256]{1,0:T(8,128)} %shard_map.94.refs_4_), channel_id=1, source_target_pairs={{0,8},{1,9},{2,10},{3,11},{4,12},{5,13},{6,14},{7,15},{8,16},{9,17... | collective-permute-start | bytes 1597448 | tf_op jit(solution)/shard_map/ppermute | solution.py:28
  7.5 0.1 collective-permute-start.4
  7.6 4.4 %collective-permute-start.5 = (f32[520,256]{1,0:T(8,128)}, f32[520,256]{1,0:T(8,128)S(1)}, u32[]{:S(2)}, u32[]{:S(2)}) collective-permute-start(f32[520,256]{1,0:T(8,128)} %shard_map.94.refs_4_), channel_id=1, source_target_pairs={{0,6},{1,7},{2,8},{3,9},{4,10},{5,11},{6,12},{7,13},{8,14},{9,15},... | collective-permute-start | bytes 1597448 | tf_op jit(solution)/shard_map/ppermute | solution.py:28
  12.0 3.4 %collective-permute-start = (f32[520,256]{1,0:T(8,128)}, f32[520,256]{1,0:T(8,128)S(1)}, u32[]{:S(2)}, u32[]{:S(2)}) collective-permute-start(f32[520,256]{1,0:T(8,128)} %shard_map.94.refs_4_), channel_id=1, source_target_pairs={{0,4},{1,5},{2,6},{3,7},{4,8},{5,9},{6,10},{7,11},{8,12},{9,13},{1... | collective-permute-start | bytes 1597448 | tf_op jit(solution)/shard_map/ppermute | solution.py:28
  15.4 2.5 %collective-permute-start.7 = (f32[520,256]{1,0:T(8,128)}, f32[520,256]{1,0:T(8,128)S(1)}, u32[]{:S(2)}, u32[]{:S(2)}) collective-permute-start(f32[520,256]{1,0:T(8,128)} %shard_map.94.refs_4_), channel_id=1, source_target_pairs={{0,2},{1,3},{2,4},{3,5},{4,6},{5,7},{6,8},{7,9},{8,10},{9,11},{10,... | collective-permute-start | bytes 1597448 | tf_op jit(solution)/shard_map/ppermute | solution.py:28
  17.9 0.9 convert_reduce_fusion
  18.9 0.7 broadcast_multiply_fusion
  19.6 0.0 collective-permute-done.2.refs_3_
  19.6 0.0 collective-permute-start.3
  19.6 1.2 slice.39
  21.5 1.1 broadcast_in_dim.27
  22.6 1.4 reshape.72
  24.0 0.1 copy.12
  24.1 0.1 reshape.71
  24.3 0.1 pad_maximum_fusion.refs_2_
  24.3 0.4 collective-permute-done.5.refs_3_
  24.8 0.1 collective-permute-start.6
  24.9 13.9 %collective-permute-done.refs_3_ = f32[520,256]{1,0:T(8,128)S(1)} collective-permute-done((f32[520,256]{1,0:T(8,128)}, f32[520,256]{1,0:T(8,128)S(1)}, u32[]{:S(2)}, u32[]{:S(2)}) %collective-permute-start) | collective-permute-done | bytes 532512 | tf_op jit(solution)/shard_map/ppermute | solution.py:28
  38.8 0.0 collective-permute-start.1
  38.8 0.0 collective-permute-done.7.refs_3_
  38.8 0.0 copy-start.1
  38.8 0.5 collective-permute-start.8
  39.3 0.0 collective-permute-done.4.refs_6_
  39.3 0.0 collective-permute-done.3.refs_5_
  39.3 0.0 copy-start.3
  39.3 1.0 copy-done.3
  40.4 0.0 copy-start.4
  40.4 0.0 copy-start.5
  40.4 27.3 %shard_map.95 = (f32[4096,256]{1,0:T(8,128)S(1)}, f32[8,4096]{1,0:T(8,128)S(1)}, f32[512,256]{1,0:T(8,128)S(1)}, f32[512,256]{1,0:T(8,128)S(1)}, f32[512,256]{1,0:T(8,128)S(1)}) custom-call(f32[4096,256]{1,0:T(8,128)} %bitcast.7, f32[4096,256]{1,0:T(8,128)} %bitcast.11, f32[8,4096]{1,0:T(8,128)S(1)} %pad_maximum_fusion.refs_2_, ...), custom_call_target="tpu_custom_call" | custom-call | flops 20132659200 | bytes 12582912 | tf_op jit(solution)/shard_map/pallas_call | solution.py:197
  67.7 0.0 collective-permute-done.6.refs_4_
  67.7 0.0 copy-done.4
  67.7 0.0 copy-done.5
  67.8 18.7 %shard_map.96 = (f32[4096,256]{1,0:T(8,128)S(1)}, f32[512,256]{1,0:T(8,128)S(1)}, f32[512,256]{1,0:T(8,128)S(1)}) custom-call(f32[4096,256]{1,0:T(8,128)S(1)} %bitcast.8, f32[4096,256]{1,0:T(8,128)S(1)} %bitcast.12, f32[8,4096]{1,0:T(8,128)S(1)} %pad_maximum_fusion.refs_2_, f32[520,256]{1,0:T(8,128)S(1)} %collective-permute-done.5.refs_3_, ...), custom_call_target="tpu_custom_call" | custom-call | flops 16106127360 | bytes 12582912 | tf_op jit(solution)/shard_map/pallas_call | solution.py:197
  86.4 0.0 collective-permute-done.1.refs_4_
  86.4 18.8 %shard_map.97 = (f32[4096,256]{1,0:T(8,128)S(1)}, f32[512,256]{1,0:T(8,128)S(1)}, f32[512,256]{1,0:T(8,128)S(1)}) custom-call(f32[4096,256]{1,0:T(8,128)S(1)} %bitcast.9, f32[4096,256]{1,0:T(8,128)S(1)} %bitcast.13, f32[8,4096]{1,0:T(8,128)S(1)} %pad_maximum_fusion.refs_2_, f32[520,256]{1,0:T(8,128)S(1)} %collective-permute-done.refs_3_, ...), custom_call_target="tpu_custom_call" | custom-call | flops 16106127360 | bytes 12582912 | tf_op jit(solution)/shard_map/pallas_call | solution.py:197
  105.2 0.0 copy-start
  105.2 0.3 collective-permute-start.13
  105.5 0.0 collective-permute-done.8.refs_4_
  105.5 0.0 copy-done.1
  105.5 16.2 %shard_map.98 = (bf16[512,4096]{1,0:T(8,128)(2,1)}, bf16[512,4096]{1,0:T(8,128)(2,1)}, f32[512,256]{1,0:T(8,128)S(1)}, f32[512,256]{1,0:T(8,128)S(1)}) custom-call(f32[4096,256]{1,0:T(8,128)S(1)} %bitcast.10, f32[4096,256]{1,0:T(8,128)S(1)} %bitcast.14, f32[8,4096]{1,0:T(8,128)S(1)} %pad_maximum_fusion.refs_2_, ...), custom_call_target="tpu_custom_call" | custom-call | flops 16106127360 | bytes 12582912 | tf_op jit(solution)/shard_map/pallas_call | solution.py:197
  121.7 0.0 copy-done
  121.7 0.0 copy-done.2
  121.7 0.3 collective-permute-start.15
  122.0 0.2 collective-permute-start.11
  122.2 0.3 collective-permute-start.9
  122.5 0.0 collective-permute-done.13
  122.5 0.1 add.101
  122.6 1.3 collective-permute-start.14
  123.9 0.0 collective-permute-done.15
  123.9 0.1 add.103
  124.0 1.3 collective-permute-start.16
  125.3 0.0 collective-permute-done.11
  125.3 0.1 add.99
  125.4 1.3 collective-permute-start.12
  126.7 0.0 collective-permute-done.9
  126.7 0.1 select_add_fusion
  126.8 1.3 collective-permute-start.10
  128.1 11.3 %shard_map.99 = f32[4096,256]{1,0:T(8,128)} custom-call(f32[4096,256]{1,0:T(8,128)} %copy-done, bf16[512,4096]{1,0:T(8,128)(2,1)} %get-tuple-element.22.refs_1_, bf16[512,4096]{1,0:T(8,128)(2,1)} %get-tuple-element.23.refs_2_, f32[520,256]{1,0:T(8,128)} %copy-done.1, f32[520,256]{1,0:T(8,128)} %copy-done.2), custom_call_target="tpu_custom_call" | custom-call | flops 3221225472 | bytes 16777216 | tf_op jit(solution)/shard_map/pallas_call | solution.py:251
  139.4 2.1 %collective-permute-done.14 = f32[512,256]{1,0:T(8,128)S(1)} collective-permute-done((f32[512,256]{1,0:T(8,128)S(1)}, f32[512,256]{1,0:T(8,128)S(1)}, u32[]{:S(2)}, u32[]{:S(2)}) %collective-permute-start.14) | collective-permute-done | bytes 524320 | tf_op jit(solution)/shard_map/ppermute | solution.py:28
  141.5 0.0 collective-permute-done.16
  141.5 25.3 %collective-permute-done.12 = f32[512,256]{1,0:T(8,128)S(1)} collective-permute-done((f32[512,256]{1,0:T(8,128)S(1)}, f32[512,256]{1,0:T(8,128)S(1)}, u32[]{:S(2)}, u32[]{:S(2)}) %collective-permute-start.12) | collective-permute-done | bytes 524320 | tf_op jit(solution)/shard_map/ppermute | solution.py:28
  166.9 22.2 %collective-permute-done.10 = f32[512,256]{1,0:T(8,128)S(1)} collective-permute-done((f32[512,256]{1,0:T(8,128)S(1)}, f32[512,256]{1,0:T(8,128)S(1)}, u32[]{:S(2)}, u32[]{:S(2)}) %collective-permute-start.10) | collective-permute-done | bytes 524320 | tf_op jit(solution)/shard_map/ppermute | solution.py:28
  189.1 1.1 slice_add_fusion
  (8 shorter events, 0.1 us)
Async XLA Ops:
  2.5 17.1 %collective-permute-start.2 = (f32[520,256]{1,0:T(8,128)}, f32[520,256]{1,0:T(8,128)S(1)}, u32[]{:S(2)}, u32[]{:S(2)}) collective-permute-start(f32[520,256]{1,0:T(8,128)} %shard_map.94.refs_4_), channel_id=1, source_target_pairs={{0,8},{1,9},{2,10},{3,11},{4,12},{5,13},{6,14},{7,15},{8,16},{9,17... | collective-permute-start | bytes 1597448 | tf_op jit(solution)/shard_map/ppermute | solution.py:28
  7.5 31.8 %collective-permute-start.4 = (f32[520,256]{1,0:T(8,128)}, f32[520,256]{1,0:T(8,128)S(1)}, u32[]{:S(2)}, u32[]{:S(2)}) collective-permute-start(f32[520,256]{1,0:T(8,128)} %shard_map.94.refs_4_), channel_id=1, source_target_pairs={{0,1},{1,0},{2,3},{3,2},{4,5},{5,4},{6,7},{7,6},{8,9},{9,8},{10,11... | collective-permute-start | bytes 1597448 | tf_op jit(solution)/shard_map/ppermute | solution.py:33
  7.6 17.2 %collective-permute-start.5 = (f32[520,256]{1,0:T(8,128)}, f32[520,256]{1,0:T(8,128)S(1)}, u32[]{:S(2)}, u32[]{:S(2)}) collective-permute-start(f32[520,256]{1,0:T(8,128)} %shard_map.94.refs_4_), channel_id=1, source_target_pairs={{0,6},{1,7},{2,8},{3,9},{4,10},{5,11},{6,12},{7,13},{8,14},{9,15},... | collective-permute-start | bytes 1597448 | tf_op jit(solution)/shard_map/ppermute | solution.py:28
  12.0 26.8 %collective-permute-start = (f32[520,256]{1,0:T(8,128)}, f32[520,256]{1,0:T(8,128)S(1)}, u32[]{:S(2)}, u32[]{:S(2)}) collective-permute-start(f32[520,256]{1,0:T(8,128)} %shard_map.94.refs_4_), channel_id=1, source_target_pairs={{0,4},{1,5},{2,6},{3,7},{4,8},{5,9},{6,10},{7,11},{8,12},{9,13},{1... | collective-permute-start | bytes 1597448 | tf_op jit(solution)/shard_map/ppermute | solution.py:28
  15.4 23.4 %collective-permute-start.7 = (f32[520,256]{1,0:T(8,128)}, f32[520,256]{1,0:T(8,128)S(1)}, u32[]{:S(2)}, u32[]{:S(2)}) collective-permute-start(f32[520,256]{1,0:T(8,128)} %shard_map.94.refs_4_), channel_id=1, source_target_pairs={{0,2},{1,3},{2,4},{3,5},{4,6},{5,7},{6,8},{7,9},{8,10},{9,11},{10,... | collective-permute-start | bytes 1597448 | tf_op jit(solution)/shard_map/ppermute | solution.py:28
  19.6 19.7 %collective-permute-start.3 = (f32[520,256]{1,0:T(8,128)S(1)}, f32[520,256]{1,0:T(8,128)S(1)}, u32[]{:S(2)}, u32[]{:S(2)}) collective-permute-start(f32[520,256]{1,0:T(8,128)S(1)} %collective-permute-done.2.refs_3_), channel_id=1, source_target_pairs={{0,1},{1,0},{2,3},{3,2},{4,5},{5,4},{6,7},{7,6},{8,9},{9,8},{10,11... | collective-permute-start | bytes 1597448 | tf_op jit(solution)/shard_map/ppermute | solution.py:33
  24.8 43.0 %collective-permute-start.6 = (f32[520,256]{1,0:T(8,128)S(1)}, f32[520,256]{1,0:T(8,128)S(1)}, u32[]{:S(2)}, u32[]{:S(2)}) collective-permute-start(f32[520,256]{1,0:T(8,128)S(1)} %collective-permute-done.5.refs_3_), channel_id=1, source_target_pairs={{0,1},{1,0},{2,3},{3,2},{4,5},{5,4},{6,7},{7,6},{8,9},{9,8},{10,11... | collective-permute-start | bytes 1597448 | tf_op jit(solution)/shard_map/ppermute | solution.py:33
  38.8 47.6 %collective-permute-start.1 = (f32[520,256]{1,0:T(8,128)S(1)}, f32[520,256]{1,0:T(8,128)S(1)}, u32[]{:S(2)}, u32[]{:S(2)}) collective-permute-start(f32[520,256]{1,0:T(8,128)S(1)} %collective-permute-done.refs_3_), channel_id=1, source_target_pairs={{0,1},{1,0},{2,3},{3,2},{4,5},{5,4},{6,7},{7,6},{8,9},{9,8},{10,11... | collective-permute-start | bytes 1597448 | tf_op jit(solution)/shard_map/ppermute | solution.py:33
  38.8 66.7 %copy-start.1 = (f32[520,256]{1,0:T(8,128)}, f32[520,256]{1,0:T(8,128)S(1)}, u32[]{:S(2)}) copy-start(f32[520,256]{1,0:T(8,128)S(1)} %collective-permute-done.7.refs_3_) | copy-start | bytes 1597444
  38.8 66.7 %collective-permute-start.8 = (f32[520,256]{1,0:T(8,128)S(1)}, f32[520,256]{1,0:T(8,128)S(1)}, u32[]{:S(2)}, u32[]{:S(2)}) collective-permute-start(f32[520,256]{1,0:T(8,128)S(1)} %collective-permute-done.7.refs_3_), channel_id=1, source_target_pairs={{0,1},{1,0},{2,3},{3,2},{4,5},{5,4},{6,7},{7,6},{8,9},{9,8},{10,11... | collective-permute-start | bytes 1597448 | tf_op jit(solution)/shard_map/ppermute | solution.py:33
  39.3 1.0 copy-start.3
  40.4 27.4 %copy-start.4 = (f32[256,16,256]{2,1,0:T(8,128)S(1)}, f32[256,16,256]{2,1,0:T(8,128)}, u32[]{:S(2)}) copy-start(f32[256,16,256]{2,1,0:T(8,128)} %param.7) | copy-start | bytes 12582916
  40.4 27.4 %copy-start.5 = (f32[256,16,256]{2,1,0:T(8,128)S(1)}, f32[256,16,256]{2,1,0:T(8,128)}, u32[]{:S(2)}) copy-start(f32[256,16,256]{2,1,0:T(8,128)} %param.11) | copy-start | bytes 12582916
  105.2 16.5 %copy-start = (f32[4096,256]{1,0:T(8,128)}, f32[4096,256]{1,0:T(8,128)S(1)}, u32[]{:S(2)}) copy-start(f32[4096,256]{1,0:T(8,128)S(1)} %get-tuple-element.21.refs_0_) | copy-start | bytes 12582916
  105.2 17.3 %collective-permute-start.13 = (f32[512,256]{1,0:T(8,128)S(1)}, f32[512,256]{1,0:T(8,128)S(1)}, u32[]{:S(2)}, u32[]{:S(2)}) collective-permute-start(f32[512,256]{1,0:T(8,128)S(1)} %get-tuple-element.30), channel_id=1, source_target_pairs={{0,1},{1,0},{2,3},{3,2},{4,5},{5,4},{6,7},{7,6},{8,9},{9,8},{10,11... | collective-permute-start | bytes 1572872 | tf_op jit(solution)/shard_map/ppermute | solution.py:33
  105.5 16.2 %copy-start.2 = (f32[520,256]{1,0:T(8,128)}, f32[520,256]{1,0:T(8,128)S(1)}, u32[]{:S(2)}) copy-start(f32[520,256]{1,0:T(8,128)S(1)} %collective-permute-done.8.refs_4_) | copy-start | bytes 1597444
  121.7 2.2 %collective-permute-start.15 = (f32[512,256]{1,0:T(8,128)S(1)}, f32[512,256]{1,0:T(8,128)S(1)}, u32[]{:S(2)}, u32[]{:S(2)}) collective-permute-start(f32[512,256]{1,0:T(8,128)S(1)} %get-tuple-element.32), channel_id=1, source_target_pairs={{0,1},{1,0},{2,3},{3,2},{4,5},{5,4},{6,7},{7,6},{8,9},{9,8},{10,11... | collective-permute-start | bytes 1572872 | tf_op jit(solution)/shard_map/ppermute | solution.py:33
  122.0 3.3 %collective-permute-start.11 = (f32[512,256]{1,0:T(8,128)S(1)}, f32[512,256]{1,0:T(8,128)S(1)}, u32[]{:S(2)}, u32[]{:S(2)}) collective-permute-start(f32[512,256]{1,0:T(8,128)S(1)} %get-tuple-element.28), channel_id=1, source_target_pairs={{0,1},{1,0},{2,3},{3,2},{4,5},{5,4},{6,7},{7,6},{8,9},{9,8},{10,11... | collective-permute-start | bytes 1572872 | tf_op jit(solution)/shard_map/ppermute | solution.py:33
  122.2 4.5 %collective-permute-start.9 = (f32[512,256]{1,0:T(8,128)S(1)}, f32[512,256]{1,0:T(8,128)S(1)}, u32[]{:S(2)}, u32[]{:S(2)}) collective-permute-start(f32[512,256]{1,0:T(8,128)S(1)} %get-tuple-element.26), channel_id=1, source_target_pairs={{0,1},{1,0},{2,3},{3,2},{4,5},{5,4},{6,7},{7,6},{8,9},{9,8},{10,11... | collective-permute-start | bytes 1572872 | tf_op jit(solution)/shard_map/ppermute | solution.py:33
  122.6 18.9 %collective-permute-start.14 = (f32[512,256]{1,0:T(8,128)S(1)}, f32[512,256]{1,0:T(8,128)S(1)}, u32[]{:S(2)}, u32[]{:S(2)}) collective-permute-start(f32[512,256]{1,0:T(8,128)S(1)} %add.101), channel_id=1, source_target_pairs={{4,0},{5,1},{6,2},{7,3},{8,4},{9,5},{10,6},{11,7},{12,8},{13,9},{1... | collective-permute-start | bytes 1572872 | tf_op jit(solution)/shard_map/ppermute | solution.py:28
  124.0 17.6 %collective-permute-start.16 = (f32[512,256]{1,0:T(8,128)S(1)}, f32[512,256]{1,0:T(8,128)S(1)}, u32[]{:S(2)}, u32[]{:S(2)}) collective-permute-start(f32[512,256]{1,0:T(8,128)S(1)} %add.103), channel_id=1, source_target_pairs={{2,0},{3,1},{4,2},{5,3},{6,4},{7,5},{8,6},{9,7},{10,8},{11,9},{12,... | collective-permute-start | bytes 1572872 | tf_op jit(solution)/shard_map/ppermute | solution.py:28
  125.4 41.5 %collective-permute-start.12 = (f32[512,256]{1,0:T(8,128)S(1)}, f32[512,256]{1,0:T(8,128)S(1)}, u32[]{:S(2)}, u32[]{:S(2)}) collective-permute-start(f32[512,256]{1,0:T(8,128)S(1)} %add.99), channel_id=1, source_target_pairs={{6,0},{7,1},{8,2},{9,3},{10,4},{11,5},{12,6},{13,7},{14,8},{15,9},... | collective-permute-start | bytes 1572872 | tf_op jit(solution)/shard_map/ppermute | solution.py:28
  126.8 62.3 %collective-permute-start.10 = (f32[512,256]{1,0:T(8,128)S(1)}, f32[512,256]{1,0:T(8,128)S(1)}, u32[]{:S(2)}, u32[]{:S(2)}) collective-permute-start(f32[512,256]{1,0:T(8,128)S(1)} %get-tuple-element.35), channel_id=1, source_target_pairs={{8,0},{9,1},{10,2},{11,3},{12,4},{13,5},{14,6},{15,7},{16,8},{17,9... | collective-permute-start | bytes 1572872 | tf_op jit(solution)/shard_map/ppermute | solution.py:28

commit v5 on v4

--- a/solution.py
+++ b/solution.py
@@ -11,8 +11,9 @@
 
 WIN = 2048
 TILE = 256
+LANES = 128
 LOG2E = math.log2(math.e)
-KEPT = 2
+KEPT = 4
 GRANT = 24 * 1024 * 1024
 LN2 = math.log(2.0)
 MASKED = -1e30
@@ -70,7 +71,7 @@
     else:
         delta_ref, sum_ref, dq_ref, *rest = rest
     outs, rest = rest[: len(sources)], rest[len(sources) :]
-    k_hi, k_lo, kt_hi, kt_lo, v_hi, v_lo, dk_acc, dv_acc, first_ref = rest
+    k_hi, k_lo, kt_hi, kt_lo, v_hi, v_lo, dk_acc, dv_acc, first_ref, *pads = rest
     step = pl.program_id(0)
     width = q_ref.shape[1]
 
@@ -116,7 +117,7 @@
     def span(tile, block):
         start, size, _ = block
         if callable(start):
-            start = pl.multiple_of(start(step * steps + tile), 128)
+            start = pl.multiple_of(start(step * steps + tile), 16)
         return pl.ds(start, size), start
 
     def front(tile, block):
@@ -149,6 +150,16 @@
             across = pl.ds(tile * TILE, TILE)
             keep_hi[at, across], keep_lo[at, across] = s_hi, s_lo
             return
+        if callable(block[0]) and pads[0].shape[1] > size:
+            base = pl.multiple_of(start // LANES * LANES, LANES)
+            padded = pads[0].shape[1]
+            at = pl.ds(base, padded)
+            inner = pl.ds(pl.multiple_of(start - base, 16), size)
+            for pad, half in zip(pads, (s_hi, s_lo)):
+                for edge in (0, padded - LANES):
+                    pad[tile, pl.ds(edge, LANES), :] = jnp.zeros((LANES, TILE), BF16)
+                pad[tile, inner, :] = half
+            s_hi, s_lo = pads[0][tile], pads[1][tile]
         new = dot(kt_hi[:, at], s_hi, NN) + dot(kt_lo[:, at], s_hi, NN) + dot(kt_hi[:, at], s_lo, NN)
         totals[tile] = totals[tile] + new if tile in totals else new
 
@@ -177,8 +188,8 @@
     count = len(sources)
     keys = count * rows
     tiles = total // TILE
-    steps = math.gcd(tiles, 4)
     opens, keeps = side[0].shape[0] == total, len(side) == 1 and side[0].shape[0] != total
+    steps = math.gcd(tiles, 4 if opens or keeps else 8)
     tile_spec = pl.BlockSpec((steps * TILE, width), lambda i: (i, 0))
     lane_spec = pl.BlockSpec((8, steps * TILE), lambda i: (0, i))
     keep_spec = pl.BlockSpec((keys, steps * TILE), lambda i: (0, i))
@@ -212,7 +223,8 @@
             pltpu.VMEM((keys, width), F32),
             pltpu.VMEM((keys, width), F32),
             pltpu.VMEM((8, TILE), F32),
-        ],
+        ]
+        + [pltpu.VMEM((steps, rows + max(b[1] - rows, LANES), TILE), BF16) for b in blocks if callable(b[0])] * 2,
         compiler_params=pltpu.CompilerParams(vmem_limit_bytes=GRANT),
         cost_estimate=pl.CostEstimate(
             flops=30 * total * computed * width, bytes_accessed=12 * total * width, transcendentals=total * computed
@@ -245,7 +257,7 @@
 def query_grads(part, kept, slabs, rows):
     total, width = part.shape
     tiles = total // TILE
-    steps = math.gcd(tiles, 2)
+    steps = math.gcd(tiles, 4)
     count = len(slabs)
     tile_spec = pl.BlockSpec((steps * TILE, width), lambda i: (i, 0))
     return pl.pallas_call(
@@ -289,7 +301,7 @@
             jnp.where(first, token + 1, rows + before),
             jnp.where(first, 0.0, 1e9),
             token + rows,
-            jnp.broadcast_to(ids[0].astype(F32) + 1, (rows,)),
+            ids.astype(F32) + 1,
             jnp.broadcast_to(odd.astype(F32), (rows,)),
         ]
     )
@@ -301,8 +313,8 @@
     q = queries.reshape(rows * heads, width)
     g = out_grad.reshape(rows * heads, width)
     tokens = TILE // heads
-    edge = max(tokens, 128)
-    edges = ((lambda i: (i * tokens) // edge * edge, rows + edge, True), (2 * rows, rows, False))
+    unit = max(tokens, 16)
+    edges = ((lambda i: (i * tokens) // unit * unit, rows + unit, True), (2 * rows, rows, False))
     out = forward_out.reshape(rows * heads, width)
     here = lambda x: pltpu.with_memory_space_constraint(x, pltpu.HBM)
     dq, delta, far, own_part, cross = attend(

time: 191 us -> 188 us (0.984)
  the two profiles are of different devices: /device:TPU:0 before, /device:TPU:12 now
where the time goes in v5:
time: 188 us; the launch traced here: 187 us
  Pallas kernels  90.3 us (48%)
  waiting for transfers between devices  65.2 us (35%)
  starting transfers between devices  23.2 us (12%)
  local copies, waits for them, and re-layouts  3.82 us (2%)
  other arithmetic  3.76 us (2%)
    pallas_call x4, Pallas kernels, attend(): pl.pallas_call(functools.partial(kernel, blocks, sources, steps, rows, op...  74.8 us
    ppermute x8, waiting for transfers between devices, shifted(): lax.ppermute(value, axis, [(source, source + steps) for source in range(l...  65.1 us
    ppermute x8, starting transfers between devices, shifted(): lax.ppermute(value, axis, [(source, source + steps) for source in range(l...  21.3 us
    pallas_call x1, Pallas kernels, query_grads(): pl.pallas_call(functools.partial(close, steps, count, rows), grid=(tiles...  13.7 us
  transfers between devices with their start and end apart: 17, of which 4 were waited for; matrix products, arithmetic and copies ran while one was open for 3% of the time, Pallas kernels for 47%

profile of v5, /device:TPU:12, one launch (start us, length us, event | category | flops | bytes accessed | tf_op | source)
XLA Modules:
  0.0 187.1 jit_solution(8938127150049241829)
XLA Ops:
  0.6 1.9 %shard_map.94.refs_4_ = f32[520,256]{1,0:T(8,128)} custom-call(f32[256,256]{1,0:T(8,128)} %k_ref.1, f32[256,256]{1,0:T(8,128)} %v_ref.1, s32[1,256]{1,0:T(1,128)} %bitcast.16), custom_call_target="tpu_custom_call" | custom-call | tf_op jit(solution)/shard_map/pallas_call | solution.py:58
  2.5 3.4 %collective-permute-start.7 = (f32[520,256]{1,0:T(8,128)}, f32[520,256]{1,0:T(8,128)S(1)}, u32[]{:S(2)}, u32[]{:S(2)}) collective-permute-start(f32[520,256]{1,0:T(8,128)} %shard_map.94.refs_4_), channel_id=1, source_target_pairs={{0,2},{1,3},{2,4},{3,5},{4,6},{5,7},{6,8},{7,9},{8,10},{9,11},{10,... | collective-permute-start | bytes 1597448 | tf_op jit(solution)/shard_map/ppermute | solution.py:29
  5.9 3.4 %collective-permute-start.5 = (f32[520,256]{1,0:T(8,128)}, f32[520,256]{1,0:T(8,128)S(1)}, u32[]{:S(2)}, u32[]{:S(2)}) collective-permute-start(f32[520,256]{1,0:T(8,128)} %shard_map.94.refs_4_), channel_id=1, source_target_pairs={{0,4},{1,5},{2,6},{3,7},{4,8},{5,9},{6,10},{7,11},{8,12},{9,13},{1... | collective-permute-start | bytes 1597448 | tf_op jit(solution)/shard_map/ppermute | solution.py:29
  9.3 0.1 collective-permute-start.4
  9.4 3.5 %collective-permute-start.2 = (f32[520,256]{1,0:T(8,128)}, f32[520,256]{1,0:T(8,128)S(1)}, u32[]{:S(2)}, u32[]{:S(2)}) collective-permute-start(f32[520,256]{1,0:T(8,128)} %shard_map.94.refs_4_), channel_id=1, source_target_pairs={{0,8},{1,9},{2,10},{3,11},{4,12},{5,13},{6,14},{7,15},{8,16},{9,17... | collective-permute-start | bytes 1597448 | tf_op jit(solution)/shard_map/ppermute | solution.py:29
  12.9 2.8 %collective-permute-start = (f32[520,256]{1,0:T(8,128)}, f32[520,256]{1,0:T(8,128)S(1)}, u32[]{:S(2)}, u32[]{:S(2)}) collective-permute-start(f32[520,256]{1,0:T(8,128)} %shard_map.94.refs_4_), channel_id=1, source_target_pairs={{0,6},{1,7},{2,8},{3,9},{4,10},{5,11},{6,12},{7,13},{8,14},{9,15},... | collective-permute-start | bytes 1597448 | tf_op jit(solution)/shard_map/ppermute | solution.py:29
  15.8 0.9 convert_reduce_fusion
  16.7 0.7 broadcast_multiply_fusion
  17.5 25.8 %collective-permute-done.2.refs_3_ = f32[520,256]{1,0:T(8,128)S(1)} collective-permute-done((f32[520,256]{1,0:T(8,128)}, f32[520,256]{1,0:T(8,128)S(1)}, u32[]{:S(2)}, u32[]{:S(2)}) %collective-permute-start.2) | collective-permute-done | bytes 532512 | tf_op jit(solution)/shard_map/ppermute | solution.py:29
  43.3 0.0 collective-permute-start.3
  43.3 0.7 convert_add_fusion
  43.9 0.1 copy.12
  44.0 0.1 reshape.68
  44.2 1.1 broadcast_in_dim.27
  45.3 1.4 reshape.69
  46.7 0.1 pad_maximum_fusion.refs_2_
  46.8 0.0 collective-permute-done.7.refs_3_.refs_7_
  46.8 0.0 copy-start.1
  46.8 0.6 collective-permute-start.8
  47.4 0.0 collective-permute-done.5.refs_3_.refs_5_
  47.4 0.1 collective-permute-start.6
  47.5 11.0 %collective-permute-done.refs_3_ = f32[520,256]{1,0:T(8,128)S(1)} collective-permute-done((f32[520,256]{1,0:T(8,128)}, f32[520,256]{1,0:T(8,128)S(1)}, u32[]{:S(2)}, u32[]{:S(2)}) %collective-permute-start) | collective-permute-done | bytes 532512 | tf_op jit(solution)/shard_map/ppermute | solution.py:29
  58.5 0.0 collective-permute-start.1
  58.5 0.0 collective-permute-done.4.refs_6_
  58.5 0.0 collective-permute-done.3.refs_5_
  58.5 0.0 copy-start.5
  58.5 1.0 copy-done.5
  59.6 24.3 %shard_map.95 = (f32[4096,256]{1,0:T(8,128)S(1)}, f32[8,4096]{1,0:T(8,128)S(1)}, f32[512,256]{1,0:T(8,128)S(1)}, f32[512,256]{1,0:T(8,128)S(1)}, f32[512,256]{1,0:T(8,128)S(1)}) custom-call(f32[4096,256]{1,0:T(8,128)} %bitcast.7, f32[4096,256]{1,0:T(8,128)} %bitcast.11, f32[8,4096]{1,0:T(8,128)S(1)} %pad_maximum_fusion.refs_2_, ...), custom_call_target="tpu_custom_call" | custom-call | flops 16609443840 | bytes 12582912 | tf_op jit(solution)/shard_map/pallas_call | solution.py:208
  83.9 0.0 collective-permute-done.1.refs_4_
  83.9 0.0 copy-done.6
  83.9 0.0 copy-done.7
  83.9 18.0 %shard_map.96 = (f32[4096,256]{1,0:T(8,128)S(1)}, f32[512,256]{1,0:T(8,128)S(1)}, f32[512,256]{1,0:T(8,128)S(1)}) custom-call(f32[4096,256]{1,0:T(8,128)S(1)} %bitcast.8, f32[4096,256]{1,0:T(8,128)S(1)} %bitcast.12, f32[8,4096]{1,0:T(8,128)S(1)} %pad_maximum_fusion.refs_2_, f32[520,256]{1,0:T(8,128)S(1)} %collective-permute-done.refs_3_, ...), custom_call_target="tpu_custom_call" | custom-call | flops 16106127360 | bytes 12582912 | tf_op jit(solution)/shard_map/pallas_call | solution.py:208
  101.9 0.0 copy-start
  101.9 0.6 collective-permute-start.11
  102.5 0.1 collective-permute-start.9
  102.5 0.0 collective-permute-done.8.refs_4_.refs_8_
  102.5 0.0 copy-done.1
  102.5 16.4 %shard_map.98 = (bf16[512,4096]{1,0:T(8,128)(2,1)}, bf16[512,4096]{1,0:T(8,128)(2,1)}, f32[512,256]{1,0:T(8,128)S(1)}, f32[512,256]{1,0:T(8,128)S(1)}) custom-call(f32[4096,256]{1,0:T(8,128)S(1)} %bitcast.9, f32[4096,256]{1,0:T(8,128)S(1)} %bitcast.13, f32[8,4096]{1,0:T(8,128)S(1)} %pad_maximum_fusion.refs_2_, ...), custom_call_target="tpu_custom_call" | custom-call | flops 16106127360 | bytes 12582912 | tf_op jit(solution)/shard_map/pallas_call | solution.py:208
  118.9 0.0 copy-done
  118.9 0.0 copy-done.3
  118.9 0.4 collective-permute-start.15
  119.4 0.0 collective-permute-done.6.refs_4_.refs_6_
  119.4 0.0 copy-done.2
  119.4 16.1 %shard_map.97 = (bf16[512,4096]{1,0:T(8,128)(2,1)}, bf16[512,4096]{1,0:T(8,128)(2,1)}, f32[512,256]{1,0:T(8,128)S(1)}, f32[512,256]{1,0:T(8,128)S(1)}) custom-call(f32[4096,256]{1,0:T(8,128)S(1)} %bitcast.10, f32[4096,256]{1,0:T(8,128)S(1)} %bitcast.14, f32[8,4096]{1,0:T(8,128)S(1)} %pad_maximum_fusion.refs_2_, ...), custom_call_target="tpu_custom_call" | custom-call | flops 16106127360 | bytes 12582912 | tf_op jit(solution)/shard_map/pallas_call | solution.py:208
  135.5 0.0 copy-done.4
  135.5 0.1 collective-permute-start.13
  135.6 0.0 collective-permute-done.11
  135.6 0.1 add.91
  135.7 1.9 %collective-permute-start.12 = (f32[512,256]{1,0:T(8,128)S(1)}, f32[512,256]{1,0:T(8,128)S(1)}, u32[]{:S(2)}, u32[]{:S(2)}) collective-permute-start(f32[512,256]{1,0:T(8,128)S(1)} %add.91), channel_id=1, source_target_pairs={{6,0},{7,1},{8,2},{9,3},{10,4},{11,5},{12,6},{13,7},{14,8},{15,9},... | collective-permute-start | bytes 1572872 | tf_op jit(solution)/shard_map/ppermute | solution.py:29
  137.6 0.0 collective-permute-done.9
  137.6 0.1 select_add_fusion
  137.7 1.9 %collective-permute-start.10 = (f32[512,256]{1,0:T(8,128)S(1)}, f32[512,256]{1,0:T(8,128)S(1)}, u32[]{:S(2)}, u32[]{:S(2)}) collective-permute-start(f32[512,256]{1,0:T(8,128)S(1)} %get-tuple-element.37), channel_id=1, source_target_pairs={{8,0},{9,1},{10,2},{11,3},{12,4},{13,5},{14,6},{15,7},{16,8},{17,9... | collective-permute-start | bytes 1572872 | tf_op jit(solution)/shard_map/ppermute | solution.py:29
  139.7 0.0 collective-permute-done.15
  139.7 0.1 add.95
  139.7 1.9 %collective-permute-start.16 = (f32[512,256]{1,0:T(8,128)S(1)}, f32[512,256]{1,0:T(8,128)S(1)}, u32[]{:S(2)}, u32[]{:S(2)}) collective-permute-start(f32[512,256]{1,0:T(8,128)S(1)} %add.95), channel_id=1, source_target_pairs={{2,0},{3,1},{4,2},{5,3},{6,4},{7,5},{8,6},{9,7},{10,8},{11,9},{12,... | collective-permute-start | bytes 1572872 | tf_op jit(solution)/shard_map/ppermute | solution.py:29
  141.7 0.0 collective-permute-done.13
  141.7 0.1 add.93
  141.8 2.4 %collective-permute-start.14 = (f32[512,256]{1,0:T(8,128)S(1)}, f32[512,256]{1,0:T(8,128)S(1)}, u32[]{:S(2)}, u32[]{:S(2)}) collective-permute-start(f32[512,256]{1,0:T(8,128)S(1)} %add.93), channel_id=1, source_target_pairs={{4,0},{5,1},{6,2},{7,3},{8,4},{9,5},{10,6},{11,7},{12,8},{13,9},{1... | collective-permute-start | bytes 1572872 | tf_op jit(solution)/shard_map/ppermute | solution.py:29
  144.2 13.7 %shard_map.99 = f32[4096,256]{1,0:T(8,128)} custom-call(f32[4096,256]{1,0:T(8,128)} %copy-done, bf16[512,4096]{1,0:T(8,128)(2,1)} %get-tuple-element.22.refs_1_, bf16[512,4096]{1,0:T(8,128)(2,1)} %get-tuple-element.23.refs_2_, bf16[512,4096]{1,0:T(8,128)(2,1)} %get-tuple-element.24.refs_3_, bf16[512,4096]{1,0:T(8,128)(2,1)} %get-tuple-element.25.refs_4_, ...), custom_call_target="tpu_custom_call" | custom-call | flops 6442450944 | bytes 25165824 | tf_op jit(solution)/shard_map/pallas_call | solution.py:263
  157.8 0.0 collective-permute-done.12
  157.8 5.1 %collective-permute-done.10 = f32[512,256]{1,0:T(8,128)S(1)} collective-permute-done((f32[512,256]{1,0:T(8,128)S(1)}, f32[512,256]{1,0:T(8,128)S(1)}, u32[]{:S(2)}, u32[]{:S(2)}) %collective-permute-start.10) | collective-permute-done | bytes 524320 | tf_op jit(solution)/shard_map/ppermute | solution.py:29
  162.9 0.0 collective-permute-done.16
  163.0 23.2 %collective-permute-done.14 = f32[512,256]{1,0:T(8,128)S(1)} collective-permute-done((f32[512,256]{1,0:T(8,128)S(1)}, f32[512,256]{1,0:T(8,128)S(1)}, u32[]{:S(2)}, u32[]{:S(2)}) %collective-permute-start.14) | collective-permute-done | bytes 524320 | tf_op jit(solution)/shard_map/ppermute | solution.py:29
  186.1 1.0 slice_add_fusion
  (11 shorter events, 0.1 us)
Async XLA Ops:
  2.5 44.3 %collective-permute-start.7 = (f32[520,256]{1,0:T(8,128)}, f32[520,256]{1,0:T(8,128)S(1)}, u32[]{:S(2)}, u32[]{:S(2)}) collective-permute-start(f32[520,256]{1,0:T(8,128)} %shard_map.94.refs_4_), channel_id=1, source_target_pairs={{0,2},{1,3},{2,4},{3,5},{4,6},{5,7},{6,8},{7,9},{8,10},{9,11},{10,... | collective-permute-start | bytes 1597448 | tf_op jit(solution)/shard_map/ppermute | solution.py:29
  5.9 41.5 %collective-permute-start.5 = (f32[520,256]{1,0:T(8,128)}, f32[520,256]{1,0:T(8,128)S(1)}, u32[]{:S(2)}, u32[]{:S(2)}) collective-permute-start(f32[520,256]{1,0:T(8,128)} %shard_map.94.refs_4_), channel_id=1, source_target_pairs={{0,4},{1,5},{2,6},{3,7},{4,8},{5,9},{6,10},{7,11},{8,12},{9,13},{1... | collective-permute-start | bytes 1597448 | tf_op jit(solution)/shard_map/ppermute | solution.py:29
  9.3 49.2 %collective-permute-start.4 = (f32[520,256]{1,0:T(8,128)}, f32[520,256]{1,0:T(8,128)S(1)}, u32[]{:S(2)}, u32[]{:S(2)}) collective-permute-start(f32[520,256]{1,0:T(8,128)} %shard_map.94.refs_4_), channel_id=1, source_target_pairs={{0,1},{1,0},{2,3},{3,2},{4,5},{5,4},{6,7},{7,6},{8,9},{9,8},{10,11... | collective-permute-start | bytes 1597448 | tf_op jit(solution)/shard_map/ppermute | solution.py:34
  9.4 33.8 %collective-permute-start.2 = (f32[520,256]{1,0:T(8,128)}, f32[520,256]{1,0:T(8,128)S(1)}, u32[]{:S(2)}, u32[]{:S(2)}) collective-permute-start(f32[520,256]{1,0:T(8,128)} %shard_map.94.refs_4_), channel_id=1, source_target_pairs={{0,8},{1,9},{2,10},{3,11},{4,12},{5,13},{6,14},{7,15},{8,16},{9,17... | collective-permute-start | bytes 1597448 | tf_op jit(solution)/shard_map/ppermute | solution.py:29
  12.9 45.6 %collective-permute-start = (f32[520,256]{1,0:T(8,128)}, f32[520,256]{1,0:T(8,128)S(1)}, u32[]{:S(2)}, u32[]{:S(2)}) collective-permute-start(f32[520,256]{1,0:T(8,128)} %shard_map.94.refs_4_), channel_id=1, source_target_pairs={{0,6},{1,7},{2,8},{3,9},{4,10},{5,11},{6,12},{7,13},{8,14},{9,15},... | collective-permute-start | bytes 1597448 | tf_op jit(solution)/shard_map/ppermute | solution.py:29
  43.3 15.3 %collective-permute-start.3 = (f32[520,256]{1,0:T(8,128)S(1)}, f32[520,256]{1,0:T(8,128)S(1)}, u32[]{:S(2)}, u32[]{:S(2)}) collective-permute-start(f32[520,256]{1,0:T(8,128)S(1)} %collective-permute-done.2.refs_3_), channel_id=1, source_target_pairs={{0,1},{1,0},{2,3},{3,2},{4,5},{5,4},{6,7},{7,6},{8,9},{9,8},{10,11... | collective-permute-start | bytes 1597448 | tf_op jit(solution)/shard_map/ppermute | solution.py:34
  46.8 55.7 %copy-start.1 = (f32[520,256]{1,0:T(8,128)}, f32[520,256]{1,0:T(8,128)S(1)}, u32[]{:S(2)}) copy-start(f32[520,256]{1,0:T(8,128)S(1)} %collective-permute-done.7.refs_3_.refs_7_) | copy-start | bytes 1597444
  46.8 55.7 %collective-permute-start.8 = (f32[520,256]{1,0:T(8,128)S(1)}, f32[520,256]{1,0:T(8,128)S(1)}, u32[]{:S(2)}, u32[]{:S(2)}) collective-permute-start(f32[520,256]{1,0:T(8,128)S(1)} %collective-permute-done.7.refs_3_.refs_7_), channel_id=1, source_target_pairs={{0,1},{1,0},{2,3},{3,2},{4,5},{5,4},{6,7},{7,6},{8,9},{9,8},{10,11... | collective-permute-start | bytes 1597448 | tf_op jit(solution)/shard_map/ppermute | solution.py:34
  47.4 72.0 %copy-start.2 = (f32[520,256]{1,0:T(8,128)}, f32[520,256]{1,0:T(8,128)S(1)}, u32[]{:S(2)}) copy-start(f32[520,256]{1,0:T(8,128)S(1)} %collective-permute-done.5.refs_3_.refs_5_) | copy-start | bytes 1597444
  47.4 72.0 %collective-permute-start.6 = (f32[520,256]{1,0:T(8,128)S(1)}, f32[520,256]{1,0:T(8,128)S(1)}, u32[]{:S(2)}, u32[]{:S(2)}) collective-permute-start(f32[520,256]{1,0:T(8,128)S(1)} %collective-permute-done.5.refs_3_.refs_5_), channel_id=1, source_target_pairs={{0,1},{1,0},{2,3},{3,2},{4,5},{5,4},{6,7},{7,6},{8,9},{9,8},{10,11... | collective-permute-start | bytes 1597448 | tf_op jit(solution)/shard_map/ppermute | solution.py:34
  58.5 25.4 %collective-permute-start.1 = (f32[520,256]{1,0:T(8,128)S(1)}, f32[520,256]{1,0:T(8,128)S(1)}, u32[]{:S(2)}, u32[]{:S(2)}) collective-permute-start(f32[520,256]{1,0:T(8,128)S(1)} %collective-permute-done.refs_3_), channel_id=1, source_target_pairs={{0,1},{1,0},{2,3},{3,2},{4,5},{5,4},{6,7},{7,6},{8,9},{9,8},{10,11... | collective-permute-start | bytes 1597448 | tf_op jit(solution)/shard_map/ppermute | solution.py:34
  58.5 1.0 copy-start.5
  59.6 24.3 %copy-start.6 = (f32[256,16,256]{2,1,0:T(8,128)S(1)}, f32[256,16,256]{2,1,0:T(8,128)}, u32[]{:S(2)}) copy-start(f32[256,16,256]{2,1,0:T(8,128)} %param.7) | copy-start | bytes 12582916
  59.6 24.3 %copy-start.7 = (f32[256,16,256]{2,1,0:T(8,128)S(1)}, f32[256,16,256]{2,1,0:T(8,128)}, u32[]{:S(2)}) copy-start(f32[256,16,256]{2,1,0:T(8,128)} %param.11) | copy-start | bytes 12582916
  101.9 17.1 %copy-start = (f32[4096,256]{1,0:T(8,128)}, f32[4096,256]{1,0:T(8,128)S(1)}, u32[]{:S(2)}) copy-start(f32[4096,256]{1,0:T(8,128)S(1)} %get-tuple-element.21.refs_0_) | copy-start | bytes 12582916
  101.9 33.7 %collective-permute-start.11 = (f32[512,256]{1,0:T(8,128)S(1)}, f32[512,256]{1,0:T(8,128)S(1)}, u32[]{:S(2)}, u32[]{:S(2)}) collective-permute-start(f32[512,256]{1,0:T(8,128)S(1)} %get-tuple-element.30), channel_id=1, source_target_pairs={{0,1},{1,0},{2,3},{3,2},{4,5},{5,4},{6,7},{7,6},{8,9},{9,8},{10,11... | collective-permute-start | bytes 1572872 | tf_op jit(solution)/shard_map/ppermute | solution.py:34
  102.5 35.1 %collective-permute-start.9 = (f32[512,256]{1,0:T(8,128)S(1)}, f32[512,256]{1,0:T(8,128)S(1)}, u32[]{:S(2)}, u32[]{:S(2)}) collective-permute-start(f32[512,256]{1,0:T(8,128)S(1)} %get-tuple-element.28), channel_id=1, source_target_pairs={{0,1},{1,0},{2,3},{3,2},{4,5},{5,4},{6,7},{7,6},{8,9},{9,8},{10,11... | collective-permute-start | bytes 1572872 | tf_op jit(solution)/shard_map/ppermute | solution.py:34
  102.5 16.4 %copy-start.3 = (f32[520,256]{1,0:T(8,128)}, f32[520,256]{1,0:T(8,128)S(1)}, u32[]{:S(2)}) copy-start(f32[520,256]{1,0:T(8,128)S(1)} %collective-permute-done.8.refs_4_.refs_8_) | copy-start | bytes 1597444
  118.9 20.7 %collective-permute-start.15 = (f32[512,256]{1,0:T(8,128)S(1)}, f32[512,256]{1,0:T(8,128)S(1)}, u32[]{:S(2)}, u32[]{:S(2)}) collective-permute-start(f32[512,256]{1,0:T(8,128)S(1)} %get-tuple-element.34), channel_id=1, source_target_pairs={{0,1},{1,0},{2,3},{3,2},{4,5},{5,4},{6,7},{7,6},{8,9},{9,8},{10,11... | collective-permute-start | bytes 1572872 | tf_op jit(solution)/shard_map/ppermute | solution.py:34
  119.4 16.1 %copy-start.4 = (f32[520,256]{1,0:T(8,128)}, f32[520,256]{1,0:T(8,128)S(1)}, u32[]{:S(2)}) copy-start(f32[520,256]{1,0:T(8,128)S(1)} %collective-permute-done.6.refs_4_.refs_6_) | copy-start | bytes 1597444
  135.5 6.2 %collective-permute-start.13 = (f32[512,256]{1,0:T(8,128)S(1)}, f32[512,256]{1,0:T(8,128)S(1)}, u32[]{:S(2)}, u32[]{:S(2)}) collective-permute-start(f32[512,256]{1,0:T(8,128)S(1)} %get-tuple-element.32), channel_id=1, source_target_pairs={{0,1},{1,0},{2,3},{3,2},{4,5},{5,4},{6,7},{7,6},{8,9},{9,8},{10,11... | collective-permute-start | bytes 1572872 | tf_op jit(solution)/shard_map/ppermute | solution.py:34
  135.7 22.1 %collective-permute-start.12 = (f32[512,256]{1,0:T(8,128)S(1)}, f32[512,256]{1,0:T(8,128)S(1)}, u32[]{:S(2)}, u32[]{:S(2)}) collective-permute-start(f32[512,256]{1,0:T(8,128)S(1)} %add.91), channel_id=1, source_target_pairs={{6,0},{7,1},{8,2},{9,3},{10,4},{11,5},{12,6},{13,7},{14,8},{15,9},... | collective-permute-start | bytes 1572872 | tf_op jit(solution)/shard_map/ppermute | solution.py:29
  137.7 25.2 %collective-permute-start.10 = (f32[512,256]{1,0:T(8,128)S(1)}, f32[512,256]{1,0:T(8,128)S(1)}, u32[]{:S(2)}, u32[]{:S(2)}) collective-permute-start(f32[512,256]{1,0:T(8,128)S(1)} %get-tuple-element.37), channel_id=1, source_target_pairs={{8,0},{9,1},{10,2},{11,3},{12,4},{13,5},{14,6},{15,7},{16,8},{17,9... | collective-permute-start | bytes 1572872 | tf_op jit(solution)/shard_map/ppermute | solution.py:29
  139.7 23.2 %collective-permute-start.16 = (f32[512,256]{1,0:T(8,128)S(1)}, f32[512,256]{1,0:T(8,128)S(1)}, u32[]{:S(2)}, u32[]{:S(2)}) collective-permute-start(f32[512,256]{1,0:T(8,128)S(1)} %add.95), channel_id=1, source_target_pairs={{2,0},{3,1},{4,2},{5,3},{6,4},{7,5},{8,6},{9,7},{10,8},{11,9},{12,... | collective-permute-start | bytes 1572872 | tf_op jit(solution)/shard_map/ppermute | solution.py:29
  141.8 44.4 %collective-permute-start.14 = (f32[512,256]{1,0:T(8,128)S(1)}, f32[512,256]{1,0:T(8,128)S(1)}, u32[]{:S(2)}, u32[]{:S(2)}) collective-permute-start(f32[512,256]{1,0:T(8,128)S(1)} %add.93), channel_id=1, source_target_pairs={{4,0},{5,1},{6,2},{7,3},{8,4},{9,5},{10,6},{11,7},{12,8},{13,9},{1... | collective-permute-start | bytes 1572872 | tf_op jit(solution)/shard_map/ppermute | solution.py:29

commit v6 on v5

--- a/solution.py
+++ b/solution.py
@@ -109,9 +109,8 @@
                 vec_ref[:, at],
             )
             if opens:
-                high, low = halves(g_ref[at, :] * out_ref[at, :])
-                ones = jnp.ones((16, width), BF16)
-                delta_ref[:, at] = (dot(ones, high, NT) + dot(ones, low, NT))[0:8, :]
+                both = (g_ref[at, :] * out_ref[at, :]).T
+                delta_ref[:, at] = jnp.broadcast_to(jnp.sum(both, axis=0, keepdims=True), (8, TILE))
         return ready[tile]
 
     def span(tile, block):

time: 188 us -> 186 us (0.989)
  the two profiles are of different devices: /device:TPU:12 before, /device:TPU:20 now
where the time goes in v6:
time: 186 us
  Pallas kernels  89.1 us (48%)
  waiting for transfers between devices  65 us (35%)
  starting transfers between devices  23.3 us (13%)
  local copies, waits for them, and re-layouts  3.82 us (2%)
  other arithmetic  3.76 us (2%)
    pallas_call x4, Pallas kernels, attend(): pl.pallas_call(functools.partial(kernel, blocks, sources, steps, rows, op...  73.6 us
    ppermute x8, waiting for transfers between devices, shifted(): lax.ppermute(value, axis, [(source, source + steps) for source in range(l...  65 us
    ppermute x8, starting transfers between devices, shifted(): lax.ppermute(value, axis, [(source, source + steps) for source in range(l...  21.4 us
    pallas_call x1, Pallas kernels, query_grads(): pl.pallas_call(functools.partial(close, steps, count, rows), grid=(tiles...  13.7 us
  transfers between devices with their start and end apart: 17, of which 4 were waited for; matrix products, arithmetic and copies ran while one was open for 3% of the time, Pallas kernels for 47%

profile of v6, /device:TPU:20, one launch (start us, length us, event | category | flops | bytes accessed | tf_op | source)
XLA Modules:
  0.0 185.9 jit_solution(1541187650198891449)
XLA Ops:
  0.6 1.9 %shard_map.94.refs_4_ = f32[520,256]{1,0:T(8,128)} custom-call(f32[256,256]{1,0:T(8,128)} %k_ref.1, f32[256,256]{1,0:T(8,128)} %v_ref.1, s32[1,256]{1,0:T(1,128)} %bitcast.16), custom_call_target="tpu_custom_call" | custom-call | tf_op jit(solution)/shard_map/pallas_call | solution.py:58
  2.5 3.4 %collective-permute-start.7 = (f32[520,256]{1,0:T(8,128)}, f32[520,256]{1,0:T(8,128)S(1)}, u32[]{:S(2)}, u32[]{:S(2)}) collective-permute-start(f32[520,256]{1,0:T(8,128)} %shard_map.94.refs_4_), channel_id=1, source_target_pairs={{0,2},{1,3},{2,4},{3,5},{4,6},{5,7},{6,8},{7,9},{8,10},{9,11},{10,... | collective-permute-start | bytes 1597448 | tf_op jit(solution)/shard_map/ppermute | solution.py:29
  5.9 3.4 %collective-permute-start.5 = (f32[520,256]{1,0:T(8,128)}, f32[520,256]{1,0:T(8,128)S(1)}, u32[]{:S(2)}, u32[]{:S(2)}) collective-permute-start(f32[520,256]{1,0:T(8,128)} %shard_map.94.refs_4_), channel_id=1, source_target_pairs={{0,4},{1,5},{2,6},{3,7},{4,8},{5,9},{6,10},{7,11},{8,12},{9,13},{1... | collective-permute-start | bytes 1597448 | tf_op jit(solution)/shard_map/ppermute | solution.py:29
  9.3 0.1 collective-permute-start.4
  9.4 1.9 %collective-permute-start.2 = (f32[520,256]{1,0:T(8,128)}, f32[520,256]{1,0:T(8,128)S(1)}, u32[]{:S(2)}, u32[]{:S(2)}) collective-permute-start(f32[520,256]{1,0:T(8,128)} %shard_map.94.refs_4_), channel_id=1, source_target_pairs={{0,8},{1,9},{2,10},{3,11},{4,12},{5,13},{6,14},{7,15},{8,16},{9,17... | collective-permute-start | bytes 1597448 | tf_op jit(solution)/shard_map/ppermute | solution.py:29
  11.3 2.2 %collective-permute-start = (f32[520,256]{1,0:T(8,128)}, f32[520,256]{1,0:T(8,128)S(1)}, u32[]{:S(2)}, u32[]{:S(2)}) collective-permute-start(f32[520,256]{1,0:T(8,128)} %shard_map.94.refs_4_), channel_id=1, source_target_pairs={{0,6},{1,7},{2,8},{3,9},{4,10},{5,11},{6,12},{7,13},{8,14},{9,15},... | collective-permute-start | bytes 1597448 | tf_op jit(solution)/shard_map/ppermute | solution.py:29
  13.6 0.9 convert_reduce_fusion
  14.5 0.7 broadcast_multiply_fusion
  15.3 28.0 %collective-permute-done.2.refs_3_ = f32[520,256]{1,0:T(8,128)S(1)} collective-permute-done((f32[520,256]{1,0:T(8,128)}, f32[520,256]{1,0:T(8,128)S(1)}, u32[]{:S(2)}, u32[]{:S(2)}) %collective-permute-start.2) | collective-permute-done | bytes 532512 | tf_op jit(solution)/shard_map/ppermute | solution.py:29
  43.3 0.0 collective-permute-start.3
  43.3 0.7 convert_add_fusion
  43.9 0.1 copy.12
  44.0 0.1 reshape.68
  44.2 1.1 broadcast_in_dim.27
  45.3 1.4 reshape.69
  46.7 0.1 pad_maximum_fusion.refs_2_
  46.8 0.0 collective-permute-done.7.refs_3_.refs_7_
  46.8 0.0 copy-start.1
  46.8 0.6 collective-permute-start.8
  47.4 0.0 collective-permute-done.5.refs_3_.refs_5_
  47.4 0.1 collective-permute-start.6
  47.5 11.0 %collective-permute-done.refs_3_ = f32[520,256]{1,0:T(8,128)S(1)} collective-permute-done((f32[520,256]{1,0:T(8,128)}, f32[520,256]{1,0:T(8,128)S(1)}, u32[]{:S(2)}, u32[]{:S(2)}) %collective-permute-start) | collective-permute-done | bytes 532512 | tf_op jit(solution)/shard_map/ppermute | solution.py:29
  58.5 0.0 collective-permute-start.1
  58.5 0.0 collective-permute-done.4.refs_6_
  58.5 0.0 collective-permute-done.3.refs_5_
  58.5 0.0 copy-start.5
  58.5 1.0 copy-done.5
  59.6 23.1 %shard_map.95 = (f32[4096,256]{1,0:T(8,128)S(1)}, f32[8,4096]{1,0:T(8,128)S(1)}, f32[512,256]{1,0:T(8,128)S(1)}, f32[512,256]{1,0:T(8,128)S(1)}, f32[512,256]{1,0:T(8,128)S(1)}) custom-call(f32[4096,256]{1,0:T(8,128)} %bitcast.7, f32[4096,256]{1,0:T(8,128)} %bitcast.11, f32[8,4096]{1,0:T(8,128)S(1)} %pad_maximum_fusion.refs_2_, ...), custom_call_target="tpu_custom_call" | custom-call | flops 16609443840 | bytes 12582912 | tf_op jit(solution)/shard_map/pallas_call | solution.py:207
  82.7 0.0 collective-permute-done.1.refs_4_
  82.7 0.0 copy-done.6
  82.7 0.0 copy-done.7
  82.7 18.0 %shard_map.96 = (f32[4096,256]{1,0:T(8,128)S(1)}, f32[512,256]{1,0:T(8,128)S(1)}, f32[512,256]{1,0:T(8,128)S(1)}) custom-call(f32[4096,256]{1,0:T(8,128)S(1)} %bitcast.8, f32[4096,256]{1,0:T(8,128)S(1)} %bitcast.12, f32[8,4096]{1,0:T(8,128)S(1)} %pad_maximum_fusion.refs_2_, f32[520,256]{1,0:T(8,128)S(1)} %collective-permute-done.refs_3_, ...), custom_call_target="tpu_custom_call" | custom-call | flops 16106127360 | bytes 12582912 | tf_op jit(solution)/shard_map/pallas_call | solution.py:207
  100.7 0.0 copy-start
  100.7 0.6 collective-permute-start.11
  101.3 0.1 collective-permute-start.9
  101.3 0.0 collective-permute-done.8.refs_4_.refs_8_
  101.4 0.0 copy-done.1
  101.4 16.4 %shard_map.98 = (bf16[512,4096]{1,0:T(8,128)(2,1)}, bf16[512,4096]{1,0:T(8,128)(2,1)}, f32[512,256]{1,0:T(8,128)S(1)}, f32[512,256]{1,0:T(8,128)S(1)}) custom-call(f32[4096,256]{1,0:T(8,128)S(1)} %bitcast.9, f32[4096,256]{1,0:T(8,128)S(1)} %bitcast.13, f32[8,4096]{1,0:T(8,128)S(1)} %pad_maximum_fusion.refs_2_, ...), custom_call_target="tpu_custom_call" | custom-call | flops 16106127360 | bytes 12582912 | tf_op jit(solution)/shard_map/pallas_call | solution.py:207
  117.7 0.0 copy-done
  117.7 0.0 copy-done.3
  117.8 0.4 collective-permute-start.15
  118.2 0.0 collective-permute-done.6.refs_4_.refs_6_
  118.2 0.0 copy-done.2
  118.2 16.1 %shard_map.97 = (bf16[512,4096]{1,0:T(8,128)(2,1)}, bf16[512,4096]{1,0:T(8,128)(2,1)}, f32[512,256]{1,0:T(8,128)S(1)}, f32[512,256]{1,0:T(8,128)S(1)}) custom-call(f32[4096,256]{1,0:T(8,128)S(1)} %bitcast.10, f32[4096,256]{1,0:T(8,128)S(1)} %bitcast.14, f32[8,4096]{1,0:T(8,128)S(1)} %pad_maximum_fusion.refs_2_, ...), custom_call_target="tpu_custom_call" | custom-call | flops 16106127360 | bytes 12582912 | tf_op jit(solution)/shard_map/pallas_call | solution.py:207
  134.3 0.0 copy-done.4
  134.3 0.1 collective-permute-start.13
  134.4 0.0 collective-permute-done.11
  134.4 0.1 add.91
  134.5 1.9 %collective-permute-start.12 = (f32[512,256]{1,0:T(8,128)S(1)}, f32[512,256]{1,0:T(8,128)S(1)}, u32[]{:S(2)}, u32[]{:S(2)}) collective-permute-start(f32[512,256]{1,0:T(8,128)S(1)} %add.91), channel_id=1, source_target_pairs={{6,0},{7,1},{8,2},{9,3},{10,4},{11,5},{12,6},{13,7},{14,8},{15,9},... | collective-permute-start | bytes 1572872 | tf_op jit(solution)/shard_map/ppermute | solution.py:29
  136.4 0.0 collective-permute-done.9
  136.4 0.1 select_add_fusion
  136.5 2.4 %collective-permute-start.10 = (f32[512,256]{1,0:T(8,128)S(1)}, f32[512,256]{1,0:T(8,128)S(1)}, u32[]{:S(2)}, u32[]{:S(2)}) collective-permute-start(f32[512,256]{1,0:T(8,128)S(1)} %get-tuple-element.37), channel_id=1, source_target_pairs={{8,0},{9,1},{10,2},{11,3},{12,4},{13,5},{14,6},{15,7},{16,8},{17,9... | collective-permute-start | bytes 1572872 | tf_op jit(solution)/shard_map/ppermute | solution.py:29
  138.9 0.0 collective-permute-done.15
  138.9 0.1 add.95
  139.0 4.3 %collective-permute-start.16 = (f32[512,256]{1,0:T(8,128)S(1)}, f32[512,256]{1,0:T(8,128)S(1)}, u32[]{:S(2)}, u32[]{:S(2)}) collective-permute-start(f32[512,256]{1,0:T(8,128)S(1)} %add.95), channel_id=1, source_target_pairs={{2,0},{3,1},{4,2},{5,3},{6,4},{7,5},{8,6},{9,7},{10,8},{11,9},{12,... | collective-permute-start | bytes 1572872 | tf_op jit(solution)/shard_map/ppermute | solution.py:29
  143.3 0.0 collective-permute-done.13
  143.3 0.1 add.93
  143.4 1.9 %collective-permute-start.14 = (f32[512,256]{1,0:T(8,128)S(1)}, f32[512,256]{1,0:T(8,128)S(1)}, u32[]{:S(2)}, u32[]{:S(2)}) collective-permute-start(f32[512,256]{1,0:T(8,128)S(1)} %add.93), channel_id=1, source_target_pairs={{4,0},{5,1},{6,2},{7,3},{8,4},{9,5},{10,6},{11,7},{12,8},{13,9},{1... | collective-permute-start | bytes 1572872 | tf_op jit(solution)/shard_map/ppermute | solution.py:29
  145.3 13.7 %shard_map.99 = f32[4096,256]{1,0:T(8,128)} custom-call(f32[4096,256]{1,0:T(8,128)} %copy-done, bf16[512,4096]{1,0:T(8,128)(2,1)} %get-tuple-element.22.refs_1_, bf16[512,4096]{1,0:T(8,128)(2,1)} %get-tuple-element.23.refs_2_, bf16[512,4096]{1,0:T(8,128)(2,1)} %get-tuple-element.24.refs_3_, bf16[512,4096]{1,0:T(8,128)(2,1)} %get-tuple-element.25.refs_4_, ...), custom_call_target="tpu_custom_call" | custom-call | flops 6442450944 | bytes 25165824 | tf_op jit(solution)/shard_map/pallas_call | solution.py:262
  158.9 0.0 collective-permute-done.12
  158.9 2.2 %collective-permute-done.10 = f32[512,256]{1,0:T(8,128)S(1)} collective-permute-done((f32[512,256]{1,0:T(8,128)S(1)}, f32[512,256]{1,0:T(8,128)S(1)}, u32[]{:S(2)}, u32[]{:S(2)}) %collective-permute-start.10) | collective-permute-done | bytes 524320 | tf_op jit(solution)/shard_map/ppermute | solution.py:29
  161.1 0.0 collective-permute-done.16
  161.1 23.8 %collective-permute-done.14 = f32[512,256]{1,0:T(8,128)S(1)} collective-permute-done((f32[512,256]{1,0:T(8,128)S(1)}, f32[512,256]{1,0:T(8,128)S(1)}, u32[]{:S(2)}, u32[]{:S(2)}) %collective-permute-start.14) | collective-permute-done | bytes 524320 | tf_op jit(solution)/shard_map/ppermute | solution.py:29
  184.9 1.0 slice_add_fusion
  (11 shorter events, 0.1 us)
Async XLA Ops:
  2.5 44.3 %collective-permute-start.7 = (f32[520,256]{1,0:T(8,128)}, f32[520,256]{1,0:T(8,128)S(1)}, u32[]{:S(2)}, u32[]{:S(2)}) collective-permute-start(f32[520,256]{1,0:T(8,128)} %shard_map.94.refs_4_), channel_id=1, source_target_pairs={{0,2},{1,3},{2,4},{3,5},{4,6},{5,7},{6,8},{7,9},{8,10},{9,11},{10,... | collective-permute-start | bytes 1597448 | tf_op jit(solution)/shard_map/ppermute | solution.py:29
  5.9 41.5 %collective-permute-start.5 = (f32[520,256]{1,0:T(8,128)}, f32[520,256]{1,0:T(8,128)S(1)}, u32[]{:S(2)}, u32[]{:S(2)}) collective-permute-start(f32[520,256]{1,0:T(8,128)} %shard_map.94.refs_4_), channel_id=1, source_target_pairs={{0,4},{1,5},{2,6},{3,7},{4,8},{5,9},{6,10},{7,11},{8,12},{9,13},{1... | collective-permute-start | bytes 1597448 | tf_op jit(solution)/shard_map/ppermute | solution.py:29
  9.3 49.2 %collective-permute-start.4 = (f32[520,256]{1,0:T(8,128)}, f32[520,256]{1,0:T(8,128)S(1)}, u32[]{:S(2)}, u32[]{:S(2)}) collective-permute-start(f32[520,256]{1,0:T(8,128)} %shard_map.94.refs_4_), channel_id=1, source_target_pairs={{0,1},{1,0},{2,3},{3,2},{4,5},{5,4},{6,7},{7,6},{8,9},{9,8},{10,11... | collective-permute-start | bytes 1597448 | tf_op jit(solution)/shard_map/ppermute | solution.py:34
  9.4 33.8 %collective-permute-start.2 = (f32[520,256]{1,0:T(8,128)}, f32[520,256]{1,0:T(8,128)S(1)}, u32[]{:S(2)}, u32[]{:S(2)}) collective-permute-start(f32[520,256]{1,0:T(8,128)} %shard_map.94.refs_4_), channel_id=1, source_target_pairs={{0,8},{1,9},{2,10},{3,11},{4,12},{5,13},{6,14},{7,15},{8,16},{9,17... | collective-permute-start | bytes 1597448 | tf_op jit(solution)/shard_map/ppermute | solution.py:29
  11.3 47.2 %collective-permute-start = (f32[520,256]{1,0:T(8,128)}, f32[520,256]{1,0:T(8,128)S(1)}, u32[]{:S(2)}, u32[]{:S(2)}) collective-permute-start(f32[520,256]{1,0:T(8,128)} %shard_map.94.refs_4_), channel_id=1, source_target_pairs={{0,6},{1,7},{2,8},{3,9},{4,10},{5,11},{6,12},{7,13},{8,14},{9,15},... | collective-permute-start | bytes 1597448 | tf_op jit(solution)/shard_map/ppermute | solution.py:29
  43.3 15.3 %collective-permute-start.3 = (f32[520,256]{1,0:T(8,128)S(1)}, f32[520,256]{1,0:T(8,128)S(1)}, u32[]{:S(2)}, u32[]{:S(2)}) collective-permute-start(f32[520,256]{1,0:T(8,128)S(1)} %collective-permute-done.2.refs_3_), channel_id=1, source_target_pairs={{0,1},{1,0},{2,3},{3,2},{4,5},{5,4},{6,7},{7,6},{8,9},{9,8},{10,11... | collective-permute-start | bytes 1597448 | tf_op jit(solution)/shard_map/ppermute | solution.py:34
  46.8 54.6 %copy-start.1 = (f32[520,256]{1,0:T(8,128)}, f32[520,256]{1,0:T(8,128)S(1)}, u32[]{:S(2)}) copy-start(f32[520,256]{1,0:T(8,128)S(1)} %collective-permute-done.7.refs_3_.refs_7_) | copy-start | bytes 1597444
  46.8 54.5 %collective-permute-start.8 = (f32[520,256]{1,0:T(8,128)S(1)}, f32[520,256]{1,0:T(8,128)S(1)}, u32[]{:S(2)}, u32[]{:S(2)}) collective-permute-start(f32[520,256]{1,0:T(8,128)S(1)} %collective-permute-done.7.refs_3_.refs_7_), channel_id=1, source_target_pairs={{0,1},{1,0},{2,3},{3,2},{4,5},{5,4},{6,7},{7,6},{8,9},{9,8},{10,11... | collective-permute-start | bytes 1597448 | tf_op jit(solution)/shard_map/ppermute | solution.py:34
  47.4 70.8 %copy-start.2 = (f32[520,256]{1,0:T(8,128)}, f32[520,256]{1,0:T(8,128)S(1)}, u32[]{:S(2)}) copy-start(f32[520,256]{1,0:T(8,128)S(1)} %collective-permute-done.5.refs_3_.refs_5_) | copy-start | bytes 1597444
  47.4 70.8 %collective-permute-start.6 = (f32[520,256]{1,0:T(8,128)S(1)}, f32[520,256]{1,0:T(8,128)S(1)}, u32[]{:S(2)}, u32[]{:S(2)}) collective-permute-start(f32[520,256]{1,0:T(8,128)S(1)} %collective-permute-done.5.refs_3_.refs_5_), channel_id=1, source_target_pairs={{0,1},{1,0},{2,3},{3,2},{4,5},{5,4},{6,7},{7,6},{8,9},{9,8},{10,11... | collective-permute-start | bytes 1597448 | tf_op jit(solution)/shard_map/ppermute | solution.py:34
  58.5 24.2 %collective-permute-start.1 = (f32[520,256]{1,0:T(8,128)S(1)}, f32[520,256]{1,0:T(8,128)S(1)}, u32[]{:S(2)}, u32[]{:S(2)}) collective-permute-start(f32[520,256]{1,0:T(8,128)S(1)} %collective-permute-done.refs_3_), channel_id=1, source_target_pairs={{0,1},{1,0},{2,3},{3,2},{4,5},{5,4},{6,7},{7,6},{8,9},{9,8},{10,11... | collective-permute-start | bytes 1597448 | tf_op jit(solution)/shard_map/ppermute | solution.py:34
  58.5 1.0 copy-start.5
  59.6 23.1 %copy-start.6 = (f32[256,16,256]{2,1,0:T(8,128)S(1)}, f32[256,16,256]{2,1,0:T(8,128)}, u32[]{:S(2)}) copy-start(f32[256,16,256]{2,1,0:T(8,128)} %param.7) | copy-start | bytes 12582916
  59.6 23.1 %copy-start.7 = (f32[256,16,256]{2,1,0:T(8,128)S(1)}, f32[256,16,256]{2,1,0:T(8,128)}, u32[]{:S(2)}) copy-start(f32[256,16,256]{2,1,0:T(8,128)} %param.11) | copy-start | bytes 12582916
  100.7 17.1 %copy-start = (f32[4096,256]{1,0:T(8,128)}, f32[4096,256]{1,0:T(8,128)S(1)}, u32[]{:S(2)}) copy-start(f32[4096,256]{1,0:T(8,128)S(1)} %get-tuple-element.21.refs_0_) | copy-start | bytes 12582916
  100.7 33.7 %collective-permute-start.11 = (f32[512,256]{1,0:T(8,128)S(1)}, f32[512,256]{1,0:T(8,128)S(1)}, u32[]{:S(2)}, u32[]{:S(2)}) collective-permute-start(f32[512,256]{1,0:T(8,128)S(1)} %get-tuple-element.30), channel_id=1, source_target_pairs={{0,1},{1,0},{2,3},{3,2},{4,5},{5,4},{6,7},{7,6},{8,9},{9,8},{10,11... | collective-permute-start | bytes 1572872 | tf_op jit(solution)/shard_map/ppermute | solution.py:34
  101.3 35.1 %collective-permute-start.9 = (f32[512,256]{1,0:T(8,128)S(1)}, f32[512,256]{1,0:T(8,128)S(1)}, u32[]{:S(2)}, u32[]{:S(2)}) collective-permute-start(f32[512,256]{1,0:T(8,128)S(1)} %get-tuple-element.28), channel_id=1, source_target_pairs={{0,1},{1,0},{2,3},{3,2},{4,5},{5,4},{6,7},{7,6},{8,9},{9,8},{10,11... | collective-permute-start | bytes 1572872 | tf_op jit(solution)/shard_map/ppermute | solution.py:34
  101.4 16.4 %copy-start.3 = (f32[520,256]{1,0:T(8,128)}, f32[520,256]{1,0:T(8,128)S(1)}, u32[]{:S(2)}) copy-start(f32[520,256]{1,0:T(8,128)S(1)} %collective-permute-done.8.refs_4_.refs_8_) | copy-start | bytes 1597444
  117.8 21.2 %collective-permute-start.15 = (f32[512,256]{1,0:T(8,128)S(1)}, f32[512,256]{1,0:T(8,128)S(1)}, u32[]{:S(2)}, u32[]{:S(2)}) collective-permute-start(f32[512,256]{1,0:T(8,128)S(1)} %get-tuple-element.34), channel_id=1, source_target_pairs={{0,1},{1,0},{2,3},{3,2},{4,5},{5,4},{6,7},{7,6},{8,9},{9,8},{10,11... | collective-permute-start | bytes 1572872 | tf_op jit(solution)/shard_map/ppermute | solution.py:34
  118.2 16.1 %copy-start.4 = (f32[520,256]{1,0:T(8,128)}, f32[520,256]{1,0:T(8,128)S(1)}, u32[]{:S(2)}) copy-start(f32[520,256]{1,0:T(8,128)S(1)} %collective-permute-done.6.refs_4_.refs_6_) | copy-start | bytes 1597444
  134.3 8.9 %collective-permute-start.13 = (f32[512,256]{1,0:T(8,128)S(1)}, f32[512,256]{1,0:T(8,128)S(1)}, u32[]{:S(2)}, u32[]{:S(2)}) collective-permute-start(f32[512,256]{1,0:T(8,128)S(1)} %get-tuple-element.32), channel_id=1, source_target_pairs={{0,1},{1,0},{2,3},{3,2},{4,5},{5,4},{6,7},{7,6},{8,9},{9,8},{10,11... | collective-permute-start | bytes 1572872 | tf_op jit(solution)/shard_map/ppermute | solution.py:34
  134.5 24.5 %collective-permute-start.12 = (f32[512,256]{1,0:T(8,128)S(1)}, f32[512,256]{1,0:T(8,128)S(1)}, u32[]{:S(2)}, u32[]{:S(2)}) collective-permute-start(f32[512,256]{1,0:T(8,128)S(1)} %add.91), channel_id=1, source_target_pairs={{6,0},{7,1},{8,2},{9,3},{10,4},{11,5},{12,6},{13,7},{14,8},{15,9},... | collective-permute-start | bytes 1572872 | tf_op jit(solution)/shard_map/ppermute | solution.py:29
  136.5 24.6 %collective-permute-start.10 = (f32[512,256]{1,0:T(8,128)S(1)}, f32[512,256]{1,0:T(8,128)S(1)}, u32[]{:S(2)}, u32[]{:S(2)}) collective-permute-start(f32[512,256]{1,0:T(8,128)S(1)} %get-tuple-element.37), channel_id=1, source_target_pairs={{8,0},{9,1},{10,2},{11,3},{12,4},{13,5},{14,6},{15,7},{16,8},{17,9... | collective-permute-start | bytes 1572872 | tf_op jit(solution)/shard_map/ppermute | solution.py:29
  139.0 22.1 %collective-permute-start.16 = (f32[512,256]{1,0:T(8,128)S(1)}, f32[512,256]{1,0:T(8,128)S(1)}, u32[]{:S(2)}, u32[]{:S(2)}) collective-permute-start(f32[512,256]{1,0:T(8,128)S(1)} %add.95), channel_id=1, source_target_pairs={{2,0},{3,1},{4,2},{5,3},{6,4},{7,5},{8,6},{9,7},{10,8},{11,9},{12,... | collective-permute-start | bytes 1572872 | tf_op jit(solution)/shard_map/ppermute | solution.py:29
  143.4 41.6 %collective-permute-start.14 = (f32[512,256]{1,0:T(8,128)S(1)}, f32[512,256]{1,0:T(8,128)S(1)}, u32[]{:S(2)}, u32[]{:S(2)}) collective-permute-start(f32[512,256]{1,0:T(8,128)S(1)} %add.93), channel_id=1, source_target_pairs={{4,0},{5,1},{6,2},{7,3},{8,4},{9,5},{10,6},{11,7},{12,8},{13,9},{1... | collective-permute-start | bytes 1572872 | tf_op jit(solution)/shard_map/ppermute | solution.py:29
